TPU v7x, 256 devices: a whole 4x4x8 slice. The times are simulated.
256 devices in a mesh: row: 32 (over y_lo, z, core), col: 8 (over x, y_hi).
Axes of the slice: x: 4, y: 4 (y_hi: 2, y_lo: 2; y = y_hi * 2 + y_lo), z: 8, core: 2. Of those that a mesh axis runs over, the one named last changes fastest.
Arguments:
- inverse_tiles: bfloat16 [128, 256, 128, 256], P('col', None, 'row'), may hold values from -6 to 6
- factor_panels: bfloat16 [2, 128, 256, 256], P(None, 'row', 'col'), may hold values from -0.0390625 to 0.0390625
- ancestors: int32 [2, 96], replicated, may hold values from 0 to 127, as said below
- valid_flags: int32 [2, 96], replicated, may hold values from 0 to 1, as said below
- block_slot: int32 [128], replicated, may hold values from 0 to 127, each once
Outputs:
- new_panels: float32 [128, 256, 2, 256], P('col', 'row')
Inputs may be any that keep to these rules, and one draw needn't show every extreme that they name: `ancestors`: within one supernode's list all 96 entries name different blocks. `valid_flags`: each list's used entries come first; supernode 0's list is used in full, the others in 64 entries or more.
All inputs are finite; a program needn't handle non-finite values.
Results may differ from a plain program's by a relative error of at most 0.0003.
Values may be sent and summed in bfloat16 or wider, within the bound.
No kernel may reach another device: no remote copies, remote signals or barrier semaphores. Data moves between devices by JAX's collectives and lax.ppermute only.
A program may use at most 64 MiB of HBM per device.

v0:
```python
import jax
import jax.numpy as jnp
from jax import lax
from jax.sharding import PartitionSpec as P


def membership(ancestors, valid_flags, block_slot):
    blocks = jnp.arange(block_slot.shape[0], dtype=jnp.int32)
    pick = (ancestors[:, :, None] == blocks[None, None, :]).astype(jnp.int32)
    slots = jnp.sum(pick * block_slot[None, None, :], axis=2)
    hits = (slots[:, :, None] == blocks[None, None, :]) & (valid_flags[:, :, None] == 1)
    return jnp.any(hits, axis=1)


def panel_product(left, right):
    return jnp.dot(left, right, preferred_element_type=jnp.float32)


def per_device(inverse_tiles, factor_panels, ancestors, valid_flags, block_slot):
    local_rows = inverse_tiles.shape[0]
    width = inverse_tiles.shape[1]
    local_cols = inverse_tiles.shape[2]
    panel_count = factor_panels.shape[0]
    member = membership(ancestors, valid_flags, block_slot)
    col_start = lax.axis_index("row") * local_cols
    row_start = lax.axis_index("col") * local_rows
    col_member = lax.dynamic_slice_in_dim(member, col_start, local_cols, 1)
    row_member = lax.dynamic_slice_in_dim(member, row_start, local_rows, 1)
    left = inverse_tiles.reshape(local_rows * width, local_cols * width)
    masked_local = jnp.where(
        col_member[:, :, None, None], factor_panels, jnp.zeros((), factor_panels.dtype)
    )
    results = []
    for which in range(panel_count):
        whole = lax.all_gather(masked_local[which], "col", axis=1, tiled=True)
        right = whole.reshape(local_cols * width, width)
        partial_value = panel_product(left, right)
        summed = lax.psum_scatter(
            partial_value.reshape(local_rows, width, width), "row", scatter_dimension=1, tiled=True
        )
        results.append(summed)
    stacked = jnp.stack(results, axis=2)
    rowmask = jnp.transpose(row_member)[:, None, :, None]
    return jnp.where(rowmask, -stacked, jnp.zeros((), jnp.float32))


def solution(mesh):
    return jax.shard_map(
        per_device,
        mesh=mesh,
        in_specs=(P("col", None, "row", None), P(None, "row", "col", None), P(), P(), P()),
        out_specs=P("col", "row", None, None),
        check_vma=False,
    )
```

profile of v0, /device:TPU:2, one launch (start us, length us, event | category | flops | bytes accessed | tf_op | source)
XLA Modules:
  0.0 325.4 jit_solution(16764533010754993528)
XLA Ops:
  6.5 0.0 reduce-scatter.3.cloned.1.call-start
  6.5 0.7 broadcast_compare_fusion
  7.2 0.9 select_reduce_fusion
  8.1 0.1 fusion.2
  8.2 0.1 constant_dynamic-slice_fusion
  8.3 1.0 broadcast_select_fusion
  9.3 34.7 %all-gather = bf16[1,4,256,256]{3,2,1,0:T(8,128)(2,1)S(1)} all-gather(bf16[1,4,32,256]{3,2,1,0:T(8,128)(2,1)S(1)} %get-tuple-element.5), channel_id=2, replica_groups=mesh['row'=32,'col'=8] {'col'}, dimensions={2}, use_global_device_ids=true | all-gather | bytes 589824 | tf_op jit(solution)/shard_map/all_gather | solution.py:35
  44.1 9.4 %copy.17 = bf16[512,8,4,256]{3,1,2,0:T(8,128)(2,1)} copy(bf16[512,8,4,256]{3,2,1,0:T(4,128)(2,1)} %bitcast.21) | data formatting | bytes 16777216
  53.4 7.8 %convolution_bitcast_fusion.1 = f32[4096,256]{0,1:T(8,128)} fusion(bf16[1024,256]{1,0:T(8,128)(2,1)S(1)} %bitcast.24, bf16[4096,1024]{1,0:T(8,128)(2,1)} %bitcast.22), kind=kOutput, calls=%fused_computation.1 | convolution fusion | flops 2147483648 | bytes 13107200 | tf_op jit(solution)/shard_map/dot_general | solution.py:16
  61.2 5.6 %copy.15 = f32[4096,256]{1,0:T(8,128)} copy(f32[4096,256]{0,1:T(8,128)} %convolution_bitcast_fusion.1) | data formatting | bytes 8388608 | tf_op jit(solution)/shard_map/reshape | solution.py:39
  66.8 0.0 reduce-scatter.3.cloned.1.call-update
  66.9 0.0 reduce-scatter.5.cloned.1.call-start
  66.9 35.3 %all-gather.1 = bf16[1,4,256,256]{3,2,1,0:T(8,128)(2,1)S(1)} all-gather(bf16[1,4,32,256]{3,2,1,0:T(8,128)(2,1)S(1)} %get-tuple-element.6), channel_id=3, replica_groups=mesh['row'=32,'col'=8] {'col'}, dimensions={2}, use_global_device_ids=true | all-gather | bytes 589824 | tf_op jit(solution)/shard_map/all_gather | solution.py:35
  102.2 7.8 %convolution_bitcast_fusion = f32[4096,256]{0,1:T(8,128)} fusion(bf16[1024,256]{1,0:T(8,128)(2,1)S(1)} %bitcast.25, bf16[4096,1024]{1,0:T(8,128)(2,1)} %bitcast.23), kind=kOutput, calls=%fused_computation | convolution fusion | flops 2147483648 | bytes 13107200 | tf_op jit(solution)/shard_map/dot_general | solution.py:16
  110.0 5.6 %copy.16 = f32[4096,256]{1,0:T(8,128)} copy(f32[4096,256]{0,1:T(8,128)} %convolution_bitcast_fusion) | data formatting | bytes 8388608 | tf_op jit(solution)/shard_map/reshape | solution.py:39
  115.6 0.0 reduce-scatter.5.cloned.1.call-update
  115.7 0.1 dynamic-slice_bitcast_fusion
  115.7 78.5 %reduce-scatter.3.cloned.1.call-done = f32[16,8,256]{2,1,0:T(8,128)} async-done(((f32[16,256,256]{2,1,0:T(8,128)}), f32[16,8,256]{2,1,0:T(8,128)}) %reduce-scatter.3.cloned.1.call-update) | async-done | bytes 131088 | tf_op jit(solution)/shard_map/reduce_scatter | solution.py:38
  194.3 122.3 %reduce-scatter.5.cloned.1.call-done = f32[16,8,256]{2,1,0:T(8,128)} async-done(((f32[16,256,256]{2,1,0:T(8,128)}), f32[16,8,256]{2,1,0:T(8,128)}) %reduce-scatter.5.cloned.1.call-update) | async-done | bytes 131088 | tf_op jit(solution)/shard_map/reduce_scatter | solution.py:38
  316.6 1.1 fusion
  317.6 0.9 copy.14
  (1 shorter events, 0.0 us)
Async XLA Ops:
  6.5 187.7 %reduce-scatter.3.cloned.1.call-start = ((), (), s32[]{:S(2)}) async-start(), calls=%async_computation.2 | async-start | bytes 4325376 | tf_op jit(solution)/shard_map/reduce_scatter | solution.py:38
  66.9 249.7 %reduce-scatter.5.cloned.1.call-start = ((), (), s32[]{:S(2)}) async-start(), calls=%async_computation.3 | async-start | bytes 4325376 | tf_op jit(solution)/shard_map/reduce_scatter | solution.py:38
Sparse Core Ops, SparseCore 0:
  67.0 127.2 reduce-scatter.2
  196.8 119.7 reduce-scatter.4
where the time goes:
time: 326 us; the launch traced here: 325 us
  waiting for transfers between devices  201 us (62%)
  blocking collectives  70.1 us (22%)
  local copies, waits for them, and re-layouts  21.6 us (7%)
  matrix products  15.6 us (5%)
  between operations  13.4 us (4%)
  other arithmetic  3.75 us (1%)
    reduce_scatter x2, waiting for transfers between devices, per_device(): lax.psum_scatter(partial_value.reshape(local_rows, width, width), 'row',...  201 us
    all_gather x2, blocking collectives, per_device(): whole = lax.all_gather(masked_local[which], 'col', axis=1, tiled=True)  70.1 us
    dot_general x2, matrix products, panel_product(): return jnp.dot(left, right, preferred_element_type=jnp.float32)  15.6 us
    reshape x2, local copies, waits for them, and re-layouts, per_device(): partial_value.reshape(local_rows, width, width)  11.2 us
    unnamed x1, local copies, waits for them, and re-layouts  9.35 us
  transfers between devices with their start and end apart: 2, of which 2 were waited for; matrix products, arithmetic and copies ran while one was open for 4% of the time, Pallas kernels for 0%

commit v1 on v0

v1 whole, which is shorter than its diff:
```python
import math

import jax
import jax.numpy as jnp
from jax import lax
from jax.experimental import pallas as pl
from jax.experimental.pallas import tpu as pltpu
from jax.sharding import PartitionSpec as P


NZ = 8
STEPS = 4
EARLY = 4
TOP = 32000.0
TAIL = 16


def membership(ancestors, valid_flags, block_slot):
    blocks = jnp.arange(block_slot.shape[0], dtype=jnp.int32)
    pick = (ancestors[:, :, None] == blocks[None, None, :]).astype(jnp.int32)
    slots = jnp.sum(pick * block_slot[None, None, :], axis=2)
    hits = (slots[:, :, None] == blocks[None, None, :]) & (valid_flags[:, :, None] == 1)
    return jnp.any(hits, axis=1)


def row_perm(move, cores=(0, 1)):
    pairs = []
    for r in range(32):
        ylo, z, core = r // 16, (r // 2) % NZ, r % 2
        if core in cores:
            y2, z2, c2 = move(ylo, z, core)
            pairs.append((r, ((y2 % 2) * NZ + z2 % NZ) * 2 + c2 % 2))
    return pairs


def col_perm(dx, dy):
    return [(c, ((c // 2 + dx) % 4) * 2 + (c % 2 + dy) % 2) for c in range(8)]


CORE = row_perm(lambda y, z, c: (y, z, 1 - c))
FIRST = row_perm(lambda y, z, c: (y, z - 1, c), cores=(1,))
ARM = row_perm(lambda y, z, c: (y, z + 1 - 2 * c, c))


def encode(v):
    top = jnp.maximum(jnp.max(jnp.abs(v), axis=0, keepdims=True), 1e-30)
    e = jnp.ceil(jnp.log2(top * (1.0 / TOP)))
    q = jnp.round(v * jnp.exp2(-e))
    tail = jnp.broadcast_to(e, (TAIL, v.shape[1]))
    return q.astype(jnp.int32).astype(jnp.int16), tail.astype(jnp.int32).astype(jnp.int16)


def scale_of(ref, rows):
    e = ref[rows : rows + TAIL, :].astype(jnp.int32).astype(jnp.float32)
    return jnp.exp2(e[0:1, :])


def decode(ref, rows):
    return ref[0:rows, :].astype(jnp.int32).astype(jnp.float32) * scale_of(ref, rows)


LARGE = 113 << 19
VMEM = pl.BlockSpec(memory_space=pltpu.VMEM)
SMEM = pl.BlockSpec(memory_space=pltpu.SMEM)
HBM = pl.BlockSpec(memory_space=pltpu.HBM)


def call(body, in_specs, out_shape, flops, nbytes, scratch=(), limit=8 << 20):
    many = isinstance(out_shape, list)
    return pl.pallas_call(
        body,
        in_specs=in_specs,
        out_specs=[VMEM] * len(out_shape) if many else VMEM,
        out_shape=out_shape,
        scratch_shapes=list(scratch),
        compiler_params=pltpu.CompilerParams(vmem_limit_bytes=limit),
        cost_estimate=pl.CostEstimate(flops=flops, bytes_accessed=nbytes, transcendentals=0),
    )


def shape(dims, dtype):
    return pltpu.VMEM(dims, dtype)


def gather_body(at_ref, keep_ref, *refs):
    *pieces, out_ref = refs
    count, cols, _, width = pieces[0].shape
    for p, piece in enumerate(pieces):
        for s in range(count):
            for b in range(cols):
                value = piece[s, b]
                keep = jnp.full(value.shape, keep_ref[s * cols + b], jnp.int32) > 0
                out_ref[b, at_ref[p], :, s * width : (s + 1) * width] = jnp.where(
                    keep, value, jnp.zeros_like(value)
                )


def assemble(at, keep, pieces):
    count, cols, rows, width = pieces[0].shape
    out = shape((cols, len(pieces), rows, count * width), pieces[0].dtype)
    f = call(gather_body, [SMEM, SMEM] + [VMEM] * len(pieces), out, 0, 4 * math.prod(out.shape))
    return f(at, keep, *pieces).reshape(-1, count * width)


def fetch(at, a_ref, buf, sem):
    return [pltpu.make_async_copy(a_ref.at[:, y, at], buf.at[y], sem.at[y]) for y in range(2)]


def flat(x):
    return x.reshape(-1, x.shape[2] * x.shape[3])


def put(out_ref, y, r):
    half = r.shape[0] // 2
    r = r.reshape(-1, 2, 8, r.shape[1])
    for c in range(2):
        start = (2 * y + c) * half
        out_ref[start : start + half, :] = r[:, c].reshape(half, r.shape[3])


def prepare_body(at_ref, a_ref, out_ref, buf, sem):
    for o in range(EARLY):
        for copy in fetch(at_ref[o], a_ref, buf.at[o], sem.at[o]):
            copy.start()
    for o in range(EARLY):
        for y, copy in enumerate(fetch(at_ref[o], a_ref, buf.at[o], sem.at[o])):
            copy.wait()
            out_ref[o, y] = flat(buf[o, y])


def prepare(at, a):
    count, ys, zs, rows, cols, width = a.shape
    f = call(
        prepare_body,
        [SMEM, HBM],
        shape((EARLY, ys, count * rows, cols * width), a.dtype),
        0,
        4 * a.size // zs * EARLY,
        [
            pltpu.VMEM((EARLY, ys, count, rows, cols, width), a.dtype),
            pltpu.SemaphoreType.DMA((EARLY, ys)),
        ],
        limit=LARGE,
    )
    return f(at, a)


def first_body(o, a_ref, b_ref, out_ref):
    for y in range(2):
        put(out_ref, y, jnp.dot(a_ref[o, y], b_ref[...], preferred_element_type=jnp.float32))


def first(o, a, b):
    m, (k, n) = a.shape[1] * a.shape[2], b.shape
    f = call(
        lambda *refs: first_body(o, *refs),
        [VMEM, VMEM],
        shape((m, n), jnp.float32),
        2 * m * n * k,
        2 * m * k + 4 * m * n,
    )
    return f(a, b)


def later_body(o, at_ref, a_ref, b_ref, out_ref, buf, sem):
    for copy in fetch(at_ref[o], a_ref, buf, sem):
        copy.start()
    for y, copy in enumerate(fetch(at_ref[o], a_ref, buf, sem)):
        copy.wait()
        put(out_ref, y, jnp.dot(flat(buf[y]), b_ref[...], preferred_element_type=jnp.float32))


def later(o, at, a, b):
    count, ys, _, rows, cols, width = a.shape
    _, n = b.shape
    m = ys * count * rows
    f = call(
        lambda *refs: later_body(o, *refs),
        [SMEM, HBM, VMEM],
        shape((m, n), jnp.float32),
        m * n,
        m,
        [pltpu.VMEM((ys, count, rows, cols, width), a.dtype), pltpu.SemaphoreType.DMA((ys,))],
        limit=LARGE,
    )
    return f(at, a, b)


def step_body(s, first, *refs):
    *q_ref, own_ref, other_ref, out_ref = refs
    m = own_ref.shape[0]
    n = out_ref.shape[1]
    v = own_ref[:, s * n : (s + 1) * n] + other_ref[:, s * n : (s + 1) * n]
    if not first:
        v = v + decode(q_ref[0], m)
    out_ref[0:m, :], out_ref[m : m + TAIL, :] = encode(v)


def step(s, n, q, own, other):
    m = own.shape[0]
    qs = [] if q is None else [q]
    f = call(
        lambda *refs: step_body(s, q is None, *refs),
        [VMEM] * (len(qs) + 2),
        shape((m + TAIL, n), jnp.int16),
        8 * m * n,
        12 * m * n,
    )
    return f(*qs, own, other)


def split_body(s, at_ref, q_ref, own_ref, other_ref, mine_ref, *out_refs):
    m = own_ref.shape[0]
    n = q_ref.shape[1]
    part = m // 4
    up = jnp.full((1, n), at_ref[1], jnp.int32) == 0
    scale = scale_of(q_ref, m)
    cols = slice(s * n, (s + 1) * n)
    for k in range(4):
        rows = pl.ds(pl.multiple_of((at_ref[0] ^ k) * part, part), part)
        v = q_ref[rows, :].astype(jnp.int32).astype(jnp.float32) * scale
        v = v + jnp.where(up, own_ref[rows, cols] + other_ref[rows, cols], 0.0)
        if k == 0:
            mine_ref[...] = v
        else:
            out_refs[k - 1][0:part, :], out_refs[k - 1][part : part + TAIL, :] = encode(v)


def split(s, at, q, own, other):
    m = own.shape[0]
    n = q.shape[1]
    part = m // 4
    f = call(
        lambda *refs: split_body(s, *refs),
        [SMEM] + [VMEM] * 3,
        [shape((part, n), jnp.float32)] + [shape((part + TAIL, n), jnp.int16)] * 3,
        8 * m * n,
        12 * m * n,
    )
    return f(at, q, own, other)


def close_body(keep_ref, *refs):
    *in_refs, out_ref = refs
    m, count, n = out_ref.shape
    for s in range(count):
        mine, *got = in_refs[4 * s : 4 * s + 4]
        v = mine[...] + sum(decode(g, m) for g in got)
        out_ref[:, s, :] = jnp.where(keep_ref[:, s * n : (s + 1) * n] > 0, -v, 0.0)


def close(keep, streams):
    m, n = streams[0][0].shape
    count = len(streams)
    f = call(
        close_body,
        [VMEM] * (1 + 4 * count),
        jax.ShapeDtypeStruct((m, count, n), jnp.float32),
        8 * count * m * n,
        14 * count * m * n,
    )
    return f(keep, *[x for stream in streams for x in stream])


def per_device(inverse_tiles, factor_panels, ancestors, valid_flags, block_slot):
    local_rows, width, local_cols, _ = inverse_tiles.shape
    count = factor_panels.shape[0]
    row, col = lax.axis_index("row"), lax.axis_index("col")
    core, z, ylo = row % 2, (row // 2) % NZ, row // (2 * NZ)
    x, yhi = col // 2, col % 2

    across = lax.ppermute(factor_panels, "col", col_perm(0, 1))
    direct = [lax.ppermute(factor_panels, "col", col_perm(d, 0)) for d in (2, 1, 3)]
    onward = [lax.ppermute(across, "col", col_perm(d, 0)) for d in (2, 1, 3)]
    places = [col, x * 2 + 1 - yhi]
    places += [((x - d) % 4) * 2 + yhi for d in (2, 1, 3)]
    places += [((x - d) % 4) * 2 + 1 - yhi for d in (2, 1, 3)]

    ancestors, across = lax.optimization_barrier((ancestors, across))
    member = membership(ancestors, valid_flags, block_slot)
    col_member = lax.dynamic_slice_in_dim(member, row * local_cols, local_cols, 1)
    row_member = lax.dynamic_slice_in_dim(member, col * local_rows, local_rows, 1)
    rowmask = jnp.repeat(jnp.transpose(row_member).astype(jnp.float32), width // 32, axis=0)
    rowmask = jnp.repeat(rowmask, width, axis=1)

    tiles = inverse_tiles.reshape(local_rows, 2, NZ, width // 16, local_cols, width)

    panels = assemble(
        jnp.stack(places).astype(jnp.int32),
        col_member.reshape(-1).astype(jnp.int32),
        [factor_panels, across] + direct + onward,
    )

    def dest(c, t):
        up = z if t == 1 else z + 5 - t
        return (jnp.where(c == 1, z - 5 + t, up) + NZ) % NZ

    at = jnp.stack([dest(c, t) for t in range(1, STEPS + 1) for c in (1 - core, core)])
    at = at.astype(jnp.int32)
    early = prepare(at, tiles)

    def terms(t, at):
        def multiply(o):
            n = 2 * (t - 1) + o
            return first(n, early, panels) if n < EARLY else later(n, at, tiles, panels)

        theirs = multiply(0)
        other = lax.ppermute(theirs, "row", CORE)
        return multiply(1), other

    here = jnp.stack([ylo * 2 + core, core]).astype(jnp.int32)
    parts = [terms(t, at) for t in range(1, STEPS + 1)]
    moving = [None] * count
    for t in range(1, STEPS + 1):
        for s in range(count):
            coded = step(s, width, moving[s], *parts[t - 1])
            moving[s] = lax.ppermute(coded, "row", FIRST if t == 1 else ARM)
    streams = []
    for s in range(count):
        mine, *rest = split(s, here, moving[s], *parts[0])
        got = [
            lax.ppermute(
                rest[k - 1], "row", row_perm(lambda y, zz, c, k=k: (y ^ (k >> 1), zz, c ^ (k & 1)))
            )
            for k in range(1, 4)
        ]
        streams.append([mine] + got)
    return close(rowmask, streams).reshape(local_rows, width // 32, count, width)


def solution(mesh):
    return jax.shard_map(
        per_device,
        mesh=mesh,
        in_specs=(P("col", None, "row", None), P(None, "row", "col", None), P(), P(), P()),
        out_specs=P("col", "row", None, None),
        check_vma=False,
    )
```

time: 326 us -> 94.2 us (0.29)
  the two profiles are of different devices: /device:TPU:2 before, /device:TPU:1 now
where the time goes in v1:
time: 94.2 us; the launch traced here: 93.5 us
  Pallas kernels  38.5 us (41%)
  starting transfers between devices  35.7 us (38%)
  waiting for transfers between devices  12.1 us (13%)
  local copies, waits for them, and re-layouts  5.58 us (6%)
  other arithmetic  1.22 us (1%)
    ppermute x8, starting transfers between devices, per_device(): moving[s] = lax.ppermute(coded, 'row', FIRST if t == 1 else ARM)  17.1 us
    pallas_call x4, Pallas kernels, later(): return f(at, a, b)  15 us
    pallas_call x8, Pallas kernels, step(): return f(*qs, own, other)  11.2 us
    ppermute x3, waiting for transfers between devices, per_device(): onward = [lax.ppermute(across, 'col', col_perm(d, 0)) for d in (2, 1, 3)]  5.44 us
    ppermute x3, starting transfers between devices, per_device(): lax.ppermute(factor_panels, 'col', col_perm(d, 0))  5.42 us
    pallas_call x4, Pallas kernels, first(): return f(a, b)  4.86 us
    unnamed x17, local copies, waits for them, and re-layouts  4.55 us
    ppermute x6, starting transfers between devices, per_device(): lax.ppermute(rest[k - 1], 'row', row_perm(lambda y, zz, c, k=k: (y ^ k >>...  4.44 us
  transfers between devices with their start and end apart: 25, of which 7 were waited for; matrix products, arithmetic and copies ran while one was open for 2% of the time, Pallas kernels for 38%

profile of v1, /device:TPU:1, one launch (start us, length us, event | category | flops | bytes accessed | tf_op | source)
XLA Modules:
  0.0 93.5 jit_solution(17513425095541531804)
XLA Ops:
  0.0 3.8 %collective-permute-start = (bf16[2,4,32,256]{3,2,1,0:T(8,128)(2,1)}, bf16[2,4,32,256]{3,2,1,0:T(8,128)(2,1)S(1)}, u32[]{:S(2)}, u32[]{:S(2)}) collective-permute-start(bf16[2,4,32,256]{3,2,1,0:T(8,128)(2,1)} %refs_0_.1), channel_id=1, source_target_pairs={{0,1},{1,0},{2,3},{3,2},{4,5},{5,4},{6,7},{7,6},{8,9},{9,8},{10,11... | collective-permute-start | bytes 393224 | tf_op jit(solution)/shard_map/ppermute | solution.py:272
  3.8 2.7 %collective-permute-start.1 = (bf16[2,4,32,256]{3,2,1,0:T(8,128)(2,1)}, bf16[2,4,32,256]{3,2,1,0:T(8,128)(2,1)S(1)}, u32[]{:S(2)}, u32[]{:S(2)}) collective-permute-start(bf16[2,4,32,256]{3,2,1,0:T(8,128)(2,1)} %refs_0_.1), channel_id=1, source_target_pairs={{0,4},{1,5},{2,6},{3,7},{4,0},{5,1},{6,2},{7,3},{8,12},{9,13},{10,... | collective-permute-start | bytes 393224 | tf_op jit(solution)/shard_map/ppermute | solution.py:273
  6.9 2.4 %collective-permute-start.3 = (bf16[2,4,32,256]{3,2,1,0:T(8,128)(2,1)}, bf16[2,4,32,256]{3,2,1,0:T(8,128)(2,1)S(1)}, u32[]{:S(2)}, u32[]{:S(2)}) collective-permute-start(bf16[2,4,32,256]{3,2,1,0:T(8,128)(2,1)} %refs_0_.1), channel_id=1, source_target_pairs={{0,6},{1,7},{2,0},{3,1},{4,2},{5,3},{6,4},{7,5},{8,14},{9,15},{10,... | collective-permute-start | bytes 393224 | tf_op jit(solution)/shard_map/ppermute | solution.py:273
  9.3 0.7 broadcast_compare_fusion
  9.9 0.6 stack.74.at_ref.refs_0_
  10.5 3.0 %shard_map.55.refs_0_ = bf16[4,2,256,1024]{3,2,1,0:T(8,128)(2,1)S(1)} custom-call(s32[8]{0:T(128)} %stack.74.at_ref.refs_0_, bf16[16,2,8,16,4,256]{5,4,3,2,1,0:T(4,128)(2,1)} %bitcast.36), custom_call_target="tpu_custom_call" | custom-call | bytes 8388608 | tf_op jit(solution)/shard_map/pallas_call | solution.py:145
  13.5 1.9 %copy-done = bf16[4,2,256,1024]{3,2,1,0:T(8,128)(2,1)} copy-done((bf16[4,2,256,1024]{3,2,1,0:T(8,128)(2,1)}, bf16[4,2,256,1024]{3,2,1,0:T(8,128)(2,1)S(1)}, u32[]{:S(2)}) %copy-start) | copy-done | bytes 4194328
  15.7 0.6 collective-permute-start.5
  16.4 2.3 %collective-permute-start.6 = (bf16[2,4,32,256]{3,2,1,0:T(8,128)(2,1)S(1)}, bf16[2,4,32,256]{3,2,1,0:T(8,128)(2,1)S(1)}, u32[]{:S(2)}, u32[]{:S(2)}) collective-permute-start(bf16[2,4,32,256]{3,2,1,0:T(8,128)(2,1)S(1)} %collective-permute-done.refs_1_), channel_id=1, source_target_pairs={{0,6},{1,7},{2,0},{3,1},{4,2},{5,3},{6,4},{7,5},{8,14},{9,15},{10,... | collective-permute-start | bytes 393224 | tf_op jit(solution)/shard_map/ppermute | solution.py:274
  19.0 2.1 %collective-permute-done.4.refs_5_ = bf16[2,4,32,256]{3,2,1,0:T(8,128)(2,1)S(1)} collective-permute-done((bf16[2,4,32,256]{3,2,1,0:T(8,128)(2,1)S(1)}, bf16[2,4,32,256]{3,2,1,0:T(8,128)(2,1)S(1)}, u32[]{:S(2)}, u32[]{:S(2)}) %collective-permute-start.4) | collective-permute-done | bytes 131104 | tf_op jit(solution)/shard_map/ppermute | solution.py:274
  21.1 3.4 %collective-permute-done.5.refs_6_ = bf16[2,4,32,256]{3,2,1,0:T(8,128)(2,1)S(1)} collective-permute-done((bf16[2,4,32,256]{3,2,1,0:T(8,128)(2,1)S(1)}, bf16[2,4,32,256]{3,2,1,0:T(8,128)(2,1)S(1)}, u32[]{:S(2)}, u32[]{:S(2)}) %collective-permute-start.5) | collective-permute-done | bytes 131104 | tf_op jit(solution)/shard_map/ppermute | solution.py:274
  24.4 0.7 shard_map.56
  25.1 2.6 %copy-done.1 = bf16[4,2,256,1024]{3,2,1,0:T(8,128)(2,1)S(1)} copy-done((bf16[4,2,256,1024]{3,2,1,0:T(8,128)(2,1)S(1)}, bf16[4,2,256,1024]{3,2,1,0:T(8,128)(2,1)}, u32[]{:S(2)}) %copy-start.1) | copy-done | bytes 4194328
  27.7 1.8 %shard_map.58 = f32[512,512]{1,0:T(8,128)} custom-call(bf16[4,2,256,1024]{3,2,1,0:T(8,128)(2,1)S(1)} %copy-done.1, bf16[1024,512]{1,0:T(8,128)(2,1)S(1)} %bitcast.27), custom_call_target="tpu_custom_call" | custom-call | flops 536870912 | bytes 2097152 | tf_op jit(solution)/shard_map/pallas_call | solution.py:162
  29.5 1.2 %collective-permute-start.7 = (f32[512,512]{1,0:T(8,128)}, f32[512,512]{1,0:T(8,128)}, u32[]{:S(2)}, u32[]{:S(2)}) collective-permute-start(f32[512,512]{1,0:T(8,128)} %shard_map.58), channel_id=1, source_target_pairs={{0,8},{8,0},{16,24},{24,16},{32,40},{40,32},{48,56},{56,48},{64,72... | collective-permute-start | bytes 3145736 | tf_op jit(solution)/shard_map/ppermute | solution.py:308
  30.7 1.7 %shard_map.61 = f32[512,512]{1,0:T(8,128)} custom-call(bf16[4,2,256,1024]{3,2,1,0:T(8,128)(2,1)S(1)} %copy-done.1, bf16[1024,512]{1,0:T(8,128)(2,1)S(1)} %bitcast.28), custom_call_target="tpu_custom_call" | custom-call | flops 536870912 | bytes 2097152 | tf_op jit(solution)/shard_map/pallas_call | solution.py:162
  32.4 4.5 %shard_map.64 = f32[512,512]{1,0:T(8,128)} custom-call(s32[8]{0:T(128)} %stack.74.at_ref.refs_0_, bf16[16,2,8,16,4,256]{5,4,3,2,1,0:T(4,128)(2,1)} %bitcast.37, bf16[1024,512]{1,0:T(8,128)(2,1)} %bitcast.29), custom_call_target="tpu_custom_call" | custom-call | flops 262144 | bytes 512 | tf_op jit(solution)/shard_map/pallas_call | solution.py:186
  37.0 0.5 collective-permute-start.11
  37.5 4.1 %shard_map.67 = f32[512,512]{1,0:T(8,128)} custom-call(s32[8]{0:T(128)} %stack.74.at_ref.refs_0_, bf16[16,2,8,16,4,256]{5,4,3,2,1,0:T(4,128)(2,1)} %bitcast.38, bf16[1024,512]{1,0:T(8,128)(2,1)} %bitcast.30), custom_call_target="tpu_custom_call" | custom-call | flops 262144 | bytes 512 | tf_op jit(solution)/shard_map/pallas_call | solution.py:186
  41.9 0.7 shard_map.57.refs_0_.refs_2_
  42.6 1.4 %shard_map.70 = s16[528,256]{1,0:T(8,128)(2,1)S(1)} custom-call(f32[512,512]{1,0:T(8,128)S(1)} %shard_map.57.refs_0_.refs_2_, f32[512,512]{1,0:T(8,128)} %collective-permute-done.7.refs_1_.refs_3_), custom_call_target="tpu_custom_call" | custom-call | flops 1048576 | bytes 1572864 | tf_op jit(solution)/shard_map/pallas_call | solution.py:209
  44.0 7.5 %collective-permute-start.18 = (s16[528,256]{1,0:T(8,128)(2,1)S(1)}, s16[528,256]{1,0:T(8,128)(2,1)S(1)}, u32[]{:S(2)}, u32[]{:S(2)}) collective-permute-start(s16[528,256]{1,0:T(8,128)(2,1)S(1)} %shard_map.70), channel_id=1, source_target_pairs={{8,120},{24,8},{40,24},{56,40},{72,56},{88,72},{104,88},{120,104},... | collective-permute-start | bytes 811016 | tf_op jit(solution)/shard_map/ppermute | solution.py:317
  51.5 1.4 %shard_map.59 = s16[528,256]{1,0:T(8,128)(2,1)S(1)} custom-call(f32[512,512]{1,0:T(8,128)S(1)} %shard_map.57.refs_0_.refs_2_, f32[512,512]{1,0:T(8,128)} %collective-permute-done.7.refs_1_.refs_3_), custom_call_target="tpu_custom_call" | custom-call | flops 1048576 | bytes 1572864 | tf_op jit(solution)/shard_map/pallas_call | solution.py:209
  52.9 2.8 %collective-permute-start.8 = (s16[528,256]{1,0:T(8,128)(2,1)S(1)}, s16[528,256]{1,0:T(8,128)(2,1)S(1)}, u32[]{:S(2)}, u32[]{:S(2)}) collective-permute-start(s16[528,256]{1,0:T(8,128)(2,1)S(1)} %shard_map.59), channel_id=1, source_target_pairs={{8,120},{24,8},{40,24},{56,40},{72,56},{88,72},{104,88},{120,104},... | collective-permute-start | bytes 811016 | tf_op jit(solution)/shard_map/ppermute | solution.py:317
  55.7 0.7 shard_map.60.refs_1_
  56.4 1.4 %shard_map.71 = s16[528,256]{1,0:T(8,128)(2,1)S(1)} custom-call(s16[528,256]{1,0:T(8,128)(2,1)S(1)} %collective-permute-done.18.refs_0_, f32[512,512]{1,0:T(8,128)S(1)} %shard_map.60.refs_1_, f32[512,512]{1,0:T(8,128)} %collective-permute-done.9.refs_2_), custom_call_target="tpu_custom_call" | custom-call | flops 1048576 | bytes 1572864 | tf_op jit(solution)/shard_map/pallas_call | solution.py:209
  57.9 1.6 %collective-permute-start.19 = (s16[528,256]{1,0:T(8,128)(2,1)S(1)}, s16[528,256]{1,0:T(8,128)(2,1)S(1)}, u32[]{:S(2)}, u32[]{:S(2)}) collective-permute-start(s16[528,256]{1,0:T(8,128)(2,1)S(1)} %shard_map.71), channel_id=1, source_target_pairs={{0,16},{8,120},{16,32},{24,8},{32,48},{40,24},{48,64},{56,40},{64,... | collective-permute-start | bytes 811016 | tf_op jit(solution)/shard_map/ppermute | solution.py:317
  59.5 0.9 collective-permute-done.8.refs_0_
  60.4 1.4 %shard_map.62 = s16[528,256]{1,0:T(8,128)(2,1)S(1)} custom-call(s16[528,256]{1,0:T(8,128)(2,1)S(1)} %collective-permute-done.8.refs_0_, f32[512,512]{1,0:T(8,128)S(1)} %shard_map.60.refs_1_, f32[512,512]{1,0:T(8,128)} %collective-permute-done.9.refs_2_), custom_call_target="tpu_custom_call" | custom-call | flops 1048576 | bytes 1572864 | tf_op jit(solution)/shard_map/pallas_call | solution.py:209
  61.8 1.7 %collective-permute-start.10 = (s16[528,256]{1,0:T(8,128)(2,1)S(1)}, s16[528,256]{1,0:T(8,128)(2,1)S(1)}, u32[]{:S(2)}, u32[]{:S(2)}) collective-permute-start(s16[528,256]{1,0:T(8,128)(2,1)S(1)} %shard_map.62), channel_id=1, source_target_pairs={{0,16},{8,120},{16,32},{24,8},{32,48},{40,24},{48,64},{56,40},{64,... | collective-permute-start | bytes 811016 | tf_op jit(solution)/shard_map/ppermute | solution.py:317
  63.5 3.2 %shard_map.63.refs_1_ = f32[512,512]{1,0:T(8,128)S(1)} custom-call(s32[8]{0:T(128)} %stack.74.at_ref.refs_0_, bf16[16,2,8,16,4,256]{5,4,3,2,1,0:T(4,128)(2,1)} %bitcast.39, bf16[1024,512]{1,0:T(8,128)(2,1)} %bitcast.31), custom_call_target="tpu_custom_call" | custom-call | flops 262144 | bytes 512 | tf_op jit(solution)/shard_map/pallas_call | solution.py:186
  66.7 1.4 %shard_map.72 = s16[528,256]{1,0:T(8,128)(2,1)S(1)} custom-call(s16[528,256]{1,0:T(8,128)(2,1)S(1)} %collective-permute-done.19.refs_0_, f32[512,512]{1,0:T(8,128)S(1)} %shard_map.63.refs_1_, f32[512,512]{1,0:T(8,128)} %collective-permute-done.11.refs_2_), custom_call_target="tpu_custom_call" | custom-call | flops 1048576 | bytes 1572864 | tf_op jit(solution)/shard_map/pallas_call | solution.py:209
  68.2 1.4 %shard_map.65 = s16[528,256]{1,0:T(8,128)(2,1)S(1)} custom-call(s16[528,256]{1,0:T(8,128)(2,1)S(1)} %collective-permute-done.10.refs_0_, f32[512,512]{1,0:T(8,128)S(1)} %shard_map.63.refs_1_, f32[512,512]{1,0:T(8,128)} %collective-permute-done.11.refs_2_), custom_call_target="tpu_custom_call" | custom-call | flops 1048576 | bytes 1572864 | tf_op jit(solution)/shard_map/pallas_call | solution.py:209
  69.7 1.9 %collective-permute-start.12 = (s16[528,256]{1,0:T(8,128)(2,1)S(1)}, s16[528,256]{1,0:T(8,128)(2,1)S(1)}, u32[]{:S(2)}, u32[]{:S(2)}) collective-permute-start(s16[528,256]{1,0:T(8,128)(2,1)S(1)} %shard_map.65), channel_id=1, source_target_pairs={{0,16},{8,120},{16,32},{24,8},{32,48},{40,24},{48,64},{56,40},{64,... | collective-permute-start | bytes 811016 | tf_op jit(solution)/shard_map/ppermute | solution.py:317
  71.5 3.2 %shard_map.66.refs_1_ = f32[512,512]{1,0:T(8,128)S(1)} custom-call(s32[8]{0:T(128)} %stack.74.at_ref.refs_0_, bf16[16,2,8,16,4,256]{5,4,3,2,1,0:T(4,128)(2,1)} %bitcast.40, bf16[1024,512]{1,0:T(8,128)(2,1)} %bitcast.32), custom_call_target="tpu_custom_call" | custom-call | flops 262144 | bytes 512 | tf_op jit(solution)/shard_map/pallas_call | solution.py:186
  74.7 1.4 %shard_map.73 = s16[528,256]{1,0:T(8,128)(2,1)S(1)} custom-call(s16[528,256]{1,0:T(8,128)(2,1)S(1)} %collective-permute-done.20.refs_0_, f32[512,512]{1,0:T(8,128)S(1)} %shard_map.66.refs_1_, f32[512,512]{1,0:T(8,128)} %collective-permute-done.13.refs_2_), custom_call_target="tpu_custom_call" | custom-call | flops 1048576 | bytes 1572864 | tf_op jit(solution)/shard_map/pallas_call | solution.py:209
  76.2 0.5 collective-permute-done.12.refs_0_
  76.7 1.4 %shard_map.68 = s16[528,256]{1,0:T(8,128)(2,1)S(1)} custom-call(s16[528,256]{1,0:T(8,128)(2,1)S(1)} %collective-permute-done.12.refs_0_, f32[512,512]{1,0:T(8,128)S(1)} %shard_map.66.refs_1_, f32[512,512]{1,0:T(8,128)} %collective-permute-done.13.refs_2_), custom_call_target="tpu_custom_call" | custom-call | flops 1048576 | bytes 1572864 | tf_op jit(solution)/shard_map/pallas_call | solution.py:209
  78.1 1.4 %collective-permute-start.14 = (s16[528,256]{1,0:T(8,128)(2,1)S(1)}, s16[528,256]{1,0:T(8,128)(2,1)S(1)}, u32[]{:S(2)}, u32[]{:S(2)}) collective-permute-start(s16[528,256]{1,0:T(8,128)(2,1)S(1)} %shard_map.68), channel_id=1, source_target_pairs={{0,16},{8,120},{16,32},{24,8},{32,48},{40,24},{48,64},{56,40},{64,... | collective-permute-start | bytes 811016 | tf_op jit(solution)/shard_map/ppermute | solution.py:317
  79.6 1.9 %collective-permute-done.21.refs_1_ = s16[528,256]{1,0:T(8,128)(2,1)S(1)} collective-permute-done((s16[528,256]{1,0:T(8,128)(2,1)S(1)}, s16[528,256]{1,0:T(8,128)(2,1)S(1)}, u32[]{:S(2)}, u32[]{:S(2)}) %collective-permute-start.21) | collective-permute-done | bytes 270368 | tf_op jit(solution)/shard_map/ppermute | solution.py:317
  81.5 1.4 %shard_map.74 = (f32[128,256]{1,0:T(8,128)S(1)}, s16[144,256]{1,0:T(8,128)(2,1)S(1)}, s16[144,256]{1,0:T(8,128)(2,1)S(1)}, s16[144,256]{1,0:T(8,128)(2,1)S(1)}) custom-call(s32[2]{0:T(128)S(1)} %pad_add_fusion.refs_0_, s16[528,256]{1,0:T(8,128)(2,1)S(1)} %collective-permute-done.21.refs_1_, f32[512,512]{1,0:T(8,128)S(1)} %shard_map.57.refs_0_.refs_2_, ...), custom_call_target="tpu_custom_call" | custom-call | flops 1048576 | bytes 1572864 | tf_op jit(solution)/shard_map/pallas_call | solution.py:240
  83.6 1.7 %collective-permute-start.24 = (s16[144,256]{1,0:T(8,128)(2,1)S(1)}, s16[144,256]{1,0:T(8,128)(2,1)S(1)}, u32[]{:S(2)}, u32[]{:S(2)}) collective-permute-start(s16[144,256]{1,0:T(8,128)(2,1)S(1)} %get-tuple-element.24), channel_id=1, source_target_pairs={{0,136},{8,128},{16,152},{24,144},{32,168},{40,160},{48,184},{56,1... | collective-permute-start | bytes 221192 | tf_op jit(solution)/shard_map/ppermute | solution.py:322
  85.3 1.4 %shard_map.69 = (f32[128,256]{1,0:T(8,128)S(1)}, s16[144,256]{1,0:T(8,128)(2,1)S(1)}, s16[144,256]{1,0:T(8,128)(2,1)S(1)}, s16[144,256]{1,0:T(8,128)(2,1)S(1)}) custom-call(s32[2]{0:T(128)S(1)} %pad_add_fusion.refs_0_, s16[528,256]{1,0:T(8,128)(2,1)S(1)} %collective-permute-done.14.refs_1_, f32[512,512]{1,0:T(8,128)S(1)} %shard_map.57.refs_0_.refs_2_, ...), custom_call_target="tpu_custom_call" | custom-call | flops 1048576 | bytes 1572864 | tf_op jit(solution)/shard_map/pallas_call | solution.py:240
  86.9 0.5 collective-permute-start.16
  87.3 1.7 %collective-permute-start.17 = (s16[144,256]{1,0:T(8,128)(2,1)S(1)}, s16[144,256]{1,0:T(8,128)(2,1)S(1)}, u32[]{:S(2)}, u32[]{:S(2)}) collective-permute-start(s16[144,256]{1,0:T(8,128)(2,1)S(1)} %get-tuple-element.20), channel_id=1, source_target_pairs={{0,136},{8,128},{16,152},{24,144},{32,168},{40,160},{48,184},{56,1... | collective-permute-start | bytes 221192 | tf_op jit(solution)/shard_map/ppermute | solution.py:322
  89.3 0.9 collective-permute-done.16.refs_2_
  90.1 2.4 %collective-permute-done.17.refs_3_ = s16[144,256]{1,0:T(8,128)(2,1)S(1)} collective-permute-done((s16[144,256]{1,0:T(8,128)(2,1)S(1)}, s16[144,256]{1,0:T(8,128)(2,1)S(1)}, u32[]{:S(2)}, u32[]{:S(2)}) %collective-permute-start.17) | collective-permute-done | bytes 73760 | tf_op jit(solution)/shard_map/ppermute | solution.py:322
  92.6 0.9 shard_map.75
  (52 shorter events, 2.5 us)
Async XLA Ops:
  0.0 24.4 %copy-start.5 = (bf16[2,4,32,256]{3,2,1,0:T(8,128)(2,1)S(1)}, bf16[2,4,32,256]{3,2,1,0:T(8,128)(2,1)}, u32[]{:S(2)}) copy-start(bf16[2,4,32,256]{3,2,1,0:T(8,128)(2,1)} %refs_0_.1) | copy-start | bytes 393220
  0.0 16.2 %copy-start.6 = (s32[2,96]{1,0:T(2,128)S(1)}, s32[2,96]{1,0:T(2,128)}, u32[]{:S(2)}) copy-start(s32[2,96]{1,0:T(2,128)} %param.7) | copy-start | bytes 2308
  0.0 16.2 %copy-start.7 = (s32[128]{0:T(128)S(1)}, s32[128]{0:T(128)}, u32[]{:S(2)}) copy-start(s32[128]{0:T(128)} %param.9) | copy-start | bytes 1540
  0.0 15.6 %collective-permute-start = (bf16[2,4,32,256]{3,2,1,0:T(8,128)(2,1)}, bf16[2,4,32,256]{3,2,1,0:T(8,128)(2,1)S(1)}, u32[]{:S(2)}, u32[]{:S(2)}) collective-permute-start(bf16[2,4,32,256]{3,2,1,0:T(8,128)(2,1)} %refs_0_.1), channel_id=1, source_target_pairs={{0,1},{1,0},{2,3},{3,2},{4,5},{5,4},{6,7},{7,6},{8,9},{9,8},{10,11... | collective-permute-start | bytes 393224 | tf_op jit(solution)/shard_map/ppermute | solution.py:272
  3.8 12.6 %collective-permute-start.1 = (bf16[2,4,32,256]{3,2,1,0:T(8,128)(2,1)}, bf16[2,4,32,256]{3,2,1,0:T(8,128)(2,1)S(1)}, u32[]{:S(2)}, u32[]{:S(2)}) collective-permute-start(bf16[2,4,32,256]{3,2,1,0:T(8,128)(2,1)} %refs_0_.1), channel_id=1, source_target_pairs={{0,4},{1,5},{2,6},{3,7},{4,0},{5,1},{6,2},{7,3},{8,12},{9,13},{10,... | collective-permute-start | bytes 393224 | tf_op jit(solution)/shard_map/ppermute | solution.py:273
  6.6 12.4 %collective-permute-start.2 = (bf16[2,4,32,256]{3,2,1,0:T(8,128)(2,1)}, bf16[2,4,32,256]{3,2,1,0:T(8,128)(2,1)S(1)}, u32[]{:S(2)}, u32[]{:S(2)}) collective-permute-start(bf16[2,4,32,256]{3,2,1,0:T(8,128)(2,1)} %refs_0_.1), channel_id=1, source_target_pairs={{0,2},{1,3},{2,4},{3,5},{4,6},{5,7},{6,0},{7,1},{8,10},{9,11},{10,... | collective-permute-start | bytes 393224 | tf_op jit(solution)/shard_map/ppermute | solution.py:273
  6.9 12.1 %collective-permute-start.3 = (bf16[2,4,32,256]{3,2,1,0:T(8,128)(2,1)}, bf16[2,4,32,256]{3,2,1,0:T(8,128)(2,1)S(1)}, u32[]{:S(2)}, u32[]{:S(2)}) collective-permute-start(bf16[2,4,32,256]{3,2,1,0:T(8,128)(2,1)} %refs_0_.1), channel_id=1, source_target_pairs={{0,6},{1,7},{2,0},{3,1},{4,2},{5,3},{6,4},{7,5},{8,14},{9,15},{10,... | collective-permute-start | bytes 393224 | tf_op jit(solution)/shard_map/ppermute | solution.py:273
  13.5 2.0 %copy-start = (bf16[4,2,256,1024]{3,2,1,0:T(8,128)(2,1)}, bf16[4,2,256,1024]{3,2,1,0:T(8,128)(2,1)S(1)}, u32[]{:S(2)}) copy-start(bf16[4,2,256,1024]{3,2,1,0:T(8,128)(2,1)S(1)} %shard_map.55.refs_0_) | copy-start | bytes 12582916
  15.6 5.5 %collective-permute-start.4 = (bf16[2,4,32,256]{3,2,1,0:T(8,128)(2,1)S(1)}, bf16[2,4,32,256]{3,2,1,0:T(8,128)(2,1)S(1)}, u32[]{:S(2)}, u32[]{:S(2)}) collective-permute-start(bf16[2,4,32,256]{3,2,1,0:T(8,128)(2,1)S(1)} %collective-permute-done.refs_1_), channel_id=1, source_target_pairs={{0,4},{1,5},{2,6},{3,7},{4,0},{5,1},{6,2},{7,3},{8,12},{9,13},{10,... | collective-permute-start | bytes 393224 | tf_op jit(solution)/shard_map/ppermute | solution.py:274
  15.7 8.8 %collective-permute-start.5 = (bf16[2,4,32,256]{3,2,1,0:T(8,128)(2,1)S(1)}, bf16[2,4,32,256]{3,2,1,0:T(8,128)(2,1)S(1)}, u32[]{:S(2)}, u32[]{:S(2)}) collective-permute-start(bf16[2,4,32,256]{3,2,1,0:T(8,128)(2,1)S(1)} %collective-permute-done.refs_1_), channel_id=1, source_target_pairs={{0,2},{1,3},{2,4},{3,5},{4,6},{5,7},{6,0},{7,1},{8,10},{9,11},{10,... | collective-permute-start | bytes 393224 | tf_op jit(solution)/shard_map/ppermute | solution.py:274
  16.4 8.0 %collective-permute-start.6 = (bf16[2,4,32,256]{3,2,1,0:T(8,128)(2,1)S(1)}, bf16[2,4,32,256]{3,2,1,0:T(8,128)(2,1)S(1)}, u32[]{:S(2)}, u32[]{:S(2)}) collective-permute-start(bf16[2,4,32,256]{3,2,1,0:T(8,128)(2,1)S(1)} %collective-permute-done.refs_1_), channel_id=1, source_target_pairs={{0,6},{1,7},{2,0},{3,1},{4,2},{5,3},{6,4},{7,5},{8,14},{9,15},{10,... | collective-permute-start | bytes 393224 | tf_op jit(solution)/shard_map/ppermute | solution.py:274
  25.1 7.3 %copy-start.3 = (bf16[4,8,32,512]{3,2,1,0:T(8,128)(2,1)}, bf16[4,8,32,512]{3,2,1,0:T(8,128)(2,1)S(1)}, u32[]{:S(2)}) copy-start(bf16[4,8,32,512]{3,2,1,0:T(8,128)(2,1)S(1)} %shard_map.56) | copy-start | bytes 3145732
  25.1 2.6 %copy-start.1 = (bf16[4,2,256,1024]{3,2,1,0:T(8,128)(2,1)S(1)}, bf16[4,2,256,1024]{3,2,1,0:T(8,128)(2,1)}, u32[]{:S(2)}) copy-start(bf16[4,2,256,1024]{3,2,1,0:T(8,128)(2,1)} %copy-done) | copy-start | bytes 12582916
  29.5 13.1 %collective-permute-start.7 = (f32[512,512]{1,0:T(8,128)}, f32[512,512]{1,0:T(8,128)}, u32[]{:S(2)}, u32[]{:S(2)}) collective-permute-start(f32[512,512]{1,0:T(8,128)} %shard_map.58), channel_id=1, source_target_pairs={{0,8},{8,0},{16,24},{24,16},{32,40},{40,32},{48,56},{56,48},{64,72... | collective-permute-start | bytes 3145736 | tf_op jit(solution)/shard_map/ppermute | solution.py:308
  32.4 9.5 %copy-start.2 = (bf16[4,2,256,1024]{3,2,1,0:T(8,128)(2,1)S(1)}, bf16[4,2,256,1024]{3,2,1,0:T(8,128)(2,1)}, u32[]{:S(2)}) copy-start(bf16[4,2,256,1024]{3,2,1,0:T(8,128)(2,1)} %copy-done) | copy-start | bytes 12582916
  32.4 24.0 %collective-permute-start.9 = (f32[512,512]{1,0:T(8,128)}, f32[512,512]{1,0:T(8,128)}, u32[]{:S(2)}, u32[]{:S(2)}) collective-permute-start(f32[512,512]{1,0:T(8,128)} %shard_map.61), channel_id=1, source_target_pairs={{0,8},{8,0},{16,24},{24,16},{32,40},{40,32},{48,56},{56,48},{64,72... | collective-permute-start | bytes 3145736 | tf_op jit(solution)/shard_map/ppermute | solution.py:308
  37.0 4.9 %copy-start.4 = (bf16[4,8,32,512]{3,2,1,0:T(8,128)(2,1)S(1)}, bf16[4,8,32,512]{3,2,1,0:T(8,128)(2,1)}, u32[]{:S(2)}) copy-start(bf16[4,8,32,512]{3,2,1,0:T(8,128)(2,1)} %copy-done.3) | copy-start | bytes 3145732
  37.0 29.7 %collective-permute-start.11 = (f32[512,512]{1,0:T(8,128)}, f32[512,512]{1,0:T(8,128)}, u32[]{:S(2)}, u32[]{:S(2)}) collective-permute-start(f32[512,512]{1,0:T(8,128)} %shard_map.64), channel_id=1, source_target_pairs={{0,8},{8,0},{16,24},{24,16},{32,40},{40,32},{48,56},{56,48},{64,72... | collective-permute-start | bytes 3145736 | tf_op jit(solution)/shard_map/ppermute | solution.py:308
  41.6 33.1 %collective-permute-start.13 = (f32[512,512]{1,0:T(8,128)}, f32[512,512]{1,0:T(8,128)}, u32[]{:S(2)}, u32[]{:S(2)}) collective-permute-start(f32[512,512]{1,0:T(8,128)} %shard_map.67), channel_id=1, source_target_pairs={{0,8},{8,0},{16,24},{24,16},{32,40},{40,32},{48,56},{56,48},{64,72... | collective-permute-start | bytes 3145736 | tf_op jit(solution)/shard_map/ppermute | solution.py:308
  44.0 12.4 %collective-permute-start.18 = (s16[528,256]{1,0:T(8,128)(2,1)S(1)}, s16[528,256]{1,0:T(8,128)(2,1)S(1)}, u32[]{:S(2)}, u32[]{:S(2)}) collective-permute-start(s16[528,256]{1,0:T(8,128)(2,1)S(1)} %shard_map.70), channel_id=1, source_target_pairs={{8,120},{24,8},{40,24},{56,40},{72,56},{88,72},{104,88},{120,104},... | collective-permute-start | bytes 811016 | tf_op jit(solution)/shard_map/ppermute | solution.py:317
  52.9 7.5 %collective-permute-start.8 = (s16[528,256]{1,0:T(8,128)(2,1)S(1)}, s16[528,256]{1,0:T(8,128)(2,1)S(1)}, u32[]{:S(2)}, u32[]{:S(2)}) collective-permute-start(s16[528,256]{1,0:T(8,128)(2,1)S(1)} %shard_map.59), channel_id=1, source_target_pairs={{8,120},{24,8},{40,24},{56,40},{72,56},{88,72},{104,88},{120,104},... | collective-permute-start | bytes 811016 | tf_op jit(solution)/shard_map/ppermute | solution.py:317
  57.9 8.9 %collective-permute-start.19 = (s16[528,256]{1,0:T(8,128)(2,1)S(1)}, s16[528,256]{1,0:T(8,128)(2,1)S(1)}, u32[]{:S(2)}, u32[]{:S(2)}) collective-permute-start(s16[528,256]{1,0:T(8,128)(2,1)S(1)} %shard_map.71), channel_id=1, source_target_pairs={{0,16},{8,120},{16,32},{24,8},{32,48},{40,24},{48,64},{56,40},{64,... | collective-permute-start | bytes 811016 | tf_op jit(solution)/shard_map/ppermute | solution.py:317
  61.8 6.5 %collective-permute-start.10 = (s16[528,256]{1,0:T(8,128)(2,1)S(1)}, s16[528,256]{1,0:T(8,128)(2,1)S(1)}, u32[]{:S(2)}, u32[]{:S(2)}) collective-permute-start(s16[528,256]{1,0:T(8,128)(2,1)S(1)} %shard_map.62), channel_id=1, source_target_pairs={{0,16},{8,120},{16,32},{24,8},{32,48},{40,24},{48,64},{56,40},{64,... | collective-permute-start | bytes 811016 | tf_op jit(solution)/shard_map/ppermute | solution.py:317
  68.1 6.6 %collective-permute-start.20 = (s16[528,256]{1,0:T(8,128)(2,1)S(1)}, s16[528,256]{1,0:T(8,128)(2,1)S(1)}, u32[]{:S(2)}, u32[]{:S(2)}) collective-permute-start(s16[528,256]{1,0:T(8,128)(2,1)S(1)} %shard_map.72), channel_id=1, source_target_pairs={{0,16},{8,120},{16,32},{24,8},{32,48},{40,24},{48,64},{56,40},{64,... | collective-permute-start | bytes 811016 | tf_op jit(solution)/shard_map/ppermute | solution.py:317
  69.7 7.1 %collective-permute-start.12 = (s16[528,256]{1,0:T(8,128)(2,1)S(1)}, s16[528,256]{1,0:T(8,128)(2,1)S(1)}, u32[]{:S(2)}, u32[]{:S(2)}) collective-permute-start(s16[528,256]{1,0:T(8,128)(2,1)S(1)} %shard_map.65), channel_id=1, source_target_pairs={{0,16},{8,120},{16,32},{24,8},{32,48},{40,24},{48,64},{56,40},{64,... | collective-permute-start | bytes 811016 | tf_op jit(solution)/shard_map/ppermute | solution.py:317
  76.1 5.4 %collective-permute-start.21 = (s16[528,256]{1,0:T(8,128)(2,1)S(1)}, s16[528,256]{1,0:T(8,128)(2,1)S(1)}, u32[]{:S(2)}, u32[]{:S(2)}) collective-permute-start(s16[528,256]{1,0:T(8,128)(2,1)S(1)} %shard_map.73), channel_id=1, source_target_pairs={{0,16},{8,120},{16,32},{24,8},{32,48},{40,24},{48,64},{56,40},{64,... | collective-permute-start | bytes 811016 | tf_op jit(solution)/shard_map/ppermute | solution.py:317
  78.1 7.2 %collective-permute-start.14 = (s16[528,256]{1,0:T(8,128)(2,1)S(1)}, s16[528,256]{1,0:T(8,128)(2,1)S(1)}, u32[]{:S(2)}, u32[]{:S(2)}) collective-permute-start(s16[528,256]{1,0:T(8,128)(2,1)S(1)} %shard_map.68), channel_id=1, source_target_pairs={{0,16},{8,120},{16,32},{24,8},{32,48},{40,24},{48,64},{56,40},{64,... | collective-permute-start | bytes 811016 | tf_op jit(solution)/shard_map/ppermute | solution.py:317
  82.9 4.4 %collective-permute-start.22 = (s16[144,256]{1,0:T(8,128)(2,1)S(1)}, s16[144,256]{1,0:T(8,128)(2,1)S(1)}, u32[]{:S(2)}, u32[]{:S(2)}) collective-permute-start(s16[144,256]{1,0:T(8,128)(2,1)S(1)} %get-tuple-element.22), channel_id=1, source_target_pairs={{0,8},{8,0},{16,24},{24,16},{32,40},{40,32},{48,56},{56,48},{64,72... | collective-permute-start | bytes 221192 | tf_op jit(solution)/shard_map/ppermute | solution.py:322
  83.2 6.0 %collective-permute-start.23 = (s16[144,256]{1,0:T(8,128)(2,1)S(1)}, s16[144,256]{1,0:T(8,128)(2,1)S(1)}, u32[]{:S(2)}, u32[]{:S(2)}) collective-permute-start(s16[144,256]{1,0:T(8,128)(2,1)S(1)} %get-tuple-element.23), channel_id=1, source_target_pairs={{0,128},{8,136},{16,144},{24,152},{32,160},{40,168},{48,176},{56,1... | collective-permute-start | bytes 221192 | tf_op jit(solution)/shard_map/ppermute | solution.py:322
  83.6 5.6 %collective-permute-start.24 = (s16[144,256]{1,0:T(8,128)(2,1)S(1)}, s16[144,256]{1,0:T(8,128)(2,1)S(1)}, u32[]{:S(2)}, u32[]{:S(2)}) collective-permute-start(s16[144,256]{1,0:T(8,128)(2,1)S(1)} %get-tuple-element.24), channel_id=1, source_target_pairs={{0,136},{8,128},{16,152},{24,144},{32,168},{40,160},{48,184},{56,1... | collective-permute-start | bytes 221192 | tf_op jit(solution)/shard_map/ppermute | solution.py:322
  86.8 2.5 %collective-permute-start.15 = (s16[144,256]{1,0:T(8,128)(2,1)S(1)}, s16[144,256]{1,0:T(8,128)(2,1)S(1)}, u32[]{:S(2)}, u32[]{:S(2)}) collective-permute-start(s16[144,256]{1,0:T(8,128)(2,1)S(1)} %get-tuple-element.18), channel_id=1, source_target_pairs={{0,8},{8,0},{16,24},{24,16},{32,40},{40,32},{48,56},{56,48},{64,72... | collective-permute-start | bytes 221192 | tf_op jit(solution)/shard_map/ppermute | solution.py:322
  86.9 3.3 %collective-permute-start.16 = (s16[144,256]{1,0:T(8,128)(2,1)S(1)}, s16[144,256]{1,0:T(8,128)(2,1)S(1)}, u32[]{:S(2)}, u32[]{:S(2)}) collective-permute-start(s16[144,256]{1,0:T(8,128)(2,1)S(1)} %get-tuple-element.19), channel_id=1, source_target_pairs={{0,128},{8,136},{16,144},{24,152},{32,160},{40,168},{48,176},{56,1... | collective-permute-start | bytes 221192 | tf_op jit(solution)/shard_map/ppermute | solution.py:322
  87.3 5.3 %collective-permute-start.17 = (s16[144,256]{1,0:T(8,128)(2,1)S(1)}, s16[144,256]{1,0:T(8,128)(2,1)S(1)}, u32[]{:S(2)}, u32[]{:S(2)}) collective-permute-start(s16[144,256]{1,0:T(8,128)(2,1)S(1)} %get-tuple-element.20), channel_id=1, source_target_pairs={{0,136},{8,128},{16,152},{24,144},{32,168},{40,160},{48,184},{56,1... | collective-permute-start | bytes 221192 | tf_op jit(solution)/shard_map/ppermute | solution.py:322

commit v2 on v1

v2 whole, which is shorter than its diff:
```python
import math

import jax
import jax.numpy as jnp
from jax import lax
from jax.experimental import pallas as pl
from jax.experimental.pallas import tpu as pltpu
from jax.sharding import PartitionSpec as P


NZ = 8
STEPS = 4
HERE = 8 * STEPS
PLACES = HERE + 2
EARLY = 3
TOP = 32000.0
TAIL = 16


def membership(ancestors, valid_flags, block_slot):
    blocks = jnp.arange(block_slot.shape[0], dtype=jnp.int32)
    pick = (ancestors[:, :, None] == blocks[None, None, :]).astype(jnp.int32)
    slots = jnp.sum(pick * block_slot[None, None, :], axis=2)
    hits = (slots[:, :, None] == blocks[None, None, :]) & (valid_flags[:, :, None] == 1)
    return jnp.any(hits, axis=1)


def row_perm(move, cores=(0, 1)):
    pairs = []
    for r in range(32):
        ylo, z, core = r // 16, (r // 2) % NZ, r % 2
        if core in cores:
            y2, z2, c2 = move(ylo, z, core)
            pairs.append((r, ((y2 % 2) * NZ + z2 % NZ) * 2 + c2 % 2))
    return pairs


def col_perm(dx, dy):
    return [(c, ((c // 2 + dx) % 4) * 2 + (c % 2 + dy) % 2) for c in range(8)]


CORE = row_perm(lambda y, z, c: (y, z, 1 - c))
YLO = row_perm(lambda y, z, c: (1 - y, z, c))
ARM = row_perm(lambda y, z, c: (y, z + 1 - 2 * c, c))
ARM_CROSSED = row_perm(lambda y, z, c: (y, z + 1 - 2 * c, 1 - c))


def exponent(top):
    return jnp.ceil(jnp.log2(jnp.maximum(top, 1e-30) * (1.0 / TOP)))


def quantize(v, e):
    return jnp.round(v * jnp.exp2(-e)).astype(jnp.int32).astype(jnp.int16)


def tail(e):
    return jnp.broadcast_to(e, (TAIL, e.shape[1])).astype(jnp.int32).astype(jnp.int16)


def encode(v):
    e = exponent(jnp.max(jnp.abs(v), axis=0, keepdims=True))
    return quantize(v, e), tail(e)


def scale_of(ref, rows):
    e = ref[rows : rows + TAIL, :].astype(jnp.int32).astype(jnp.float32)
    return jnp.exp2(e[0:1, :])


def decode(ref, rows):
    return ref[0:rows, :].astype(jnp.int32).astype(jnp.float32) * scale_of(ref, rows)


VMEM = pl.BlockSpec(memory_space=pltpu.VMEM)
SMEM = pl.BlockSpec(memory_space=pltpu.SMEM)
HBM = pl.BlockSpec(memory_space=pltpu.HBM)


def call(body, in_specs, out_shape, flops, nbytes, scratch=(), limit=8 << 20):
    many = isinstance(out_shape, list)
    return pl.pallas_call(
        body,
        in_specs=in_specs,
        out_specs=[VMEM] * len(out_shape) if many else VMEM,
        out_shape=out_shape,
        scratch_shapes=list(scratch),
        compiler_params=pltpu.CompilerParams(vmem_limit_bytes=limit),
        cost_estimate=pl.CostEstimate(flops=flops, bytes_accessed=nbytes, transcendentals=0),
    )


def shape(dims, dtype):
    return pltpu.VMEM(dims, dtype)


def gather_body(at_ref, keep_ref, *refs):
    *pieces, out_ref = refs
    count, cols, _, width = pieces[0].shape
    for p, piece in enumerate(pieces):
        for s in range(count):
            for b in range(cols):
                value = piece[s, b]
                keep = jnp.full(value.shape, keep_ref[s * cols + b], jnp.int32) > 0
                out_ref[b, at_ref[PLACES + p], :, s * width : (s + 1) * width] = jnp.where(
                    keep, value, jnp.zeros_like(value)
                )


def assemble(at, keep, pieces):
    count, cols, rows, width = pieces[0].shape
    out = shape((cols, len(pieces), rows, count * width), pieces[0].dtype)
    f = call(gather_body, [SMEM, SMEM] + [VMEM] * len(pieces), out, 0, 4 * math.prod(out.shape))
    return f(at, keep, *pieces).reshape(-1, count * width)


def fetch(at_ref, o, a_ref, buf, sem):
    return [
        pltpu.make_async_copy(
            a_ref.at[:, at_ref[4 * o + 2 * h + 1], at_ref[4 * o + 2 * h]], buf.at[h], sem.at[h]
        )
        for h in range(2)
    ]


def flat(x):
    return x.reshape(-1, x.shape[2] * x.shape[3])


def put(out_ref, y, r):
    half = r.shape[0] // 2
    r = r.reshape(-1, 2, 8, r.shape[1])
    for c in range(2):
        start = (2 * y + c) * half
        out_ref[start : start + half, :] = r[:, c].reshape(half, r.shape[3])


def prepare_body(offset, at_ref, a_ref, *refs):
    *out_refs, buf, sem = refs
    count = 2 * len(out_refs)
    for o in range(count):
        for copy in fetch(at_ref, offset + o, a_ref, buf.at[o], sem.at[o]):
            copy.start()
    for o in range(count):
        for y, copy in enumerate(fetch(at_ref, offset + o, a_ref, buf.at[o], sem.at[o])):
            copy.wait()
            out_refs[o // 2][o % 2, y] = flat(buf[o, y])


def prepare(offset, steps, at, a, limit):
    count, ys, zs, rows, cols, width = a.shape
    f = call(
        lambda *refs: prepare_body(offset, *refs),
        [SMEM, HBM],
        [shape((2, ys, count * rows, cols * width), a.dtype)] * steps,
        0,
        8 * a.size // zs * steps,
        [
            pltpu.VMEM((2 * steps, ys, count, rows, cols, width), a.dtype),
            pltpu.SemaphoreType.DMA((2 * steps, ys)),
        ],
        limit=limit,
    )
    return f(at, a)


def multiply_body(o, a_ref, b_ref, out_ref):
    for y in range(2):
        put(out_ref, y, jnp.dot(a_ref[o, y], b_ref[...], preferred_element_type=jnp.float32))


def multiply(o, a, b):
    m, (k, n) = a.shape[1] * a.shape[2], b.shape
    f = call(
        lambda *refs: multiply_body(o, *refs),
        [VMEM, VMEM],
        shape((m, n), jnp.float32),
        2 * m * n * k,
        2 * m * k + 4 * m * n,
    )
    return f(a, b)


def decoded(q_ref, rows, scale):
    return q_ref[rows, :].astype(jnp.int32).astype(jnp.float32) * scale


def code_body(s, own_ref, other_ref, out_ref):
    half, n = own_ref.shape[0] // 2, out_ref.shape[1]
    cols = slice(s * n, (s + 1) * n)
    v = own_ref[0:half, cols] + other_ref[0:half, cols]
    out_ref[0:half, :], out_ref[half : half + TAIL, :] = encode(v)


def code(s, n, own, other):
    half = own.shape[0] // 2
    out = shape((half + TAIL, n), jnp.int16)
    f = call(lambda *r: code_body(s, *r), [VMEM] * 2, out, 4 * half * n, 12 * half * n)
    return f(own, other)


def meet_body(s, at_ref, q_ref, own_ref, other_ref, out_ref):
    m, n = own_ref.shape[0], out_ref.shape[1]
    half = m // 2
    cols = slice(s * n, (s + 1) * n)
    near = pl.ds(pl.multiple_of(at_ref[HERE + 1] * half, half), half)
    far = pl.ds(pl.multiple_of((1 - at_ref[HERE + 1]) * half, half), half)
    v = own_ref[near, cols] + other_ref[near, cols] + decode(q_ref, half)
    w = own_ref[far, cols] + other_ref[far, cols]
    top = jnp.maximum(jnp.abs(v), jnp.abs(w))
    e = exponent(jnp.max(top, axis=0, keepdims=True))
    out_ref[near, :] = quantize(v, e)
    out_ref[far, :] = quantize(w, e)
    out_ref[m : m + TAIL, :] = tail(e)


def meet(s, at, q, own, other):
    m, n = own.shape[0], q.shape[1]
    out = shape((m + TAIL, n), jnp.int16)
    f = call(lambda *r: meet_body(s, *r), [SMEM] + [VMEM] * 3, out, 8 * m * n, 12 * m * n)
    return f(at, q, own, other)


def join_body(s, q_ref, own_ref, other_ref, out_ref):
    m, n = own_ref.shape[0], out_ref.shape[1]
    cols = slice(s * n, (s + 1) * n)
    v = own_ref[:, cols] + other_ref[:, cols] + decode(q_ref, m)
    out_ref[0:m, :], out_ref[m : m + TAIL, :] = encode(v)


def join(s, q, own, other):
    m, n = own.shape[0], q.shape[1]
    out = shape((m + TAIL, n), jnp.int16)
    f = call(lambda *r: join_body(s, *r), [VMEM] * 3, out, 8 * m * n, 12 * m * n)
    return f(q, own, other)


def last_body(s, at_ref, q_ref, own_ref, other_ref, *out_refs):
    m, n = own_ref.shape[0], q_ref.shape[1]
    part = m // 4
    scale = scale_of(q_ref, m)
    cols = slice(s * n, (s + 1) * n)
    for k, out in enumerate(out_refs):
        vs = []
        for y in range(2):
            start = pl.multiple_of((2 * y + (at_ref[HERE + 1] ^ k)) * part, part)
            rows = pl.ds(start, part)
            vs.append(own_ref[rows, cols] + other_ref[rows, cols] + decoded(q_ref, rows, scale))
        top = jnp.maximum(jnp.abs(vs[0]), jnp.abs(vs[1]))
        e = exponent(jnp.max(top, axis=0, keepdims=True))
        for y in range(2):
            out[y * part : (y + 1) * part, :] = quantize(vs[y], e)
        out[2 * part : 2 * part + TAIL, :] = tail(e)


def last(s, at, q, own, other):
    m, n = own.shape[0], q.shape[1]
    outs = [shape((m // 2 + TAIL, n), jnp.int16)] * 2
    f = call(lambda *r: last_body(s, *r), [SMEM] + [VMEM] * 3, outs, 8 * m * n, 12 * m * n)
    return f(at, q, own, other)


def share_body(at_ref, own_ref, other_ref, mine_ref, out_ref):
    part = mine_ref.shape[0]
    for k, ref in enumerate((mine_ref, out_ref)):
        start = pl.multiple_of((2 + (at_ref[HERE + 1] ^ k)) * part, part)
        ref[...] = own_ref[pl.ds(start, part), :] + other_ref[pl.ds(start, part), :]


def share(at, own, other):
    m, n = own.shape
    outs = [shape((m // 4, n), jnp.float32)] * 2
    f = call(share_body, [SMEM] + [VMEM] * 2, outs, m * n, 12 * m * n)
    return f(at, own, other)


def fold_body(s, at_ref, a_ref, b_ref, mine_ref, other_ref, keep_ref, out_ref):
    part, n = keep_ref.shape
    cols = slice(s * n, (s + 1) * n)
    ylo, core = at_ref[HERE], at_ref[HERE + 1]
    scales = [scale_of(r, 2 * part) for r in (a_ref, b_ref)]
    for k in range(2):
        y = ylo ^ k
        rows = pl.ds(pl.multiple_of(y * part, part), part)
        from_mine = jnp.full((part, n), y ^ core, jnp.int32) == 0
        v = jnp.where(from_mine, mine_ref[:, cols], other_ref[:, cols])
        for r, scale in zip((a_ref, b_ref), scales):
            v = v + decoded(r, rows, scale)
        if k == 0:
            keep_ref[...] = v
        else:
            out_ref[0:part, :], out_ref[part : part + TAIL, :] = encode(v)


def fold(s, at, a, b, mine, other):
    part, n = mine.shape[0], a.shape[1]
    outs = [shape((part, n), jnp.float32), shape((part + TAIL, n), jnp.int16)]
    f = call(lambda *r: fold_body(s, *r), [SMEM] + [VMEM] * 4, outs, 8 * part * n, 12 * part * n)
    return f(at, a, b, mine, other)


def close_body(rows, keep_ref, *refs):
    *in_refs, out_ref = refs
    m, count, _ = out_ref.shape
    for s in range(count):
        v = -(in_refs[2 * s][...] + decode(in_refs[2 * s + 1], m))
        for i in range(m // rows):
            block = v[i * rows : (i + 1) * rows]
            keep = jnp.full(block.shape, keep_ref[i * count + s], jnp.int32) > 0
            out_ref[i * rows : (i + 1) * rows, s, :] = jnp.where(keep, block, 0.0)


def close(keep, rows, streams):
    m, n = streams[0][0].shape
    count = len(streams)
    f = call(
        lambda *r: close_body(rows, *r),
        [SMEM] + [VMEM] * (2 * count),
        jax.ShapeDtypeStruct((m, count, n), jnp.float32),
        8 * count * m * n,
        14 * count * m * n,
    )
    return f(keep, *[x for stream in streams for x in stream])


def per_device(inverse_tiles, factor_panels, ancestors, valid_flags, block_slot):
    local_rows, width, local_cols, _ = inverse_tiles.shape
    count = factor_panels.shape[0]
    row, col = lax.axis_index("row"), lax.axis_index("col")
    core, z, ylo = row % 2, (row // 2) % NZ, row // (2 * NZ)
    x, yhi = col // 2, col % 2

    across = lax.ppermute(factor_panels, "col", col_perm(0, 1))
    direct = [lax.ppermute(factor_panels, "col", col_perm(d, 0)) for d in (2, 1, 3)]
    onward = [lax.ppermute(across, "col", col_perm(d, 0)) for d in (2, 1, 3)]
    member = membership(ancestors, valid_flags, block_slot)
    col_member = lax.dynamic_slice_in_dim(member, row * local_cols, local_cols, 1)
    row_member = lax.dynamic_slice_in_dim(member, col * local_rows, local_rows, 1)
    col_keep = col_member.reshape(-1).astype(jnp.int32)
    row_keep = jnp.transpose(row_member).reshape(-1).astype(jnp.int32)

    at = []
    for t in range(1, STEPS + 1):
        for c in (1 - core, core):
            if t == 1:
                at += [(z + NZ // 2) % NZ, c, z, c]
            else:
                zd = (z + NZ + (1 - 2 * c) * (5 - t)) % NZ
                at += [zd, 0, zd, 1]
    at += [ylo, core, col, x * 2 + 1 - yhi]
    at += [((x - d) % 4) * 2 + yhi for d in (2, 1, 3)]
    at += [((x - d) % 4) * 2 + 1 - yhi for d in (2, 1, 3)]
    at = jnp.stack([jnp.asarray(v, jnp.int32) for v in at])

    panels = assemble(at, col_keep, [factor_panels, across] + direct + onward)

    tiles = inverse_tiles.reshape(local_rows, 2, NZ, width // 16, local_cols, width)
    ready = list(prepare(0, EARLY, at, tiles, 54 << 20))
    ready += prepare(2 * EARLY, STEPS - EARLY, at, tiles, 50 << 20)

    def terms(t):
        theirs = multiply(0, ready[t - 1], panels)
        other = lax.ppermute(theirs, "row", CORE)
        return multiply(1, ready[t - 1], panels), other

    parts = [terms(t) for t in range(1, STEPS + 1)]
    mine, rest = share(at, *parts[0])
    shared = lax.ppermute(rest, "row", CORE)
    moving = [None] * count
    for t in range(1, STEPS):
        for s in range(count):
            if t == 1:
                coded = code(s, width, *parts[0])
            elif t == 2:
                coded = meet(s, at, moving[s], *parts[1])
            else:
                coded = join(s, moving[s], *parts[t - 1])
            moving[s] = lax.ppermute(coded, "row", ARM)
    streams = []
    for s in range(count):
        straight, crossed = last(s, at, moving[s], *parts[STEPS - 1])
        crossed = lax.ppermute(crossed, "row", ARM_CROSSED)
        straight = lax.ppermute(straight, "row", ARM)
        kept, sent = fold(s, at, straight, crossed, mine, shared)
        streams.append([kept, lax.ppermute(sent, "row", YLO)])
    out = close(row_keep, width // 32, streams)
    return out.reshape(local_rows, width // 32, count, width)


def solution(mesh):
    return jax.shard_map(
        per_device,
        mesh=mesh,
        in_specs=(P("col", None, "row", None), P(None, "row", "col", None), P(), P(), P()),
        out_specs=P("col", "row", None, None),
        check_vma=False,
    )
```

time: 94.2 us -> 75.1 us (0.80)
  the two profiles are of different devices: /device:TPU:1 before, /device:TPU:2 now
where the time goes in v2:
time: 75.1 us; the launch traced here: 74 us
  starting transfers between devices  24.6 us (33%)
  waiting for transfers between devices  23.9 us (32%)
  Pallas kernels  22.1 us (29%)
  other arithmetic  1.83 us (2%)
  local copies, waits for them, and re-layouts  0.92 us (1%)
    ppermute x6, waiting for transfers between devices, per_device(): moving[s] = lax.ppermute(coded, 'row', ARM)  17.4 us
    pallas_call x8, Pallas kernels, multiply(): return f(a, b)  8.67 us
    ppermute x3, starting transfers between devices, per_device(): lax.ppermute(factor_panels, 'col', col_perm(d, 0))  6.46 us
    pallas_call x2, Pallas kernels, prepare(): return f(at, a)  6.03 us
    ppermute x6, starting transfers between devices, per_device(): moving[s] = lax.ppermute(coded, 'row', ARM)  4.69 us
    ppermute x3, starting transfers between devices, per_device(): onward = [lax.ppermute(across, 'col', col_perm(d, 0)) for d in (2, 1, 3)]  3.95 us
    ppermute x2, starting transfers between devices, per_device(): streams.append([kept, lax.ppermute(sent, 'row', YLO)])  3.31 us
    ppermute x2, waiting for transfers between devices, per_device(): streams.append([kept, lax.ppermute(sent, 'row', YLO)])  3.17 us
  transfers between devices with their start and end apart: 24, of which 11 were waited for; matrix products, arithmetic and copies ran while one was open for 4% of the time, Pallas kernels for 25%

profile of v2, /device:TPU:2, one launch (start us, length us, event | category | flops | bytes accessed | tf_op | source)
XLA Modules:
  0.0 74.0 jit_solution(5041545724766674769)
XLA Ops:
  0.0 1.5 %collective-permute-start.2 = (bf16[2,4,32,256]{3,2,1,0:T(8,128)(2,1)}, bf16[2,4,32,256]{3,2,1,0:T(8,128)(2,1)S(1)}, u32[]{:S(2)}, u32[]{:S(2)}) collective-permute-start(bf16[2,4,32,256]{3,2,1,0:T(8,128)(2,1)} %refs_0_.1), channel_id=1, source_target_pairs={{0,2},{1,3},{2,4},{3,5},{4,6},{5,7},{6,0},{7,1},{8,10},{9,11},{10,... | collective-permute-start | bytes 393224 | tf_op jit(solution)/shard_map/ppermute | solution.py:333
  1.5 2.8 %collective-permute-start.1 = (bf16[2,4,32,256]{3,2,1,0:T(8,128)(2,1)}, bf16[2,4,32,256]{3,2,1,0:T(8,128)(2,1)S(1)}, u32[]{:S(2)}, u32[]{:S(2)}) collective-permute-start(bf16[2,4,32,256]{3,2,1,0:T(8,128)(2,1)} %refs_0_.1), channel_id=1, source_target_pairs={{0,4},{1,5},{2,6},{3,7},{4,0},{5,1},{6,2},{7,3},{8,12},{9,13},{10,... | collective-permute-start | bytes 393224 | tf_op jit(solution)/shard_map/ppermute | solution.py:333
  4.3 1.5 %collective-permute-start = (bf16[2,4,32,256]{3,2,1,0:T(8,128)(2,1)}, bf16[2,4,32,256]{3,2,1,0:T(8,128)(2,1)S(1)}, u32[]{:S(2)}, u32[]{:S(2)}) collective-permute-start(bf16[2,4,32,256]{3,2,1,0:T(8,128)(2,1)} %refs_0_.1), channel_id=1, source_target_pairs={{0,1},{1,0},{2,3},{3,2},{4,5},{5,4},{6,7},{7,6},{8,9},{9,8},{10,11... | collective-permute-start | bytes 393224 | tf_op jit(solution)/shard_map/ppermute | solution.py:332
  5.8 2.2 %collective-permute-start.3 = (bf16[2,4,32,256]{3,2,1,0:T(8,128)(2,1)}, bf16[2,4,32,256]{3,2,1,0:T(8,128)(2,1)S(1)}, u32[]{:S(2)}, u32[]{:S(2)}) collective-permute-start(bf16[2,4,32,256]{3,2,1,0:T(8,128)(2,1)} %refs_0_.1), channel_id=1, source_target_pairs={{0,6},{1,7},{2,0},{3,1},{4,2},{5,3},{6,4},{7,5},{8,14},{9,15},{10,... | collective-permute-start | bytes 393224 | tf_op jit(solution)/shard_map/ppermute | solution.py:333
  8.0 0.7 broadcast_compare_fusion
  8.6 0.9 %select_reduce_fusion = s32[2,96]{1,0:T(2,128)S(1)} fusion(s32[128]{0:T(128)} %param.9, s32[2,96]{1,0:T(2,128)} %param.7), kind=kLoop, calls=%fused_computation.1 | loop fusion | flops 73536 | bytes 2048 | tf_op jit(solution)/shard_map/reduce_sum | solution.py:23
  9.5 1.5 %collective-permute-done.refs_1_ = bf16[2,4,32,256]{3,2,1,0:T(8,128)(2,1)S(1)} collective-permute-done((bf16[2,4,32,256]{3,2,1,0:T(8,128)(2,1)}, bf16[2,4,32,256]{3,2,1,0:T(8,128)(2,1)S(1)}, u32[]{:S(2)}, u32[]{:S(2)}) %collective-permute-start) | collective-permute-done | bytes 131104 | tf_op jit(solution)/shard_map/ppermute | solution.py:332
  11.0 0.4 collective-permute-start.6
  11.4 1.6 %collective-permute-start.5 = (bf16[2,4,32,256]{3,2,1,0:T(8,128)(2,1)S(1)}, bf16[2,4,32,256]{3,2,1,0:T(8,128)(2,1)S(1)}, u32[]{:S(2)}, u32[]{:S(2)}) collective-permute-start(bf16[2,4,32,256]{3,2,1,0:T(8,128)(2,1)S(1)} %collective-permute-done.refs_1_), channel_id=1, source_target_pairs={{0,2},{1,3},{2,4},{3,5},{4,6},{5,7},{6,0},{7,1},{8,10},{9,11},{10,... | collective-permute-start | bytes 393224 | tf_op jit(solution)/shard_map/ppermute | solution.py:334
  13.0 1.9 %collective-permute-start.4 = (bf16[2,4,32,256]{3,2,1,0:T(8,128)(2,1)S(1)}, bf16[2,4,32,256]{3,2,1,0:T(8,128)(2,1)S(1)}, u32[]{:S(2)}, u32[]{:S(2)}) collective-permute-start(bf16[2,4,32,256]{3,2,1,0:T(8,128)(2,1)S(1)} %collective-permute-done.refs_1_), channel_id=1, source_target_pairs={{0,4},{1,5},{2,6},{3,7},{4,0},{5,1},{6,2},{7,3},{8,12},{9,13},{10,... | collective-permute-start | bytes 393224 | tf_op jit(solution)/shard_map/ppermute | solution.py:334
  15.5 0.7 stack.90.refs_0_.at_ref.r_0_
  16.1 3.8 %shard_map.55 = (bf16[2,2,256,1024]{3,2,1,0:T(8,128)(2,1)S(1)}, bf16[2,2,256,1024]{3,2,1,0:T(8,128)(2,1)S(1)}, bf16[2,2,256,1024]{3,2,1,0:T(8,128)(2,1)S(1)}) custom-call(s32[42]{0:T(128)} %stack.90.refs_0_.at_ref.r_0_, bf16[16,2,8,16,4,256]{5,4,3,2,1,0:T(4,128)(2,1)} %bitcast.32), custom_call_target="tpu_custom_call" | custom-call | bytes 12582912 | tf_op jit(solution)/shard_map/pallas_call | solution.py:163
  20.0 0.7 shard_map.56
  20.7 1.7 %shard_map.58 = f32[512,512]{1,0:T(8,128)} custom-call(bf16[2,2,256,1024]{3,2,1,0:T(8,128)(2,1)S(1)} %get-tuple-element.18.refs_0_, bf16[1024,512]{1,0:T(8,128)(2,1)S(1)} %bitcast.24), custom_call_target="tpu_custom_call" | custom-call | flops 536870912 | bytes 2097152 | tf_op jit(solution)/shard_map/pallas_call | solution.py:180
  22.5 1.7 %shard_map.61 = f32[512,512]{1,0:T(8,128)} custom-call(bf16[2,2,256,1024]{3,2,1,0:T(8,128)(2,1)S(1)} %get-tuple-element.19.refs_0_, bf16[1024,512]{1,0:T(8,128)(2,1)S(1)} %bitcast.25), custom_call_target="tpu_custom_call" | custom-call | flops 536870912 | bytes 2097152 | tf_op jit(solution)/shard_map/pallas_call | solution.py:180
  24.1 0.5 collective-permute-start.9
  24.7 1.7 %shard_map.64 = f32[512,512]{1,0:T(8,128)} custom-call(bf16[2,2,256,1024]{3,2,1,0:T(8,128)(2,1)S(1)} %get-tuple-element.20.refs_0_, bf16[1024,512]{1,0:T(8,128)(2,1)S(1)} %bitcast.26), custom_call_target="tpu_custom_call" | custom-call | flops 536870912 | bytes 2097152 | tf_op jit(solution)/shard_map/pallas_call | solution.py:180
  26.4 2.2 %shard_map.66.refs_0_ = bf16[2,2,256,1024]{3,2,1,0:T(8,128)(2,1)S(1)} custom-call(s32[42]{0:T(128)S(1)} %copy-done.1, bf16[16,2,8,16,4,256]{5,4,3,2,1,0:T(4,128)(2,1)} %bitcast.33), custom_call_target="tpu_custom_call" | custom-call | bytes 4194304 | tf_op jit(solution)/shard_map/pallas_call | solution.py:163
  28.6 0.7 shard_map.68
  29.3 0.6 collective-permute-start.13
  29.9 0.7 shard_map.57.r_0_.own_ref
  30.7 2.2 %collective-permute-start.18 = (s16[272,256]{1,0:T(8,128)(2,1)S(1)}, s16[272,256]{1,0:T(8,128)(2,1)S(1)}, u32[]{:S(2)}, u32[]{:S(2)}) collective-permute-start(s16[272,256]{1,0:T(8,128)(2,1)S(1)} %shard_map.72), channel_id=1, source_target_pairs={{0,16},{8,120},{16,32},{24,8},{32,48},{40,24},{48,64},{56,40},{64,... | collective-permute-start | bytes 417800 | tf_op jit(solution)/shard_map/ppermute | solution.py:377
  33.0 2.0 %collective-permute-start.8 = (s16[272,256]{1,0:T(8,128)(2,1)S(1)}, s16[272,256]{1,0:T(8,128)(2,1)S(1)}, u32[]{:S(2)}, u32[]{:S(2)}) collective-permute-start(s16[272,256]{1,0:T(8,128)(2,1)S(1)} %shard_map.59), channel_id=1, source_target_pairs={{0,16},{8,120},{16,32},{24,8},{32,48},{40,24},{48,64},{56,40},{64,... | collective-permute-start | bytes 417800 | tf_op jit(solution)/shard_map/ppermute | solution.py:377
  35.0 0.7 shard_map.60.r_2_
  35.7 4.2 %collective-permute-done.18.r_1_ = s16[272,256]{1,0:T(8,128)(2,1)S(1)} collective-permute-done((s16[272,256]{1,0:T(8,128)(2,1)S(1)}, s16[272,256]{1,0:T(8,128)(2,1)S(1)}, u32[]{:S(2)}, u32[]{:S(2)}) %collective-permute-start.18) | collective-permute-done | bytes 139296 | tf_op jit(solution)/shard_map/ppermute | solution.py:377
  39.9 0.7 shard_map.73
  40.7 0.7 collective-permute-done.8.r_1_
  41.4 0.7 shard_map.62
  42.4 0.7 shard_map.63.r_1_
  43.1 5.2 %collective-permute-done.19.r_0_ = s16[528,256]{1,0:T(8,128)(2,1)S(1)} collective-permute-done((s16[528,256]{1,0:T(8,128)(2,1)S(1)}, s16[528,256]{1,0:T(8,128)(2,1)S(1)}, u32[]{:S(2)}, u32[]{:S(2)}) %collective-permute-start.19) | collective-permute-done | bytes 270368 | tf_op jit(solution)/shard_map/ppermute | solution.py:377
  48.6 2.6 %collective-permute-done.10.r_0_ = s16[528,256]{1,0:T(8,128)(2,1)S(1)} collective-permute-done((s16[528,256]{1,0:T(8,128)(2,1)S(1)}, s16[528,256]{1,0:T(8,128)(2,1)S(1)}, u32[]{:S(2)}, u32[]{:S(2)}) %collective-permute-start.10) | collective-permute-done | bytes 270368 | tf_op jit(solution)/shard_map/ppermute | solution.py:377
  51.5 0.6 shard_map.70
  52.1 0.7 collective-permute-start.16
  52.9 0.7 shard_map.67.r_2_
  53.6 2.7 %collective-permute-done.20.r_1_ = s16[528,256]{1,0:T(8,128)(2,1)S(1)} collective-permute-done((s16[528,256]{1,0:T(8,128)(2,1)S(1)}, s16[528,256]{1,0:T(8,128)(2,1)S(1)}, u32[]{:S(2)}, u32[]{:S(2)}) %collective-permute-start.20) | collective-permute-done | bytes 270368 | tf_op jit(solution)/shard_map/ppermute | solution.py:377
  56.3 0.7 shard_map.75
  57.2 2.0 %collective-permute-done.12.r_1_ = s16[528,256]{1,0:T(8,128)(2,1)S(1)} collective-permute-done((s16[528,256]{1,0:T(8,128)(2,1)S(1)}, s16[528,256]{1,0:T(8,128)(2,1)S(1)}, u32[]{:S(2)}, u32[]{:S(2)}) %collective-permute-start.12) | collective-permute-done | bytes 270368 | tf_op jit(solution)/shard_map/ppermute | solution.py:377
  59.2 0.7 shard_map.69
  60.0 2.6 %collective-permute-start.15 = (s16[272,256]{1,0:T(8,128)(2,1)S(1)}, s16[272,256]{1,0:T(8,128)(2,1)S(1)}, u32[]{:S(2)}, u32[]{:S(2)}) collective-permute-start(s16[272,256]{1,0:T(8,128)(2,1)S(1)} %get-tuple-element.22), channel_id=1, source_target_pairs={{0,24},{8,112},{16,40},{24,0},{32,56},{40,16},{48,72},{56,32},{64,... | collective-permute-start | bytes 417800 | tf_op jit(solution)/shard_map/ppermute | solution.py:381
  62.6 0.8 %collective-permute-done.21.r_1_ = s16[272,256]{1,0:T(8,128)(2,1)S(1)} collective-permute-done((s16[272,256]{1,0:T(8,128)(2,1)S(1)}, s16[272,256]{1,0:T(8,128)(2,1)S(1)}, u32[]{:S(2)}, u32[]{:S(2)}) %collective-permute-start.21) | collective-permute-done | bytes 139296 | tf_op jit(solution)/shard_map/ppermute | solution.py:382
  63.3 0.7 shard_map.76
  64.0 1.7 %collective-permute-start.23 = (s16[144,256]{1,0:T(8,128)(2,1)S(1)}, s16[144,256]{1,0:T(8,128)(2,1)S(1)}, u32[]{:S(2)}, u32[]{:S(2)}) collective-permute-start(s16[144,256]{1,0:T(8,128)(2,1)S(1)} %get-tuple-element.30), channel_id=1, source_target_pairs={{0,128},{8,136},{16,144},{24,152},{32,160},{40,168},{48,176},{56,1... | collective-permute-start | bytes 221192 | tf_op jit(solution)/shard_map/ppermute | solution.py:384
  65.7 0.6 collective-permute-done.14.r_1_
  66.3 0.5 collective-permute-done.15.r_2_
  66.8 0.7 shard_map.71
  67.5 1.7 %collective-permute-start.17 = (s16[144,256]{1,0:T(8,128)(2,1)S(1)}, s16[144,256]{1,0:T(8,128)(2,1)S(1)}, u32[]{:S(2)}, u32[]{:S(2)}) collective-permute-start(s16[144,256]{1,0:T(8,128)(2,1)S(1)} %get-tuple-element.26), channel_id=1, source_target_pairs={{0,128},{8,136},{16,144},{24,152},{32,160},{40,168},{48,176},{56,1... | collective-permute-start | bytes 221192 | tf_op jit(solution)/shard_map/ppermute | solution.py:384
  69.4 3.2 %collective-permute-done.17.r_2_ = s16[144,256]{1,0:T(8,128)(2,1)S(1)} collective-permute-done((s16[144,256]{1,0:T(8,128)(2,1)S(1)}, s16[144,256]{1,0:T(8,128)(2,1)S(1)}, u32[]{:S(2)}, u32[]{:S(2)}) %collective-permute-start.17) | collective-permute-done | bytes 73760 | tf_op jit(solution)/shard_map/ppermute | solution.py:384
  72.6 1.4 %shard_map.77 = f32[128,2,256]{2,1,0:T(2,128)} custom-call(s32[32]{0:T(128)S(1)} %reshape.23.r_0_, f32[128,256]{1,0:T(8,128)S(1)} %get-tuple-element.25.r_1_, s16[144,256]{1,0:T(8,128)(2,1)S(1)} %collective-permute-done.17.r_2_, f32[128,256]{1,0:T(8,128)S(1)} %get-tuple-element.29.r_3_, s16[144,256]{1,0:T(8,128)(2,1)S(1)} %collective-permute-done.23.r_4_), custom_call_target="tpu_custom_call" | custom-call | flops 524288 | bytes 917504 | tf_op jit(solution)/shard_map/pallas_call | solution.py:322
  (36 shorter events, 1.9 us)
Async XLA Ops:
  0.0 13.0 %collective-permute-start.2 = (bf16[2,4,32,256]{3,2,1,0:T(8,128)(2,1)}, bf16[2,4,32,256]{3,2,1,0:T(8,128)(2,1)S(1)}, u32[]{:S(2)}, u32[]{:S(2)}) collective-permute-start(bf16[2,4,32,256]{3,2,1,0:T(8,128)(2,1)} %refs_0_.1), channel_id=1, source_target_pairs={{0,2},{1,3},{2,4},{3,5},{4,6},{5,7},{6,0},{7,1},{8,10},{9,11},{10,... | collective-permute-start | bytes 393224 | tf_op jit(solution)/shard_map/ppermute | solution.py:333
  1.5 18.5 %collective-permute-start.1 = (bf16[2,4,32,256]{3,2,1,0:T(8,128)(2,1)}, bf16[2,4,32,256]{3,2,1,0:T(8,128)(2,1)S(1)}, u32[]{:S(2)}, u32[]{:S(2)}) collective-permute-start(bf16[2,4,32,256]{3,2,1,0:T(8,128)(2,1)} %refs_0_.1), channel_id=1, source_target_pairs={{0,4},{1,5},{2,6},{3,7},{4,0},{5,1},{6,2},{7,3},{8,12},{9,13},{10,... | collective-permute-start | bytes 393224 | tf_op jit(solution)/shard_map/ppermute | solution.py:333
  4.3 6.7 %collective-permute-start = (bf16[2,4,32,256]{3,2,1,0:T(8,128)(2,1)}, bf16[2,4,32,256]{3,2,1,0:T(8,128)(2,1)S(1)}, u32[]{:S(2)}, u32[]{:S(2)}) collective-permute-start(bf16[2,4,32,256]{3,2,1,0:T(8,128)(2,1)} %refs_0_.1), channel_id=1, source_target_pairs={{0,1},{1,0},{2,3},{3,2},{4,5},{5,4},{6,7},{7,6},{8,9},{9,8},{10,11... | collective-permute-start | bytes 393224 | tf_op jit(solution)/shard_map/ppermute | solution.py:332
  5.8 14.2 %collective-permute-start.3 = (bf16[2,4,32,256]{3,2,1,0:T(8,128)(2,1)}, bf16[2,4,32,256]{3,2,1,0:T(8,128)(2,1)S(1)}, u32[]{:S(2)}, u32[]{:S(2)}) collective-permute-start(bf16[2,4,32,256]{3,2,1,0:T(8,128)(2,1)} %refs_0_.1), channel_id=1, source_target_pairs={{0,6},{1,7},{2,0},{3,1},{4,2},{5,3},{6,4},{7,5},{8,14},{9,15},{10,... | collective-permute-start | bytes 393224 | tf_op jit(solution)/shard_map/ppermute | solution.py:333
  11.0 9.0 %collective-permute-start.6 = (bf16[2,4,32,256]{3,2,1,0:T(8,128)(2,1)S(1)}, bf16[2,4,32,256]{3,2,1,0:T(8,128)(2,1)S(1)}, u32[]{:S(2)}, u32[]{:S(2)}) collective-permute-start(bf16[2,4,32,256]{3,2,1,0:T(8,128)(2,1)S(1)} %collective-permute-done.refs_1_), channel_id=1, source_target_pairs={{0,6},{1,7},{2,0},{3,1},{4,2},{5,3},{6,4},{7,5},{8,14},{9,15},{10,... | collective-permute-start | bytes 393224 | tf_op jit(solution)/shard_map/ppermute | solution.py:334
  11.4 8.5 %collective-permute-start.5 = (bf16[2,4,32,256]{3,2,1,0:T(8,128)(2,1)S(1)}, bf16[2,4,32,256]{3,2,1,0:T(8,128)(2,1)S(1)}, u32[]{:S(2)}, u32[]{:S(2)}) collective-permute-start(bf16[2,4,32,256]{3,2,1,0:T(8,128)(2,1)S(1)} %collective-permute-done.refs_1_), channel_id=1, source_target_pairs={{0,2},{1,3},{2,4},{3,5},{4,6},{5,7},{6,0},{7,1},{8,10},{9,11},{10,... | collective-permute-start | bytes 393224 | tf_op jit(solution)/shard_map/ppermute | solution.py:334
  13.0 7.0 %collective-permute-start.4 = (bf16[2,4,32,256]{3,2,1,0:T(8,128)(2,1)S(1)}, bf16[2,4,32,256]{3,2,1,0:T(8,128)(2,1)S(1)}, u32[]{:S(2)}, u32[]{:S(2)}) collective-permute-start(bf16[2,4,32,256]{3,2,1,0:T(8,128)(2,1)S(1)} %collective-permute-done.refs_1_), channel_id=1, source_target_pairs={{0,4},{1,5},{2,6},{3,7},{4,0},{5,1},{6,2},{7,3},{8,12},{9,13},{10,... | collective-permute-start | bytes 393224 | tf_op jit(solution)/shard_map/ppermute | solution.py:334
  16.1 3.9 %copy-start = (bf16[2,4,32,256]{3,2,1,0:T(8,128)(2,1)S(1)}, bf16[2,4,32,256]{3,2,1,0:T(8,128)(2,1)}, u32[]{:S(2)}) copy-start(bf16[2,4,32,256]{3,2,1,0:T(8,128)(2,1)} %refs_0_.1) | copy-start | bytes 393220
  16.1 3.9 %copy-start.1 = (s32[42]{0:T(128)S(1)}, s32[42]{0:T(128)}, u32[]{:S(2)}) copy-start(s32[42]{0:T(128)} %stack.90.refs_0_.at_ref.r_0_) | copy-start | bytes 508
  22.5 8.2 %collective-permute-start.7 = (f32[512,512]{1,0:T(8,128)}, f32[512,512]{1,0:T(8,128)S(1)}, u32[]{:S(2)}, u32[]{:S(2)}) collective-permute-start(f32[512,512]{1,0:T(8,128)} %shard_map.58), channel_id=1, source_target_pairs={{0,8},{8,0},{16,24},{24,16},{32,40},{40,32},{48,56},{56,48},{64,72... | collective-permute-start | bytes 3145736 | tf_op jit(solution)/shard_map/ppermute | solution.py:362
  24.1 11.5 %collective-permute-start.9 = (f32[512,512]{1,0:T(8,128)}, f32[512,512]{1,0:T(8,128)S(1)}, u32[]{:S(2)}, u32[]{:S(2)}) collective-permute-start(f32[512,512]{1,0:T(8,128)} %shard_map.61), channel_id=1, source_target_pairs={{0,8},{8,0},{16,24},{24,16},{32,40},{40,32},{48,56},{56,48},{64,72... | collective-permute-start | bytes 3145736 | tf_op jit(solution)/shard_map/ppermute | solution.py:362
  26.4 16.7 %collective-permute-start.11 = (f32[512,512]{1,0:T(8,128)}, f32[512,512]{1,0:T(8,128)S(1)}, u32[]{:S(2)}, u32[]{:S(2)}) collective-permute-start(f32[512,512]{1,0:T(8,128)} %shard_map.64), channel_id=1, source_target_pairs={{0,8},{8,0},{16,24},{24,16},{32,40},{40,32},{48,56},{56,48},{64,72... | collective-permute-start | bytes 3145736 | tf_op jit(solution)/shard_map/ppermute | solution.py:362
  29.3 24.3 %collective-permute-start.13 = (f32[512,512]{1,0:T(8,128)S(1)}, f32[512,512]{1,0:T(8,128)S(1)}, u32[]{:S(2)}, u32[]{:S(2)}) collective-permute-start(f32[512,512]{1,0:T(8,128)S(1)} %shard_map.68), channel_id=1, source_target_pairs={{0,8},{8,0},{16,24},{24,16},{32,40},{40,32},{48,56},{56,48},{64,72... | collective-permute-start | bytes 3145736 | tf_op jit(solution)/shard_map/ppermute | solution.py:362
  30.7 9.2 %collective-permute-start.18 = (s16[272,256]{1,0:T(8,128)(2,1)S(1)}, s16[272,256]{1,0:T(8,128)(2,1)S(1)}, u32[]{:S(2)}, u32[]{:S(2)}) collective-permute-start(s16[272,256]{1,0:T(8,128)(2,1)S(1)} %shard_map.72), channel_id=1, source_target_pairs={{0,16},{8,120},{16,32},{24,8},{32,48},{40,24},{48,64},{56,40},{64,... | collective-permute-start | bytes 417800 | tf_op jit(solution)/shard_map/ppermute | solution.py:377
  33.0 8.4 %collective-permute-start.8 = (s16[272,256]{1,0:T(8,128)(2,1)S(1)}, s16[272,256]{1,0:T(8,128)(2,1)S(1)}, u32[]{:S(2)}, u32[]{:S(2)}) collective-permute-start(s16[272,256]{1,0:T(8,128)(2,1)S(1)} %shard_map.59), channel_id=1, source_target_pairs={{0,16},{8,120},{16,32},{24,8},{32,48},{40,24},{48,64},{56,40},{64,... | collective-permute-start | bytes 417800 | tf_op jit(solution)/shard_map/ppermute | solution.py:377
  40.6 7.7 %collective-permute-start.19 = (s16[528,256]{1,0:T(8,128)(2,1)S(1)}, s16[528,256]{1,0:T(8,128)(2,1)S(1)}, u32[]{:S(2)}, u32[]{:S(2)}) collective-permute-start(s16[528,256]{1,0:T(8,128)(2,1)S(1)} %shard_map.73), channel_id=1, source_target_pairs={{0,16},{8,120},{16,32},{24,8},{32,48},{40,24},{48,64},{56,40},{64,... | collective-permute-start | bytes 811016 | tf_op jit(solution)/shard_map/ppermute | solution.py:377
  42.1 9.1 %collective-permute-start.10 = (s16[528,256]{1,0:T(8,128)(2,1)S(1)}, s16[528,256]{1,0:T(8,128)(2,1)S(1)}, u32[]{:S(2)}, u32[]{:S(2)}) collective-permute-start(s16[528,256]{1,0:T(8,128)(2,1)S(1)} %shard_map.62), channel_id=1, source_target_pairs={{0,16},{8,120},{16,32},{24,8},{32,48},{40,24},{48,64},{56,40},{64,... | collective-permute-start | bytes 811016 | tf_op jit(solution)/shard_map/ppermute | solution.py:377
  48.5 7.7 %collective-permute-start.20 = (s16[528,256]{1,0:T(8,128)(2,1)S(1)}, s16[528,256]{1,0:T(8,128)(2,1)S(1)}, u32[]{:S(2)}, u32[]{:S(2)}) collective-permute-start(s16[528,256]{1,0:T(8,128)(2,1)S(1)} %shard_map.74), channel_id=1, source_target_pairs={{0,16},{8,120},{16,32},{24,8},{32,48},{40,24},{48,64},{56,40},{64,... | collective-permute-start | bytes 811016 | tf_op jit(solution)/shard_map/ppermute | solution.py:377
  51.4 7.8 %collective-permute-start.12 = (s16[528,256]{1,0:T(8,128)(2,1)S(1)}, s16[528,256]{1,0:T(8,128)(2,1)S(1)}, u32[]{:S(2)}, u32[]{:S(2)}) collective-permute-start(s16[528,256]{1,0:T(8,128)(2,1)S(1)} %shard_map.65), channel_id=1, source_target_pairs={{0,16},{8,120},{16,32},{24,8},{32,48},{40,24},{48,64},{56,40},{64,... | collective-permute-start | bytes 811016 | tf_op jit(solution)/shard_map/ppermute | solution.py:377
  52.1 10.5 %collective-permute-start.16 = (f32[128,512]{1,0:T(8,128)S(1)}, f32[128,512]{1,0:T(8,128)S(1)}, u32[]{:S(2)}, u32[]{:S(2)}) collective-permute-start(f32[128,512]{1,0:T(8,128)S(1)} %get-tuple-element.24), channel_id=1, source_target_pairs={{0,8},{8,0},{16,24},{24,16},{32,40},{40,32},{48,56},{56,48},{64,72... | collective-permute-start | bytes 786440 | tf_op jit(solution)/shard_map/ppermute | solution.py:367
  57.0 6.3 %collective-permute-start.21 = (s16[272,256]{1,0:T(8,128)(2,1)S(1)}, s16[272,256]{1,0:T(8,128)(2,1)S(1)}, u32[]{:S(2)}, u32[]{:S(2)}) collective-permute-start(s16[272,256]{1,0:T(8,128)(2,1)S(1)} %get-tuple-element.27), channel_id=1, source_target_pairs={{0,16},{8,120},{16,32},{24,8},{32,48},{40,24},{48,64},{56,40},{64,... | collective-permute-start | bytes 417800 | tf_op jit(solution)/shard_map/ppermute | solution.py:382
  57.1 6.3 %collective-permute-start.22 = (s16[272,256]{1,0:T(8,128)(2,1)S(1)}, s16[272,256]{1,0:T(8,128)(2,1)S(1)}, u32[]{:S(2)}, u32[]{:S(2)}) collective-permute-start(s16[272,256]{1,0:T(8,128)(2,1)S(1)} %get-tuple-element.28), channel_id=1, source_target_pairs={{0,24},{8,112},{16,40},{24,0},{32,56},{40,16},{48,72},{56,32},{64,... | collective-permute-start | bytes 417800 | tf_op jit(solution)/shard_map/ppermute | solution.py:381
  59.9 6.4 %collective-permute-start.14 = (s16[272,256]{1,0:T(8,128)(2,1)S(1)}, s16[272,256]{1,0:T(8,128)(2,1)S(1)}, u32[]{:S(2)}, u32[]{:S(2)}) collective-permute-start(s16[272,256]{1,0:T(8,128)(2,1)S(1)} %get-tuple-element.21), channel_id=1, source_target_pairs={{0,16},{8,120},{16,32},{24,8},{32,48},{40,24},{48,64},{56,40},{64,... | collective-permute-start | bytes 417800 | tf_op jit(solution)/shard_map/ppermute | solution.py:382
  60.0 6.8 %collective-permute-start.15 = (s16[272,256]{1,0:T(8,128)(2,1)S(1)}, s16[272,256]{1,0:T(8,128)(2,1)S(1)}, u32[]{:S(2)}, u32[]{:S(2)}) collective-permute-start(s16[272,256]{1,0:T(8,128)(2,1)S(1)} %get-tuple-element.22), channel_id=1, source_target_pairs={{0,24},{8,112},{16,40},{24,0},{32,56},{40,16},{48,72},{56,32},{64,... | collective-permute-start | bytes 417800 | tf_op jit(solution)/shard_map/ppermute | solution.py:381
  64.0 5.4 %collective-permute-start.23 = (s16[144,256]{1,0:T(8,128)(2,1)S(1)}, s16[144,256]{1,0:T(8,128)(2,1)S(1)}, u32[]{:S(2)}, u32[]{:S(2)}) collective-permute-start(s16[144,256]{1,0:T(8,128)(2,1)S(1)} %get-tuple-element.30), channel_id=1, source_target_pairs={{0,128},{8,136},{16,144},{24,152},{32,160},{40,168},{48,176},{56,1... | collective-permute-start | bytes 221192 | tf_op jit(solution)/shard_map/ppermute | solution.py:384
  67.5 5.1 %collective-permute-start.17 = (s16[144,256]{1,0:T(8,128)(2,1)S(1)}, s16[144,256]{1,0:T(8,128)(2,1)S(1)}, u32[]{:S(2)}, u32[]{:S(2)}) collective-permute-start(s16[144,256]{1,0:T(8,128)(2,1)S(1)} %get-tuple-element.26), channel_id=1, source_target_pairs={{0,128},{8,136},{16,144},{24,152},{32,160},{40,168},{48,176},{56,1... | collective-permute-start | bytes 221192 | tf_op jit(solution)/shard_map/ppermute | solution.py:384

commit v3 on v2

v3 whole, which is shorter than its diff:
```python
import math

import jax
import jax.numpy as jnp
from jax import lax
from jax.experimental import pallas as pl
from jax.experimental.pallas import tpu as pltpu
from jax.sharding import PartitionSpec as P


NZ = 8
STEPS = 4
TOP = 32000.0
TAIL = 16


def row_perm(move, cores=(0, 1)):
    pairs = []
    for r in range(32):
        ylo, z, core = r // 16, (r // 2) % NZ, r % 2
        if core in cores:
            y2, z2, c2 = move(ylo, z, core)
            pairs.append((r, ((y2 % 2) * NZ + z2 % NZ) * 2 + c2 % 2))
    return pairs


def place():
    row = lax.axis_index("row")
    return row // (2 * NZ), (row // 2) % NZ, row % 2


def col_perm(dx, dy):
    return [(c, ((c // 2 + dx) % 4) * 2 + (c % 2 + dy) % 2) for c in range(8)]


MOVES = ((0, 0), (0, 1), (2, 0), (1, 0), (3, 0), (2, 1), (1, 1), (3, 1))
CORE = row_perm(lambda y, z, c: (y, z, 1 - c))
YLO = row_perm(lambda y, z, c: (1 - y, z, c))
ARM = row_perm(lambda y, z, c: (y, z + 1 - 2 * c, c))
ARM_CROSSED = row_perm(lambda y, z, c: (y, z + 1 - 2 * c, 1 - c))


def exponent(top):
    return jnp.ceil(jnp.log2(jnp.maximum(top, 1e-30) * (1.0 / TOP)))


def quantize(v, e):
    return jnp.round(v * jnp.exp2(-e)).astype(jnp.int32).astype(jnp.int16)


def tail(e):
    return jnp.broadcast_to(e, (TAIL, e.shape[1])).astype(jnp.int32).astype(jnp.int16)


def encode(v):
    e = exponent(jnp.max(jnp.abs(v), axis=0, keepdims=True))
    return quantize(v, e), tail(e)


def scale_of(ref, rows):
    e = ref[rows : rows + TAIL, :].astype(jnp.int32).astype(jnp.float32)
    return jnp.exp2(e[0:1, :])


def decode(ref, rows):
    return ref[0:rows, :].astype(jnp.int32).astype(jnp.float32) * scale_of(ref, rows)


def decoded(q_ref, rows, scale):
    return q_ref[rows, :].astype(jnp.int32).astype(jnp.float32) * scale


VMEM = pl.BlockSpec(memory_space=pltpu.VMEM)
HBM = pl.BlockSpec(memory_space=pltpu.HBM)


def call(body, in_specs, out_shape, flops, nbytes, scratch=(), limit=8 << 20):
    many = isinstance(out_shape, list)
    return pl.pallas_call(
        body,
        in_specs=in_specs,
        out_specs=[VMEM] * len(out_shape) if many else VMEM,
        out_shape=out_shape,
        scratch_shapes=list(scratch),
        compiler_params=pltpu.CompilerParams(vmem_limit_bytes=limit),
        cost_estimate=pl.CostEstimate(flops=flops, bytes_accessed=nbytes, transcendentals=0),
    )


def shape(dims, dtype):
    return pltpu.VMEM(dims, dtype)


def members_body(ancestors_ref, flags_ref, slot_ref, out_ref):
    n = slot_ref.shape[1]
    count, entries = ancestors_ref.shape
    block = lax.broadcasted_iota(jnp.int32, (n, n), 0)
    slots = (jnp.broadcast_to(slot_ref[...], (n, n)) == block).astype(jnp.float32)
    for s in range(count):
        ids = jnp.broadcast_to(ancestors_ref[s : s + 1, :], (n, entries))
        used = jnp.broadcast_to(flags_ref[s : s + 1, :], (n, entries)) == 1
        named = (ids == block[:, 0:entries]) & used
        hits = jnp.dot(
            slots.astype(jnp.bfloat16),
            named.astype(jnp.float32).astype(jnp.bfloat16),
            preferred_element_type=jnp.float32,
        )
        member = jnp.max(hits, axis=1, keepdims=True)
        out_ref[s] = jnp.broadcast_to(member, out_ref.shape[1:])


def members(ancestors, flags, slot, width):
    count, n = ancestors.shape[0], slot.shape[0]
    out = shape((count, n, width), jnp.float32)
    f = call(members_body, [VMEM] * 3, out, 4 * n * n * n, 4 * n * n)
    return f(ancestors, flags, slot.reshape(1, n))


def gather_body(keep_ref, *refs):
    *pieces, out_ref = refs
    count, cols, rows, width = pieces[0].shape
    col = lax.axis_index("col")
    x, yhi = col // 2, col % 2
    for p, piece in enumerate(pieces):
        dx, dy = MOVES[p]
        at = ((x + 4 - dx) % 4) * 2 + (yhi + dy) % 2
        for s in range(count):
            for b in range(cols):
                block = lax.axis_index("row") * cols + b
                keep = jnp.broadcast_to(keep_ref[s, pl.ds(block, 1), :], (rows, width)) > 0
                value = piece[s, b].astype(jnp.float32)
                value = jnp.where(keep, value, 0.0).astype(piece.dtype)
                out_ref[b, at, :, s * width : (s + 1) * width] = value


def assemble(keep, pieces):
    count, cols, rows, width = pieces[0].shape
    out = shape((cols, len(pieces), rows, count * width), pieces[0].dtype)
    f = call(gather_body, [VMEM] * (1 + len(pieces)), out, 0, 4 * math.prod(out.shape))
    return f(keep, *pieces).reshape(-1, count * width)


def source(o):
    _, z, core = place()
    if o == 0:
        far = (z + NZ // 2) % NZ
        return (far, 1 - core), (far, core)
    c = core if o % 2 else 1 - core
    zd = z if o == 1 else (z + NZ + (1 - 2 * c) * (STEPS - o // 2)) % NZ
    return (zd, 0), (zd, 1)


def fetch(o, a_ref, buf, sem):
    return [
        pltpu.make_async_copy(a_ref.at[:, y, z], buf.at[h], sem.at[h])
        for h, (z, y) in enumerate(source(o))
    ]


def flat(x):
    return x.reshape(-1, x.shape[2] * x.shape[3])


def put(out_ref, y, r):
    half = r.shape[0] // 2
    r = r.reshape(-1, 2, 8, r.shape[1])
    for c in range(2):
        start = (2 * y + c) * half
        out_ref[start : start + half, :] = r[:, c].reshape(half, r.shape[3])


def prepare_body(a_ref, *refs):
    *out_refs, buf, sem = refs
    for o in range(len(out_refs)):
        for copy in fetch(o, a_ref, buf.at[o], sem.at[o]):
            copy.start()
    for o, out_ref in enumerate(out_refs):
        for h, copy in enumerate(fetch(o, a_ref, buf.at[o], sem.at[o])):
            copy.wait()
            out_ref[h] = flat(buf[o, h])


def prepare(a):
    count, ys, _, rows, cols, width = a.shape
    outs = 2 * STEPS
    f = call(
        prepare_body,
        [HBM],
        [shape((ys, count * rows, cols * width), a.dtype)] * outs,
        0,
        4 * a.size,
        [pltpu.VMEM((outs, ys, count, rows, cols, width), a.dtype), pltpu.SemaphoreType.DMA((outs, ys))],
        limit=48 << 20,
    )
    return f(a)


def multiply_body(halves, a_ref, b_ref, out_ref):
    for i, h in enumerate(halves):
        put(out_ref, i, jnp.dot(a_ref[h], b_ref[...], preferred_element_type=jnp.float32))


def multiply(halves, a, b):
    m, (k, n) = a.shape[1] * len(halves), b.shape
    f = call(
        lambda *refs: multiply_body(halves, *refs),
        [VMEM, VMEM],
        shape((m, n), jnp.float32),
        2 * m * n * k,
        2 * m * k + 4 * m * n,
    )
    return f(a, b)


def code_body(s, own_ref, other_ref, out_ref):
    half, n = own_ref.shape[0], out_ref.shape[1]
    cols = slice(s * n, (s + 1) * n)
    v = own_ref[:, cols] + other_ref[:, cols]
    out_ref[0:half, :], out_ref[half : half + TAIL, :] = encode(v)


def code(s, n, own, other):
    half = own.shape[0]
    out = shape((half + TAIL, n), jnp.int16)
    f = call(lambda *r: code_body(s, *r), [VMEM] * 2, out, 4 * half * n, 12 * half * n)
    return f(own, other)


def meet_body(s, q_ref, own_ref, other_ref, out_ref):
    m, n = own_ref.shape[0], out_ref.shape[1]
    half = m // 2
    core = place()[2]
    cols = slice(s * n, (s + 1) * n)
    near = pl.ds(pl.multiple_of(core * half, half), half)
    far = pl.ds(pl.multiple_of((1 - core) * half, half), half)
    v = own_ref[near, cols] + other_ref[near, cols] + decode(q_ref, half)
    w = own_ref[far, cols] + other_ref[far, cols]
    top = jnp.maximum(jnp.abs(v), jnp.abs(w))
    e = exponent(jnp.max(top, axis=0, keepdims=True))
    out_ref[near, :] = quantize(v, e)
    out_ref[far, :] = quantize(w, e)
    out_ref[m : m + TAIL, :] = tail(e)


def meet(s, q, own, other):
    m, n = own.shape[0], q.shape[1]
    out = shape((m + TAIL, n), jnp.int16)
    f = call(lambda *r: meet_body(s, *r), [VMEM] * 3, out, 8 * m * n, 12 * m * n)
    return f(q, own, other)


def join_body(s, q_ref, own_ref, other_ref, out_ref):
    m, n = own_ref.shape[0], out_ref.shape[1]
    cols = slice(s * n, (s + 1) * n)
    v = own_ref[:, cols] + other_ref[:, cols] + decode(q_ref, m)
    out_ref[0:m, :], out_ref[m : m + TAIL, :] = encode(v)


def join(s, q, own, other):
    m, n = own.shape[0], q.shape[1]
    out = shape((m + TAIL, n), jnp.int16)
    f = call(lambda *r: join_body(s, *r), [VMEM] * 3, out, 8 * m * n, 12 * m * n)
    return f(q, own, other)


def last_body(s, q_ref, own_ref, other_ref, *out_refs):
    m, n = own_ref.shape[0], q_ref.shape[1]
    part = m // 4
    core = place()[2]
    scale = scale_of(q_ref, m)
    cols = slice(s * n, (s + 1) * n)
    for k, out in enumerate(out_refs):
        vs = []
        for y in range(2):
            start = pl.multiple_of((2 * y + (core ^ k)) * part, part)
            rows = pl.ds(start, part)
            vs.append(own_ref[rows, cols] + other_ref[rows, cols] + decoded(q_ref, rows, scale))
        top = jnp.maximum(jnp.abs(vs[0]), jnp.abs(vs[1]))
        e = exponent(jnp.max(top, axis=0, keepdims=True))
        for y in range(2):
            out[y * part : (y + 1) * part, :] = quantize(vs[y], e)
        out[2 * part : 2 * part + TAIL, :] = tail(e)


def last(s, q, own, other):
    m, n = own.shape[0], q.shape[1]
    outs = [shape((m // 2 + TAIL, n), jnp.int16)] * 2
    f = call(lambda *r: last_body(s, *r), [VMEM] * 3, outs, 8 * m * n, 12 * m * n)
    return f(q, own, other)


def near_body(a_ref, b_ref, mine_ref, theirs_ref):
    part = mine_ref.shape[0] // 2
    first = jnp.full((part, b_ref.shape[1]), place()[2], jnp.int32) == 0
    for y in range(2):
        r = jnp.dot(a_ref[y], b_ref[...], preferred_element_type=jnp.float32)
        r = r.reshape(-1, 2, 8, r.shape[1])
        r = [r[:, c].reshape(part, r.shape[3]) for c in range(2)]
        rows = slice(y * part, (y + 1) * part)
        mine_ref[rows, :] = jnp.where(first, r[0], r[1])
        theirs_ref[rows, :] = jnp.where(first, r[1], r[0])


def near(a, b):
    m, (k, n) = a.shape[0] * a.shape[1], b.shape
    outs = [shape((m // 2, n), jnp.float32)] * 2
    return call(near_body, [VMEM] * 2, outs, 2 * m * n * k, 2 * m * k + 4 * m * n)(a, b)


def fold_body(s, a_ref, b_ref, mine_ref, other_ref, keep_ref, out_ref):
    part, n = keep_ref.shape
    cols = slice(s * n, (s + 1) * n)
    ylo = place()[0]
    scales = [scale_of(r, 2 * part) for r in (a_ref, b_ref)]
    for k in range(2):
        y = ylo ^ k
        rows = pl.ds(pl.multiple_of(y * part, part), part)
        v = mine_ref[rows, cols] + other_ref[rows, cols]
        for r, scale in zip((a_ref, b_ref), scales):
            v = v + decoded(r, rows, scale)
        if k == 0:
            keep_ref[...] = v
        else:
            out_ref[0:part, :], out_ref[part : part + TAIL, :] = encode(v)


def fold(s, a, b, mine, other):
    part, n = mine.shape[0] // 2, a.shape[1]
    outs = [shape((part, n), jnp.float32), shape((part + TAIL, n), jnp.int16)]
    f = call(lambda *r: fold_body(s, *r), [VMEM] * 4, outs, 8 * part * n, 12 * part * n)
    return f(a, b, mine, other)


def close_body(rows, keep_ref, *refs):
    *in_refs, out_ref = refs
    m, count, _ = out_ref.shape
    for s in range(count):
        v = -(in_refs[2 * s][...] + decode(in_refs[2 * s + 1], m))
        for i in range(m // rows):
            block = v[i * rows : (i + 1) * rows]
            own = lax.axis_index("col") * (m // rows) + i
            keep = jnp.broadcast_to(keep_ref[s, pl.ds(own, 1), :], block.shape) > 0
            out_ref[i * rows : (i + 1) * rows, s, :] = jnp.where(keep, block, 0.0)


def close(keep, rows, streams):
    m, n = streams[0][0].shape
    count = len(streams)
    f = call(
        lambda *r: close_body(rows, *r),
        [VMEM] * (1 + 2 * count),
        jax.ShapeDtypeStruct((m, count, n), jnp.float32),
        8 * count * m * n,
        14 * count * m * n,
    )
    return f(keep, *[x for stream in streams for x in stream])


def per_device(inverse_tiles, factor_panels, ancestors, valid_flags, block_slot):
    local_rows, width, local_cols, _ = inverse_tiles.shape
    count = factor_panels.shape[0]

    across = lax.ppermute(factor_panels, "col", col_perm(0, 1))
    pieces = [factor_panels, across]
    pieces += [lax.ppermute(factor_panels, "col", col_perm(*move)) for move in MOVES[2:5]]
    pieces += [lax.ppermute(across, "col", col_perm(dx, 0)) for dx, _ in MOVES[5:8]]
    keep = members(ancestors, valid_flags, block_slot, width)
    panels = assemble(keep, pieces)

    ready = prepare(inverse_tiles.reshape(local_rows, 2, NZ, width // 16, local_cols, width))

    def terms(t):
        theirs = multiply((0,), ready[0], panels) if t == 1 else multiply((0, 1), ready[2 * t - 2], panels)
        other = lax.ppermute(theirs, "row", CORE)
        mine = multiply((1,), ready[0], panels) if t == 1 else multiply((0, 1), ready[2 * t - 1], panels)
        return mine, other

    parts = [terms(t) for t in range(1, STEPS + 1)]
    mine, rest = near(ready[1], panels)
    shared = lax.ppermute(rest, "row", CORE)
    moving = [None] * count
    streams = []
    for t in range(1, STEPS + 1):
        for s in range(count):
            if t == 1:
                coded = code(s, width, *parts[0])
            elif t == 2:
                coded = meet(s, moving[s], *parts[1])
            elif t < STEPS:
                coded = join(s, moving[s], *parts[t - 1])
            else:
                straight, crossed = last(s, moving[s], *parts[t - 1])
            if t < STEPS:
                moving[s] = lax.ppermute(coded, "row", ARM)
            else:
                crossed = lax.ppermute(crossed, "row", ARM_CROSSED)
                straight = lax.ppermute(straight, "row", ARM)
            if t == STEPS:
                kept, sent = fold(s, straight, crossed, mine, shared)
                streams.append([kept, lax.ppermute(sent, "row", YLO)])
    out = close(keep, width // 32, streams)
    return out.reshape(local_rows, width // 32, count, width)


def solution(mesh):
    return jax.shard_map(
        per_device,
        mesh=mesh,
        in_specs=(P("col", None, "row", None), P(None, "row", "col", None), P(), P(), P()),
        out_specs=P("col", "row", None, None),
        check_vma=False,
    )
```

time: 75.1 us -> 66.7 us (0.89)
  Pallas kernels: 22.1 us -> 12.2 us
  waiting for transfers between devices: 23.9 us -> 29.3 us
  other arithmetic: 1.83 us -> 0 us
  local copies, waits for them, and re-layouts: 0.92 us -> 0.02 us
    pallas_call x10, Pallas kernels: 11.5 us -> 5.81 us  [the longest x1 3.65 us: prepare(): return f(a)]
    pallas_call x8, Pallas kernels: 8.67 us -> 5.05 us  [multiply(): return f(a, b)]
    ppermute x6, waiting for transfers between devices: 0.02 us -> 3.28 us  [the longest x3 3.27 us: per_device(): lax.ppermute(across, 'col', col_perm(dx, 0))]
    ppermute x2, waiting for transfers between devices: 1.4 us -> 3.36 us  [per_device(): straight = lax.ppermute(straight, 'row', ARM)]
    ppermute x1, starting transfers between devices: 1.49 us -> 3.28 us  [per_device(): across = lax.ppermute(factor_panels, 'col', col_perm(0, 1))]
    ppermute x2, starting transfers between devices: 3.31 us -> 1.53 us  [per_device(): streams.append([kept, lax.ppermute(sent, 'row', YLO)])]
    ppermute x1, waiting for transfers between devices: 1.49 us -> 0.01 us  [per_device(): across = lax.ppermute(factor_panels, 'col', col_perm(0, 1))]
    ppermute x4, waiting for transfers between devices: 0.01 us -> 1.36 us  [terms(): other = lax.ppermute(theirs, 'row', CORE)]
  transfers between devices with their start and end apart: 24 -> 24, of which waited for: 11 -> 13; matrix products, arithmetic and copies ran while one was open for 4% -> 0% of each run, Pallas kernels for 25% -> 16%
where the time goes in v3:
time: 66.7 us; the launch traced here: 65.9 us
  waiting for transfers between devices  29.3 us (44%)
  starting transfers between devices  24.1 us (36%)
  Pallas kernels  12.2 us (18%)
    ppermute x6, waiting for transfers between devices, per_device(): moving[s] = lax.ppermute(coded, 'row', ARM)  17.2 us
    pallas_call x8, Pallas kernels, multiply(): return f(a, b)  5.05 us
    ppermute x3, starting transfers between devices, per_device(): lax.ppermute(factor_panels, 'col', col_perm(*move))  4.76 us
    ppermute x6, starting transfers between devices, per_device(): moving[s] = lax.ppermute(coded, 'row', ARM)  4.5 us
    ppermute x3, starting transfers between devices, per_device(): lax.ppermute(across, 'col', col_perm(dx, 0))  4.36 us
    ppermute x2, waiting for transfers between devices, per_device(): streams.append([kept, lax.ppermute(sent, 'row', YLO)])  4.12 us
    pallas_call x1, Pallas kernels, prepare(): return f(a)  3.65 us
    ppermute x2, waiting for transfers between devices, per_device(): straight = lax.ppermute(straight, 'row', ARM)  3.36 us
  transfers between devices with their start and end apart: 24, of which 13 were waited for; matrix products, arithmetic and copies ran while one was open for 0% of the time, Pallas kernels for 16%

profile of v3, /device:TPU:2, one launch (start us, length us, event | category | flops | bytes accessed | tf_op | source)
XLA Modules:
  0.0 65.9 jit_solution(14627410189038870031)
XLA Ops:
  0.0 3.3 %collective-permute-start = (bf16[2,4,32,256]{3,2,1,0:T(8,128)(2,1)}, bf16[2,4,32,256]{3,2,1,0:T(8,128)(2,1)S(1)}, u32[]{:S(2)}, u32[]{:S(2)}) collective-permute-start(bf16[2,4,32,256]{3,2,1,0:T(8,128)(2,1)} %refs_0_.1), channel_id=1, source_target_pairs={{0,1},{1,0},{2,3},{3,2},{4,5},{5,4},{6,7},{7,6},{8,9},{9,8},{10,11... | collective-permute-start | bytes 393224 | tf_op jit(solution)/shard_map/ppermute | solution.py:363
  3.3 1.5 %collective-permute-start.2 = (bf16[2,4,32,256]{3,2,1,0:T(8,128)(2,1)}, bf16[2,4,32,256]{3,2,1,0:T(8,128)(2,1)S(1)}, u32[]{:S(2)}, u32[]{:S(2)}) collective-permute-start(bf16[2,4,32,256]{3,2,1,0:T(8,128)(2,1)} %refs_0_.1), channel_id=1, source_target_pairs={{0,2},{1,3},{2,4},{3,5},{4,6},{5,7},{6,0},{7,1},{8,10},{9,11},{10,... | collective-permute-start | bytes 393224 | tf_op jit(solution)/shard_map/ppermute | solution.py:365
  4.8 1.1 %collective-permute-start.1 = (bf16[2,4,32,256]{3,2,1,0:T(8,128)(2,1)}, bf16[2,4,32,256]{3,2,1,0:T(8,128)(2,1)S(1)}, u32[]{:S(2)}, u32[]{:S(2)}) collective-permute-start(bf16[2,4,32,256]{3,2,1,0:T(8,128)(2,1)} %refs_0_.1), channel_id=1, source_target_pairs={{0,4},{1,5},{2,6},{3,7},{4,0},{5,1},{6,2},{7,3},{8,12},{9,13},{10,... | collective-permute-start | bytes 393224 | tf_op jit(solution)/shard_map/ppermute | solution.py:365
  5.9 2.2 %collective-permute-start.3 = (bf16[2,4,32,256]{3,2,1,0:T(8,128)(2,1)}, bf16[2,4,32,256]{3,2,1,0:T(8,128)(2,1)S(1)}, u32[]{:S(2)}, u32[]{:S(2)}) collective-permute-start(bf16[2,4,32,256]{3,2,1,0:T(8,128)(2,1)} %refs_0_.1), channel_id=1, source_target_pairs={{0,6},{1,7},{2,0},{3,1},{4,2},{5,3},{6,4},{7,5},{8,14},{9,15},{10,... | collective-permute-start | bytes 393224 | tf_op jit(solution)/shard_map/ppermute | solution.py:365
  8.1 1.4 %collective-permute-start.6 = (bf16[2,4,32,256]{3,2,1,0:T(8,128)(2,1)S(1)}, bf16[2,4,32,256]{3,2,1,0:T(8,128)(2,1)S(1)}, u32[]{:S(2)}, u32[]{:S(2)}) collective-permute-start(bf16[2,4,32,256]{3,2,1,0:T(8,128)(2,1)S(1)} %collective-permute-done.refs_1_), channel_id=1, source_target_pairs={{0,6},{1,7},{2,0},{3,1},{4,2},{5,3},{6,4},{7,5},{8,14},{9,15},{10,... | collective-permute-start | bytes 393224 | tf_op jit(solution)/shard_map/ppermute | solution.py:366
  9.5 0.6 collective-permute-start.5
  10.1 2.3 %collective-permute-start.4 = (bf16[2,4,32,256]{3,2,1,0:T(8,128)(2,1)S(1)}, bf16[2,4,32,256]{3,2,1,0:T(8,128)(2,1)S(1)}, u32[]{:S(2)}, u32[]{:S(2)}) collective-permute-start(bf16[2,4,32,256]{3,2,1,0:T(8,128)(2,1)S(1)} %collective-permute-done.refs_1_), channel_id=1, source_target_pairs={{0,4},{1,5},{2,6},{3,7},{4,0},{5,1},{6,2},{7,3},{8,12},{9,13},{10,... | collective-permute-start | bytes 393224 | tf_op jit(solution)/shard_map/ppermute | solution.py:366
  12.4 3.6 %shard_map.56 = (bf16[2,256,1024]{2,1,0:T(8,128)(2,1)S(1)}, bf16[2,256,1024]{2,1,0:T(8,128)(2,1)S(1)}, bf16[2,256,1024]{2,1,0:T(8,128)(2,1)S(1)}, bf16[2,256,102...) custom-call(bf16[16,2,8,16,4,256]{5,4,3,2,1,0:T(4,128)(2,1)} %bitcast.14), custom_call_target="tpu_custom_call" | custom-call | bytes 16777216 | tf_op jit(solution)/shard_map/pallas_call | solution.py:195
  16.1 0.2 shard_map.55.keep_ref.r_0_
  16.4 0.7 %collective-permute-done.6.refs_7_ = bf16[2,4,32,256]{3,2,1,0:T(8,128)(2,1)S(1)} collective-permute-done((bf16[2,4,32,256]{3,2,1,0:T(8,128)(2,1)S(1)}, bf16[2,4,32,256]{3,2,1,0:T(8,128)(2,1)S(1)}, u32[]{:S(2)}, u32[]{:S(2)}) %collective-permute-start.6) | collective-permute-done | bytes 131104 | tf_op jit(solution)/shard_map/ppermute | solution.py:366
  17.1 2.6 %collective-permute-done.4.refs_5_ = bf16[2,4,32,256]{3,2,1,0:T(8,128)(2,1)S(1)} collective-permute-done((bf16[2,4,32,256]{3,2,1,0:T(8,128)(2,1)S(1)}, bf16[2,4,32,256]{3,2,1,0:T(8,128)(2,1)S(1)}, u32[]{:S(2)}, u32[]{:S(2)}) %collective-permute-start.4) | collective-permute-done | bytes 131104 | tf_op jit(solution)/shard_map/ppermute | solution.py:366
  19.7 0.3 shard_map.57
  19.9 0.7 %shard_map.62 = f32[512,512]{1,0:T(8,128)S(1)} custom-call(bf16[2,256,1024]{2,1,0:T(8,128)(2,1)S(1)} %get-tuple-element.25.refs_0_, bf16[1024,512]{1,0:T(8,128)(2,1)S(1)} %bitcast.4), custom_call_target="tpu_custom_call" | custom-call | flops 536870912 | bytes 2097152 | tf_op jit(solution)/shard_map/pallas_call | solution.py:212
  20.7 0.7 %shard_map.65 = f32[512,512]{1,0:T(8,128)S(1)} custom-call(bf16[2,256,1024]{2,1,0:T(8,128)(2,1)S(1)} %get-tuple-element.27.refs_0_, bf16[1024,512]{1,0:T(8,128)(2,1)S(1)} %bitcast.5), custom_call_target="tpu_custom_call" | custom-call | flops 536870912 | bytes 2097152 | tf_op jit(solution)/shard_map/pallas_call | solution.py:212
  21.4 0.6 collective-permute-start.11
  22.0 0.4 shard_map.59
  22.5 0.7 %shard_map.68 = f32[512,512]{1,0:T(8,128)S(1)} custom-call(bf16[2,256,1024]{2,1,0:T(8,128)(2,1)S(1)} %get-tuple-element.29.refs_0_, bf16[1024,512]{1,0:T(8,128)(2,1)S(1)} %bitcast.7), custom_call_target="tpu_custom_call" | custom-call | flops 536870912 | bytes 2097152 | tf_op jit(solution)/shard_map/pallas_call | solution.py:212
  23.3 0.6 collective-permute-start.13
  23.8 0.4 shard_map.58.r_0_
  24.3 1.3 %collective-permute-done.7.r_1_ = f32[256,512]{1,0:T(8,128)S(1)} collective-permute-done((f32[256,512]{1,0:T(8,128)S(1)}, f32[256,512]{1,0:T(8,128)S(1)}, u32[]{:S(2)}, u32[]{:S(2)}) %collective-permute-start.7) | collective-permute-done | bytes 524320 | tf_op jit(solution)/shard_map/ppermute | solution.py:374
  25.7 2.0 %collective-permute-start.18 = (s16[272,256]{1,0:T(8,128)(2,1)S(1)}, s16[272,256]{1,0:T(8,128)(2,1)S(1)}, u32[]{:S(2)}, u32[]{:S(2)}) collective-permute-start(s16[272,256]{1,0:T(8,128)(2,1)S(1)} %shard_map.72), channel_id=1, source_target_pairs={{0,16},{8,120},{16,32},{24,8},{32,48},{40,24},{48,64},{56,40},{64,... | collective-permute-start | bytes 417800 | tf_op jit(solution)/shard_map/ppermute | solution.py:394
  27.8 2.2 %collective-permute-start.8 = (s16[272,256]{1,0:T(8,128)(2,1)S(1)}, s16[272,256]{1,0:T(8,128)(2,1)S(1)}, u32[]{:S(2)}, u32[]{:S(2)}) collective-permute-start(s16[272,256]{1,0:T(8,128)(2,1)S(1)} %shard_map.60), channel_id=1, source_target_pairs={{0,16},{8,120},{16,32},{24,8},{32,48},{40,24},{48,64},{56,40},{64,... | collective-permute-start | bytes 417800 | tf_op jit(solution)/shard_map/ppermute | solution.py:394
  30.0 0.7 %shard_map.61.r_1_ = f32[512,512]{1,0:T(8,128)S(1)} custom-call(bf16[2,256,1024]{2,1,0:T(8,128)(2,1)S(1)} %get-tuple-element.24.refs_0_, bf16[1024,512]{1,0:T(8,128)(2,1)S(1)} %bitcast.9), custom_call_target="tpu_custom_call" | custom-call | flops 536870912 | bytes 2097152 | tf_op jit(solution)/shard_map/pallas_call | solution.py:212
  30.7 4.0 %collective-permute-done.18.r_0_ = s16[272,256]{1,0:T(8,128)(2,1)S(1)} collective-permute-done((s16[272,256]{1,0:T(8,128)(2,1)S(1)}, s16[272,256]{1,0:T(8,128)(2,1)S(1)}, u32[]{:S(2)}, u32[]{:S(2)}) %collective-permute-start.18) | collective-permute-done | bytes 139296 | tf_op jit(solution)/shard_map/ppermute | solution.py:394
  34.7 0.2 shard_map.73
  34.9 1.2 %collective-permute-done.8.r_0_ = s16[272,256]{1,0:T(8,128)(2,1)S(1)} collective-permute-done((s16[272,256]{1,0:T(8,128)(2,1)S(1)}, s16[272,256]{1,0:T(8,128)(2,1)S(1)}, u32[]{:S(2)}, u32[]{:S(2)}) %collective-permute-start.8) | collective-permute-done | bytes 139296 | tf_op jit(solution)/shard_map/ppermute | solution.py:394
  36.2 0.2 shard_map.63
  36.4 0.7 %shard_map.70 = (f32[256,512]{1,0:T(8,128)S(1)}, f32[256,512]{1,0:T(8,128)S(1)}) custom-call(bf16[2,256,1024]{2,1,0:T(8,128)(2,1)S(1)} %get-tuple-element.32.a_ref, bf16[1024,512]{1,0:T(8,128)(2,1)S(1)} %bitcast.10), custom_call_target="tpu_custom_call" | custom-call | flops 536870912 | bytes 2097152 | tf_op jit(solution)/shard_map/pallas_call | solution.py:307
  37.2 2.0 %collective-permute-start.16 = (f32[256,512]{1,0:T(8,128)S(1)}, f32[256,512]{1,0:T(8,128)S(1)}, u32[]{:S(2)}, u32[]{:S(2)}) collective-permute-start(f32[256,512]{1,0:T(8,128)S(1)} %get-tuple-element.34), channel_id=1, source_target_pairs={{0,8},{8,0},{16,24},{24,16},{32,40},{40,32},{48,56},{56,48},{64,72... | collective-permute-start | bytes 1572872 | tf_op jit(solution)/shard_map/ppermute | solution.py:380
  39.2 0.7 %shard_map.64.r_1_ = f32[512,512]{1,0:T(8,128)S(1)} custom-call(bf16[2,256,1024]{2,1,0:T(8,128)(2,1)S(1)} %get-tuple-element.26.refs_0_, bf16[1024,512]{1,0:T(8,128)(2,1)S(1)} %bitcast.11), custom_call_target="tpu_custom_call" | custom-call | flops 536870912 | bytes 2097152 | tf_op jit(solution)/shard_map/pallas_call | solution.py:212
  39.9 2.7 %collective-permute-done.19.r_0_ = s16[528,256]{1,0:T(8,128)(2,1)S(1)} collective-permute-done((s16[528,256]{1,0:T(8,128)(2,1)S(1)}, s16[528,256]{1,0:T(8,128)(2,1)S(1)}, u32[]{:S(2)}, u32[]{:S(2)}) %collective-permute-start.19) | collective-permute-done | bytes 270368 | tf_op jit(solution)/shard_map/ppermute | solution.py:394
  42.6 0.2 shard_map.74
  42.9 2.6 %collective-permute-done.10.r_0_ = s16[528,256]{1,0:T(8,128)(2,1)S(1)} collective-permute-done((s16[528,256]{1,0:T(8,128)(2,1)S(1)}, s16[528,256]{1,0:T(8,128)(2,1)S(1)}, u32[]{:S(2)}, u32[]{:S(2)}) %collective-permute-start.10) | collective-permute-done | bytes 270368 | tf_op jit(solution)/shard_map/ppermute | solution.py:394
  45.5 0.2 shard_map.66
  45.8 0.7 %shard_map.67.r_1_ = f32[512,512]{1,0:T(8,128)S(1)} custom-call(bf16[2,256,1024]{2,1,0:T(8,128)(2,1)S(1)} %get-tuple-element.28.refs_0_, bf16[1024,512]{1,0:T(8,128)(2,1)S(1)} %bitcast.12), custom_call_target="tpu_custom_call" | custom-call | flops 536870912 | bytes 2097152 | tf_op jit(solution)/shard_map/pallas_call | solution.py:212
  46.5 4.0 %collective-permute-done.20.r_0_ = s16[528,256]{1,0:T(8,128)(2,1)S(1)} collective-permute-done((s16[528,256]{1,0:T(8,128)(2,1)S(1)}, s16[528,256]{1,0:T(8,128)(2,1)S(1)}, u32[]{:S(2)}, u32[]{:S(2)}) %collective-permute-start.20) | collective-permute-done | bytes 270368 | tf_op jit(solution)/shard_map/ppermute | solution.py:394
  50.5 0.2 shard_map.75
  50.9 2.5 %collective-permute-done.12.r_0_ = s16[528,256]{1,0:T(8,128)(2,1)S(1)} collective-permute-done((s16[528,256]{1,0:T(8,128)(2,1)S(1)}, s16[528,256]{1,0:T(8,128)(2,1)S(1)}, u32[]{:S(2)}, u32[]{:S(2)}) %collective-permute-start.12) | collective-permute-done | bytes 270368 | tf_op jit(solution)/shard_map/ppermute | solution.py:394
  53.4 0.2 shard_map.69
  53.7 2.0 %collective-permute-start.15 = (s16[272,256]{1,0:T(8,128)(2,1)S(1)}, s16[272,256]{1,0:T(8,128)(2,1)S(1)}, u32[]{:S(2)}, u32[]{:S(2)}) collective-permute-start(s16[272,256]{1,0:T(8,128)(2,1)S(1)} %get-tuple-element.31), channel_id=1, source_target_pairs={{0,24},{8,112},{16,40},{24,0},{32,56},{40,16},{48,72},{56,32},{64,... | collective-permute-start | bytes 417800 | tf_op jit(solution)/shard_map/ppermute | solution.py:396
  55.8 1.3 %collective-permute-done.21.r_0_ = s16[272,256]{1,0:T(8,128)(2,1)S(1)} collective-permute-done((s16[272,256]{1,0:T(8,128)(2,1)S(1)}, s16[272,256]{1,0:T(8,128)(2,1)S(1)}, u32[]{:S(2)}, u32[]{:S(2)}) %collective-permute-start.21) | collective-permute-done | bytes 139296 | tf_op jit(solution)/shard_map/ppermute | solution.py:397
  57.2 0.8 %collective-permute-start.23 = (s16[144,256]{1,0:T(8,128)(2,1)S(1)}, s16[144,256]{1,0:T(8,128)(2,1)S(1)}, u32[]{:S(2)}, u32[]{:S(2)}) collective-permute-start(s16[144,256]{1,0:T(8,128)(2,1)S(1)} %get-tuple-element.40), channel_id=1, source_target_pairs={{0,128},{8,136},{16,144},{24,152},{32,160},{40,168},{48,176},{56,1... | collective-permute-start | bytes 221192 | tf_op jit(solution)/shard_map/ppermute | solution.py:400
  58.0 2.1 %collective-permute-done.14.r_0_ = s16[272,256]{1,0:T(8,128)(2,1)S(1)} collective-permute-done((s16[272,256]{1,0:T(8,128)(2,1)S(1)}, s16[272,256]{1,0:T(8,128)(2,1)S(1)}, u32[]{:S(2)}, u32[]{:S(2)}) %collective-permute-start.14) | collective-permute-done | bytes 139296 | tf_op jit(solution)/shard_map/ppermute | solution.py:397
  60.0 0.1 shard_map.71
  60.2 0.8 %collective-permute-start.17 = (s16[144,256]{1,0:T(8,128)(2,1)S(1)}, s16[144,256]{1,0:T(8,128)(2,1)S(1)}, u32[]{:S(2)}, u32[]{:S(2)}) collective-permute-start(s16[144,256]{1,0:T(8,128)(2,1)S(1)} %get-tuple-element.36), channel_id=1, source_target_pairs={{0,128},{8,136},{16,144},{24,152},{32,160},{40,168},{48,176},{56,1... | collective-permute-start | bytes 221192 | tf_op jit(solution)/shard_map/ppermute | solution.py:400
  61.0 1.1 %collective-permute-done.23.r_4_ = s16[144,256]{1,0:T(8,128)(2,1)S(1)} collective-permute-done((s16[144,256]{1,0:T(8,128)(2,1)S(1)}, s16[144,256]{1,0:T(8,128)(2,1)S(1)}, u32[]{:S(2)}, u32[]{:S(2)}) %collective-permute-start.23) | collective-permute-done | bytes 73760 | tf_op jit(solution)/shard_map/ppermute | solution.py:400
  62.1 3.0 %collective-permute-done.17.r_2_ = s16[144,256]{1,0:T(8,128)(2,1)S(1)} collective-permute-done((s16[144,256]{1,0:T(8,128)(2,1)S(1)}, s16[144,256]{1,0:T(8,128)(2,1)S(1)}, u32[]{:S(2)}, u32[]{:S(2)}) %collective-permute-start.17) | collective-permute-done | bytes 73760 | tf_op jit(solution)/shard_map/ppermute | solution.py:400
  65.1 0.8 %shard_map.77 = f32[128,2,256]{2,1,0:T(2,128)} custom-call(f32[2,128,256]{2,1,0:T(8,128)S(1)} %shard_map.55.keep_ref.r_0_, f32[128,256]{1,0:T(8,128)S(1)} %get-tuple-element.35.r_1_, s16[144,256]{1,0:T(8,128)(2,1)S(1)} %collective-permute-done.17.r_2_, f32[128,256]{1,0:T(8,128)S(1)} %get-tuple-element.39.r_3_, s16[144,256]{1,0:T(8,128)(2,1)S(1)} %collective-permute-done.23.r_4_), custom_call_target="tpu_custom_call" | custom-call | flops 524288 | bytes 917504 | tf_op jit(solution)/shard_map/pallas_call | solution.py:356
  (31 shorter events, 1.1 us)
Async XLA Ops:
  0.0 19.7 %copy-start = (bf16[2,4,32,256]{3,2,1,0:T(8,128)(2,1)S(1)}, bf16[2,4,32,256]{3,2,1,0:T(8,128)(2,1)}, u32[]{:S(2)}) copy-start(bf16[2,4,32,256]{3,2,1,0:T(8,128)(2,1)} %refs_0_.1) | copy-start | bytes 393220
  0.0 16.1 %copy-start.3 = (s32[128]{0:T(128)S(1)}, s32[128]{0:T(128)}, u32[]{:S(2)}) copy-start(s32[128]{0:T(128)} %param.9) | copy-start | bytes 1540
  0.0 16.1 %copy-start.2 = (s32[2,96]{1,0:T(2,128)S(1)}, s32[2,96]{1,0:T(2,128)}, u32[]{:S(2)}) copy-start(s32[2,96]{1,0:T(2,128)} %flags_ref.1) | copy-start | bytes 2308
  0.0 16.1 %copy-start.1 = (s32[2,96]{1,0:T(2,128)S(1)}, s32[2,96]{1,0:T(2,128)}, u32[]{:S(2)}) copy-start(s32[2,96]{1,0:T(2,128)} %ancestors_ref.1) | copy-start | bytes 2308
  0.0 8.0 %collective-permute-start = (bf16[2,4,32,256]{3,2,1,0:T(8,128)(2,1)}, bf16[2,4,32,256]{3,2,1,0:T(8,128)(2,1)S(1)}, u32[]{:S(2)}, u32[]{:S(2)}) collective-permute-start(bf16[2,4,32,256]{3,2,1,0:T(8,128)(2,1)} %refs_0_.1), channel_id=1, source_target_pairs={{0,1},{1,0},{2,3},{3,2},{4,5},{5,4},{6,7},{7,6},{8,9},{9,8},{10,11... | collective-permute-start | bytes 393224 | tf_op jit(solution)/shard_map/ppermute | solution.py:363
  3.3 6.8 %collective-permute-start.2 = (bf16[2,4,32,256]{3,2,1,0:T(8,128)(2,1)}, bf16[2,4,32,256]{3,2,1,0:T(8,128)(2,1)S(1)}, u32[]{:S(2)}, u32[]{:S(2)}) collective-permute-start(bf16[2,4,32,256]{3,2,1,0:T(8,128)(2,1)} %refs_0_.1), channel_id=1, source_target_pairs={{0,2},{1,3},{2,4},{3,5},{4,6},{5,7},{6,0},{7,1},{8,10},{9,11},{10,... | collective-permute-start | bytes 393224 | tf_op jit(solution)/shard_map/ppermute | solution.py:365
  4.8 11.6 %collective-permute-start.1 = (bf16[2,4,32,256]{3,2,1,0:T(8,128)(2,1)}, bf16[2,4,32,256]{3,2,1,0:T(8,128)(2,1)S(1)}, u32[]{:S(2)}, u32[]{:S(2)}) collective-permute-start(bf16[2,4,32,256]{3,2,1,0:T(8,128)(2,1)} %refs_0_.1), channel_id=1, source_target_pairs={{0,4},{1,5},{2,6},{3,7},{4,0},{5,1},{6,2},{7,3},{8,12},{9,13},{10,... | collective-permute-start | bytes 393224 | tf_op jit(solution)/shard_map/ppermute | solution.py:365
  5.9 10.5 %collective-permute-start.3 = (bf16[2,4,32,256]{3,2,1,0:T(8,128)(2,1)}, bf16[2,4,32,256]{3,2,1,0:T(8,128)(2,1)S(1)}, u32[]{:S(2)}, u32[]{:S(2)}) collective-permute-start(bf16[2,4,32,256]{3,2,1,0:T(8,128)(2,1)} %refs_0_.1), channel_id=1, source_target_pairs={{0,6},{1,7},{2,0},{3,1},{4,2},{5,3},{6,4},{7,5},{8,14},{9,15},{10,... | collective-permute-start | bytes 393224 | tf_op jit(solution)/shard_map/ppermute | solution.py:365
  8.1 9.0 %collective-permute-start.6 = (bf16[2,4,32,256]{3,2,1,0:T(8,128)(2,1)S(1)}, bf16[2,4,32,256]{3,2,1,0:T(8,128)(2,1)S(1)}, u32[]{:S(2)}, u32[]{:S(2)}) collective-permute-start(bf16[2,4,32,256]{3,2,1,0:T(8,128)(2,1)S(1)} %collective-permute-done.refs_1_), channel_id=1, source_target_pairs={{0,6},{1,7},{2,0},{3,1},{4,2},{5,3},{6,4},{7,5},{8,14},{9,15},{10,... | collective-permute-start | bytes 393224 | tf_op jit(solution)/shard_map/ppermute | solution.py:366
  9.5 7.6 %collective-permute-start.5 = (bf16[2,4,32,256]{3,2,1,0:T(8,128)(2,1)S(1)}, bf16[2,4,32,256]{3,2,1,0:T(8,128)(2,1)S(1)}, u32[]{:S(2)}, u32[]{:S(2)}) collective-permute-start(bf16[2,4,32,256]{3,2,1,0:T(8,128)(2,1)S(1)} %collective-permute-done.refs_1_), channel_id=1, source_target_pairs={{0,2},{1,3},{2,4},{3,5},{4,6},{5,7},{6,0},{7,1},{8,10},{9,11},{10,... | collective-permute-start | bytes 393224 | tf_op jit(solution)/shard_map/ppermute | solution.py:366
  10.1 9.6 %collective-permute-start.4 = (bf16[2,4,32,256]{3,2,1,0:T(8,128)(2,1)S(1)}, bf16[2,4,32,256]{3,2,1,0:T(8,128)(2,1)S(1)}, u32[]{:S(2)}, u32[]{:S(2)}) collective-permute-start(bf16[2,4,32,256]{3,2,1,0:T(8,128)(2,1)S(1)} %collective-permute-done.refs_1_), channel_id=1, source_target_pairs={{0,4},{1,5},{2,6},{3,7},{4,0},{5,1},{6,2},{7,3},{8,12},{9,13},{10,... | collective-permute-start | bytes 393224 | tf_op jit(solution)/shard_map/ppermute | solution.py:366
  20.6 14.1 %collective-permute-start.9 = (f32[512,512]{1,0:T(8,128)S(1)}, f32[512,512]{1,0:T(8,128)S(1)}, u32[]{:S(2)}, u32[]{:S(2)}) collective-permute-start(f32[512,512]{1,0:T(8,128)S(1)} %shard_map.62), channel_id=1, source_target_pairs={{0,8},{8,0},{16,24},{24,16},{32,40},{40,32},{48,56},{56,48},{64,72... | collective-permute-start | bytes 3145736 | tf_op jit(solution)/shard_map/ppermute | solution.py:374
  21.4 18.4 %collective-permute-start.11 = (f32[512,512]{1,0:T(8,128)S(1)}, f32[512,512]{1,0:T(8,128)S(1)}, u32[]{:S(2)}, u32[]{:S(2)}) collective-permute-start(f32[512,512]{1,0:T(8,128)S(1)} %shard_map.65), channel_id=1, source_target_pairs={{0,8},{8,0},{16,24},{24,16},{32,40},{40,32},{48,56},{56,48},{64,72... | collective-permute-start | bytes 3145736 | tf_op jit(solution)/shard_map/ppermute | solution.py:374
  22.4 3.2 %collective-permute-start.7 = (f32[256,512]{1,0:T(8,128)S(1)}, f32[256,512]{1,0:T(8,128)S(1)}, u32[]{:S(2)}, u32[]{:S(2)}) collective-permute-start(f32[256,512]{1,0:T(8,128)S(1)} %shard_map.59), channel_id=1, source_target_pairs={{0,8},{8,0},{16,24},{24,16},{32,40},{40,32},{48,56},{56,48},{64,72... | collective-permute-start | bytes 1572872 | tf_op jit(solution)/shard_map/ppermute | solution.py:374
  23.3 23.2 %collective-permute-start.13 = (f32[512,512]{1,0:T(8,128)S(1)}, f32[512,512]{1,0:T(8,128)S(1)}, u32[]{:S(2)}, u32[]{:S(2)}) collective-permute-start(f32[512,512]{1,0:T(8,128)S(1)} %shard_map.68), channel_id=1, source_target_pairs={{0,8},{8,0},{16,24},{24,16},{32,40},{40,32},{48,56},{56,48},{64,72... | collective-permute-start | bytes 3145736 | tf_op jit(solution)/shard_map/ppermute | solution.py:374
  25.7 9.0 %collective-permute-start.18 = (s16[272,256]{1,0:T(8,128)(2,1)S(1)}, s16[272,256]{1,0:T(8,128)(2,1)S(1)}, u32[]{:S(2)}, u32[]{:S(2)}) collective-permute-start(s16[272,256]{1,0:T(8,128)(2,1)S(1)} %shard_map.72), channel_id=1, source_target_pairs={{0,16},{8,120},{16,32},{24,8},{32,48},{40,24},{48,64},{56,40},{64,... | collective-permute-start | bytes 417800 | tf_op jit(solution)/shard_map/ppermute | solution.py:394
  27.8 8.4 %collective-permute-start.8 = (s16[272,256]{1,0:T(8,128)(2,1)S(1)}, s16[272,256]{1,0:T(8,128)(2,1)S(1)}, u32[]{:S(2)}, u32[]{:S(2)}) collective-permute-start(s16[272,256]{1,0:T(8,128)(2,1)S(1)} %shard_map.60), channel_id=1, source_target_pairs={{0,16},{8,120},{16,32},{24,8},{32,48},{40,24},{48,64},{56,40},{64,... | collective-permute-start | bytes 417800 | tf_op jit(solution)/shard_map/ppermute | solution.py:394
  34.9 7.7 %collective-permute-start.19 = (s16[528,256]{1,0:T(8,128)(2,1)S(1)}, s16[528,256]{1,0:T(8,128)(2,1)S(1)}, u32[]{:S(2)}, u32[]{:S(2)}) collective-permute-start(s16[528,256]{1,0:T(8,128)(2,1)S(1)} %shard_map.73), channel_id=1, source_target_pairs={{0,16},{8,120},{16,32},{24,8},{32,48},{40,24},{48,64},{56,40},{64,... | collective-permute-start | bytes 811016 | tf_op jit(solution)/shard_map/ppermute | solution.py:394
  36.3 9.2 %collective-permute-start.10 = (s16[528,256]{1,0:T(8,128)(2,1)S(1)}, s16[528,256]{1,0:T(8,128)(2,1)S(1)}, u32[]{:S(2)}, u32[]{:S(2)}) collective-permute-start(s16[528,256]{1,0:T(8,128)(2,1)S(1)} %shard_map.63), channel_id=1, source_target_pairs={{0,16},{8,120},{16,32},{24,8},{32,48},{40,24},{48,64},{56,40},{64,... | collective-permute-start | bytes 811016 | tf_op jit(solution)/shard_map/ppermute | solution.py:394
  37.2 18.6 %collective-permute-start.16 = (f32[256,512]{1,0:T(8,128)S(1)}, f32[256,512]{1,0:T(8,128)S(1)}, u32[]{:S(2)}, u32[]{:S(2)}) collective-permute-start(f32[256,512]{1,0:T(8,128)S(1)} %get-tuple-element.34), channel_id=1, source_target_pairs={{0,8},{8,0},{16,24},{24,16},{32,40},{40,32},{48,56},{56,48},{64,72... | collective-permute-start | bytes 1572872 | tf_op jit(solution)/shard_map/ppermute | solution.py:380
  42.8 7.7 %collective-permute-start.20 = (s16[528,256]{1,0:T(8,128)(2,1)S(1)}, s16[528,256]{1,0:T(8,128)(2,1)S(1)}, u32[]{:S(2)}, u32[]{:S(2)}) collective-permute-start(s16[528,256]{1,0:T(8,128)(2,1)S(1)} %shard_map.74), channel_id=1, source_target_pairs={{0,16},{8,120},{16,32},{24,8},{32,48},{40,24},{48,64},{56,40},{64,... | collective-permute-start | bytes 811016 | tf_op jit(solution)/shard_map/ppermute | solution.py:394
  45.7 7.7 %collective-permute-start.12 = (s16[528,256]{1,0:T(8,128)(2,1)S(1)}, s16[528,256]{1,0:T(8,128)(2,1)S(1)}, u32[]{:S(2)}, u32[]{:S(2)}) collective-permute-start(s16[528,256]{1,0:T(8,128)(2,1)S(1)} %shard_map.66), channel_id=1, source_target_pairs={{0,16},{8,120},{16,32},{24,8},{32,48},{40,24},{48,64},{56,40},{64,... | collective-permute-start | bytes 811016 | tf_op jit(solution)/shard_map/ppermute | solution.py:394
  50.7 6.3 %collective-permute-start.21 = (s16[272,256]{1,0:T(8,128)(2,1)S(1)}, s16[272,256]{1,0:T(8,128)(2,1)S(1)}, u32[]{:S(2)}, u32[]{:S(2)}) collective-permute-start(s16[272,256]{1,0:T(8,128)(2,1)S(1)} %get-tuple-element.37), channel_id=1, source_target_pairs={{0,16},{8,120},{16,32},{24,8},{32,48},{40,24},{48,64},{56,40},{64,... | collective-permute-start | bytes 417800 | tf_op jit(solution)/shard_map/ppermute | solution.py:397
  50.8 6.3 %collective-permute-start.22 = (s16[272,256]{1,0:T(8,128)(2,1)S(1)}, s16[272,256]{1,0:T(8,128)(2,1)S(1)}, u32[]{:S(2)}, u32[]{:S(2)}) collective-permute-start(s16[272,256]{1,0:T(8,128)(2,1)S(1)} %get-tuple-element.38), channel_id=1, source_target_pairs={{0,24},{8,112},{16,40},{24,0},{32,56},{40,16},{48,72},{56,32},{64,... | collective-permute-start | bytes 417800 | tf_op jit(solution)/shard_map/ppermute | solution.py:396
  53.6 6.4 %collective-permute-start.14 = (s16[272,256]{1,0:T(8,128)(2,1)S(1)}, s16[272,256]{1,0:T(8,128)(2,1)S(1)}, u32[]{:S(2)}, u32[]{:S(2)}) collective-permute-start(s16[272,256]{1,0:T(8,128)(2,1)S(1)} %get-tuple-element.30), channel_id=1, source_target_pairs={{0,16},{8,120},{16,32},{24,8},{32,48},{40,24},{48,64},{56,40},{64,... | collective-permute-start | bytes 417800 | tf_op jit(solution)/shard_map/ppermute | solution.py:397
  53.7 6.3 %collective-permute-start.15 = (s16[272,256]{1,0:T(8,128)(2,1)S(1)}, s16[272,256]{1,0:T(8,128)(2,1)S(1)}, u32[]{:S(2)}, u32[]{:S(2)}) collective-permute-start(s16[272,256]{1,0:T(8,128)(2,1)S(1)} %get-tuple-element.31), channel_id=1, source_target_pairs={{0,24},{8,112},{16,40},{24,0},{32,56},{40,16},{48,72},{56,32},{64,... | collective-permute-start | bytes 417800 | tf_op jit(solution)/shard_map/ppermute | solution.py:396
  57.2 4.9 %collective-permute-start.23 = (s16[144,256]{1,0:T(8,128)(2,1)S(1)}, s16[144,256]{1,0:T(8,128)(2,1)S(1)}, u32[]{:S(2)}, u32[]{:S(2)}) collective-permute-start(s16[144,256]{1,0:T(8,128)(2,1)S(1)} %get-tuple-element.40), channel_id=1, source_target_pairs={{0,128},{8,136},{16,144},{24,152},{32,160},{40,168},{48,176},{56,1... | collective-permute-start | bytes 221192 | tf_op jit(solution)/shard_map/ppermute | solution.py:400
  60.2 4.9 %collective-permute-start.17 = (s16[144,256]{1,0:T(8,128)(2,1)S(1)}, s16[144,256]{1,0:T(8,128)(2,1)S(1)}, u32[]{:S(2)}, u32[]{:S(2)}) collective-permute-start(s16[144,256]{1,0:T(8,128)(2,1)S(1)} %get-tuple-element.36), channel_id=1, source_target_pairs={{0,128},{8,136},{16,144},{24,152},{32,160},{40,168},{48,176},{56,1... | collective-permute-start | bytes 221192 | tf_op jit(solution)/shard_map/ppermute | solution.py:400

commit v4 on v3

--- a/solution.py
+++ b/solution.py
@@ -37,7 +37,7 @@
 CORE = row_perm(lambda y, z, c: (y, z, 1 - c))
 YLO = row_perm(lambda y, z, c: (1 - y, z, c))
 ARM = row_perm(lambda y, z, c: (y, z + 1 - 2 * c, c))
-ARM_CROSSED = row_perm(lambda y, z, c: (y, z + 1 - 2 * c, 1 - c))
+ARM_CROSSED = row_perm(lambda y, z, c: (1 - y, z + 1 - 2 * c, c))
 
 
 def exponent(top):
@@ -265,21 +265,14 @@
 
 def last_body(s, q_ref, own_ref, other_ref, *out_refs):
     m, n = own_ref.shape[0], q_ref.shape[1]
-    part = m // 4
-    core = place()[2]
+    half = m // 2
+    ylo = place()[0]
     scale = scale_of(q_ref, m)
     cols = slice(s * n, (s + 1) * n)
     for k, out in enumerate(out_refs):
-        vs = []
-        for y in range(2):
-            start = pl.multiple_of((2 * y + (core ^ k)) * part, part)
-            rows = pl.ds(start, part)
-            vs.append(own_ref[rows, cols] + other_ref[rows, cols] + decoded(q_ref, rows, scale))
-        top = jnp.maximum(jnp.abs(vs[0]), jnp.abs(vs[1]))
-        e = exponent(jnp.max(top, axis=0, keepdims=True))
-        for y in range(2):
-            out[y * part : (y + 1) * part, :] = quantize(vs[y], e)
-        out[2 * part : 2 * part + TAIL, :] = tail(e)
+        rows = pl.ds(pl.multiple_of((ylo ^ k) * half, half), half)
+        v = own_ref[rows, cols] + other_ref[rows, cols] + decoded(q_ref, rows, scale)
+        out[0:half, :], out[half : half + TAIL, :] = encode(v)
 
 
 def last(s, q, own, other):
@@ -290,43 +283,38 @@
 
 
 def near_body(a_ref, b_ref, mine_ref, theirs_ref):
-    part = mine_ref.shape[0] // 2
-    first = jnp.full((part, b_ref.shape[1]), place()[2], jnp.int32) == 0
-    for y in range(2):
-        r = jnp.dot(a_ref[y], b_ref[...], preferred_element_type=jnp.float32)
-        r = r.reshape(-1, 2, 8, r.shape[1])
-        r = [r[:, c].reshape(part, r.shape[3]) for c in range(2)]
-        rows = slice(y * part, (y + 1) * part)
-        mine_ref[rows, :] = jnp.where(first, r[0], r[1])
-        theirs_ref[rows, :] = jnp.where(first, r[1], r[0])
+    half = mine_ref.shape[0]
+    ylo = place()[0]
+    put(mine_ref, 0, jnp.dot(a_ref[ylo], b_ref[...], preferred_element_type=jnp.float32))
+    r = jnp.dot(a_ref[1 - ylo], b_ref[...], preferred_element_type=jnp.float32)
+    r = r.reshape(-1, 2, 8, r.shape[1])
+    v = jnp.concatenate([r[:, c].reshape(half // 2, r.shape[3]) for c in range(2)], axis=0)
+    theirs_ref[0:half, :], theirs_ref[half : half + TAIL, :] = encode(v)
 
 
 def near(a, b):
     m, (k, n) = a.shape[0] * a.shape[1], b.shape
-    outs = [shape((m // 2, n), jnp.float32)] * 2
+    outs = [shape((m // 2, n), jnp.float32), shape((m // 2 + TAIL, n), jnp.int16)]
     return call(near_body, [VMEM] * 2, outs, 2 * m * n * k, 2 * m * k + 4 * m * n)(a, b)
 
 
 def fold_body(s, a_ref, b_ref, mine_ref, other_ref, keep_ref, out_ref):
     part, n = keep_ref.shape
     cols = slice(s * n, (s + 1) * n)
-    ylo = place()[0]
-    scales = [scale_of(r, 2 * part) for r in (a_ref, b_ref)]
-    for k in range(2):
-        y = ylo ^ k
-        rows = pl.ds(pl.multiple_of(y * part, part), part)
-        v = mine_ref[rows, cols] + other_ref[rows, cols]
+    core = place()[2]
+    scales = [scale_of(r, 2 * part) for r in (a_ref, b_ref, other_ref)]
+    scales[2] = scales[2][:, cols]
+    for k, out in enumerate((keep_ref, out_ref)):
+        rows = pl.ds(pl.multiple_of((core ^ k) * part, part), part)
+        v = mine_ref[rows, cols] + other_ref[rows, cols].astype(jnp.int32).astype(jnp.float32) * scales[2]
         for r, scale in zip((a_ref, b_ref), scales):
             v = v + decoded(r, rows, scale)
-        if k == 0:
-            keep_ref[...] = v
-        else:
-            out_ref[0:part, :], out_ref[part : part + TAIL, :] = encode(v)
+        out[...] = v
 
 
 def fold(s, a, b, mine, other):
     part, n = mine.shape[0] // 2, a.shape[1]
-    outs = [shape((part, n), jnp.float32), shape((part + TAIL, n), jnp.int16)]
+    outs = [shape((part, n), jnp.float32)] * 2
     f = call(lambda *r: fold_body(s, *r), [VMEM] * 4, outs, 8 * part * n, 12 * part * n)
     return f(a, b, mine, other)
 
@@ -335,7 +323,7 @@
     *in_refs, out_ref = refs
     m, count, _ = out_ref.shape
     for s in range(count):
-        v = -(in_refs[2 * s][...] + decode(in_refs[2 * s + 1], m))
+        v = -(in_refs[2 * s][...] + in_refs[2 * s + 1][...])
         for i in range(m // rows):
             block = v[i * rows : (i + 1) * rows]
             own = lax.axis_index("col") * (m // rows) + i
@@ -377,7 +365,7 @@
 
     parts = [terms(t) for t in range(1, STEPS + 1)]
     mine, rest = near(ready[1], panels)
-    shared = lax.ppermute(rest, "row", CORE)
+    shared = lax.ppermute(rest, "row", YLO)
     moving = [None] * count
     streams = []
     for t in range(1, STEPS + 1):
@@ -397,7 +385,7 @@
                 straight = lax.ppermute(straight, "row", ARM)
             if t == STEPS:
                 kept, sent = fold(s, straight, crossed, mine, shared)
-                streams.append([kept, lax.ppermute(sent, "row", YLO)])
+                streams.append([kept, lax.ppermute(sent, "row", CORE)])
     out = close(keep, width // 32, streams)
     return out.reshape(local_rows, width // 32, count, width)
 

time: 66.7 us -> 65.9 us (0.988)
  waiting for transfers between devices: 29.3 us -> 26.8 us
  starting transfers between devices: 24.1 us -> 25.8 us
    ppermute x2, waiting for transfers between devices: 3.36 us -> 0.01 us  [per_device(): straight = lax.ppermute(straight, 'row', ARM)]
    ppermute x3, starting transfers between devices: 3.54 us -> 0.95 us  [the longest x1 0.76 us: per_device(): shared = lax.ppermute(rest, 'row', YLO)]
    ppermute x2, starting transfers between devices: 2.14 us -> 4.51 us  [per_device(): crossed = lax.ppermute(crossed, 'row', ARM_CROSSED)]
    ppermute x2, waiting for transfers between devices: 0.01 us -> 2.08 us  [per_device(): crossed = lax.ppermute(crossed, 'row', ARM_CROSSED)]
    ppermute x2, starting transfers between devices: 0.17 us -> 2.09 us  [per_device(): straight = lax.ppermute(straight, 'row', ARM)]
  transfers between devices with their start and end apart: 24 -> 24, of which waited for: 13 -> 12; matrix products, arithmetic and copies ran while one was open for 0% -> 0% of each run, Pallas kernels for 16% -> 16%
where the time goes in v4:
time: 65.9 us; the launch traced here: 65.2 us
  waiting for transfers between devices  26.8 us (41%)
  starting transfers between devices  25.8 us (39%)
  Pallas kernels  12.2 us (19%)
    ppermute x6, waiting for transfers between devices, per_device(): moving[s] = lax.ppermute(coded, 'row', ARM)  16.5 us
    pallas_call x8, Pallas kernels, multiply(): return f(a, b)  5.05 us
    ppermute x3, starting transfers between devices, per_device(): lax.ppermute(factor_panels, 'col', col_perm(*move))  4.76 us
    ppermute x2, starting transfers between devices, per_device(): crossed = lax.ppermute(crossed, 'row', ARM_CROSSED)  4.51 us
    ppermute x6, starting transfers between devices, per_device(): moving[s] = lax.ppermute(coded, 'row', ARM)  4.5 us
    ppermute x3, starting transfers between devices, per_device(): lax.ppermute(across, 'col', col_perm(dx, 0))  4.36 us
    pallas_call x1, Pallas kernels, prepare(): return f(a)  3.65 us
    ppermute x1, starting transfers between devices, per_device(): across = lax.ppermute(factor_panels, 'col', col_perm(0, 1))  3.28 us
  transfers between devices with their start and end apart: 24, of which 12 were waited for; matrix products, arithmetic and copies ran while one was open for 0% of the time, Pallas kernels for 16%

profile of v4, /device:TPU:2, one launch (start us, length us, event | category | flops | bytes accessed | tf_op | source)
XLA Modules:
  0.0 65.2 jit_solution(17052510812360773220)
XLA Ops:
  0.0 3.3 %collective-permute-start = (bf16[2,4,32,256]{3,2,1,0:T(8,128)(2,1)}, bf16[2,4,32,256]{3,2,1,0:T(8,128)(2,1)S(1)}, u32[]{:S(2)}, u32[]{:S(2)}) collective-permute-start(bf16[2,4,32,256]{3,2,1,0:T(8,128)(2,1)} %refs_0_.1), channel_id=1, source_target_pairs={{0,1},{1,0},{2,3},{3,2},{4,5},{5,4},{6,7},{7,6},{8,9},{9,8},{10,11... | collective-permute-start | bytes 393224 | tf_op jit(solution)/shard_map/ppermute | solution.py:351
  3.3 1.5 %collective-permute-start.2 = (bf16[2,4,32,256]{3,2,1,0:T(8,128)(2,1)}, bf16[2,4,32,256]{3,2,1,0:T(8,128)(2,1)S(1)}, u32[]{:S(2)}, u32[]{:S(2)}) collective-permute-start(bf16[2,4,32,256]{3,2,1,0:T(8,128)(2,1)} %refs_0_.1), channel_id=1, source_target_pairs={{0,2},{1,3},{2,4},{3,5},{4,6},{5,7},{6,0},{7,1},{8,10},{9,11},{10,... | collective-permute-start | bytes 393224 | tf_op jit(solution)/shard_map/ppermute | solution.py:353
  4.8 1.1 %collective-permute-start.1 = (bf16[2,4,32,256]{3,2,1,0:T(8,128)(2,1)}, bf16[2,4,32,256]{3,2,1,0:T(8,128)(2,1)S(1)}, u32[]{:S(2)}, u32[]{:S(2)}) collective-permute-start(bf16[2,4,32,256]{3,2,1,0:T(8,128)(2,1)} %refs_0_.1), channel_id=1, source_target_pairs={{0,4},{1,5},{2,6},{3,7},{4,0},{5,1},{6,2},{7,3},{8,12},{9,13},{10,... | collective-permute-start | bytes 393224 | tf_op jit(solution)/shard_map/ppermute | solution.py:353
  5.9 2.2 %collective-permute-start.3 = (bf16[2,4,32,256]{3,2,1,0:T(8,128)(2,1)}, bf16[2,4,32,256]{3,2,1,0:T(8,128)(2,1)S(1)}, u32[]{:S(2)}, u32[]{:S(2)}) collective-permute-start(bf16[2,4,32,256]{3,2,1,0:T(8,128)(2,1)} %refs_0_.1), channel_id=1, source_target_pairs={{0,6},{1,7},{2,0},{3,1},{4,2},{5,3},{6,4},{7,5},{8,14},{9,15},{10,... | collective-permute-start | bytes 393224 | tf_op jit(solution)/shard_map/ppermute | solution.py:353
  8.1 1.4 %collective-permute-start.6 = (bf16[2,4,32,256]{3,2,1,0:T(8,128)(2,1)S(1)}, bf16[2,4,32,256]{3,2,1,0:T(8,128)(2,1)S(1)}, u32[]{:S(2)}, u32[]{:S(2)}) collective-permute-start(bf16[2,4,32,256]{3,2,1,0:T(8,128)(2,1)S(1)} %collective-permute-done.refs_1_), channel_id=1, source_target_pairs={{0,6},{1,7},{2,0},{3,1},{4,2},{5,3},{6,4},{7,5},{8,14},{9,15},{10,... | collective-permute-start | bytes 393224 | tf_op jit(solution)/shard_map/ppermute | solution.py:354
  9.5 0.6 collective-permute-start.5
  10.1 2.3 %collective-permute-start.4 = (bf16[2,4,32,256]{3,2,1,0:T(8,128)(2,1)S(1)}, bf16[2,4,32,256]{3,2,1,0:T(8,128)(2,1)S(1)}, u32[]{:S(2)}, u32[]{:S(2)}) collective-permute-start(bf16[2,4,32,256]{3,2,1,0:T(8,128)(2,1)S(1)} %collective-permute-done.refs_1_), channel_id=1, source_target_pairs={{0,4},{1,5},{2,6},{3,7},{4,0},{5,1},{6,2},{7,3},{8,12},{9,13},{10,... | collective-permute-start | bytes 393224 | tf_op jit(solution)/shard_map/ppermute | solution.py:354
  12.4 3.6 %shard_map.56 = (bf16[2,256,1024]{2,1,0:T(8,128)(2,1)S(1)}, bf16[2,256,1024]{2,1,0:T(8,128)(2,1)S(1)}, bf16[2,256,1024]{2,1,0:T(8,128)(2,1)S(1)}, bf16[2,256,102...) custom-call(bf16[16,2,8,16,4,256]{5,4,3,2,1,0:T(4,128)(2,1)} %bitcast.14), custom_call_target="tpu_custom_call" | custom-call | bytes 16777216 | tf_op jit(solution)/shard_map/pallas_call | solution.py:195
  16.1 0.2 shard_map.55.keep_ref.r_0_
  16.4 0.7 %collective-permute-done.6.refs_7_ = bf16[2,4,32,256]{3,2,1,0:T(8,128)(2,1)S(1)} collective-permute-done((bf16[2,4,32,256]{3,2,1,0:T(8,128)(2,1)S(1)}, bf16[2,4,32,256]{3,2,1,0:T(8,128)(2,1)S(1)}, u32[]{:S(2)}, u32[]{:S(2)}) %collective-permute-start.6) | collective-permute-done | bytes 131104 | tf_op jit(solution)/shard_map/ppermute | solution.py:354
  17.1 2.6 %collective-permute-done.4.refs_5_ = bf16[2,4,32,256]{3,2,1,0:T(8,128)(2,1)S(1)} collective-permute-done((bf16[2,4,32,256]{3,2,1,0:T(8,128)(2,1)S(1)}, bf16[2,4,32,256]{3,2,1,0:T(8,128)(2,1)S(1)}, u32[]{:S(2)}, u32[]{:S(2)}) %collective-permute-start.4) | collective-permute-done | bytes 131104 | tf_op jit(solution)/shard_map/ppermute | solution.py:354
  19.7 0.3 shard_map.57
  19.9 0.7 %shard_map.62 = f32[512,512]{1,0:T(8,128)S(1)} custom-call(bf16[2,256,1024]{2,1,0:T(8,128)(2,1)S(1)} %get-tuple-element.25.refs_0_, bf16[1024,512]{1,0:T(8,128)(2,1)S(1)} %bitcast.4), custom_call_target="tpu_custom_call" | custom-call | flops 536870912 | bytes 2097152 | tf_op jit(solution)/shard_map/pallas_call | solution.py:212
  20.7 0.7 %shard_map.65 = f32[512,512]{1,0:T(8,128)S(1)} custom-call(bf16[2,256,1024]{2,1,0:T(8,128)(2,1)S(1)} %get-tuple-element.27.refs_0_, bf16[1024,512]{1,0:T(8,128)(2,1)S(1)} %bitcast.5), custom_call_target="tpu_custom_call" | custom-call | flops 536870912 | bytes 2097152 | tf_op jit(solution)/shard_map/pallas_call | solution.py:212
  21.4 0.6 collective-permute-start.11
  22.0 0.4 shard_map.59
  22.5 0.7 %shard_map.68 = f32[512,512]{1,0:T(8,128)S(1)} custom-call(bf16[2,256,1024]{2,1,0:T(8,128)(2,1)S(1)} %get-tuple-element.29.refs_0_, bf16[1024,512]{1,0:T(8,128)(2,1)S(1)} %bitcast.7), custom_call_target="tpu_custom_call" | custom-call | flops 536870912 | bytes 2097152 | tf_op jit(solution)/shard_map/pallas_call | solution.py:212
  23.3 0.6 collective-permute-start.13
  23.8 0.4 shard_map.58.r_0_
  24.3 1.3 %collective-permute-done.7.r_1_ = f32[256,512]{1,0:T(8,128)S(1)} collective-permute-done((f32[256,512]{1,0:T(8,128)S(1)}, f32[256,512]{1,0:T(8,128)S(1)}, u32[]{:S(2)}, u32[]{:S(2)}) %collective-permute-start.7) | collective-permute-done | bytes 524320 | tf_op jit(solution)/shard_map/ppermute | solution.py:362
  25.7 2.0 %collective-permute-start.18 = (s16[272,256]{1,0:T(8,128)(2,1)S(1)}, s16[272,256]{1,0:T(8,128)(2,1)S(1)}, u32[]{:S(2)}, u32[]{:S(2)}) collective-permute-start(s16[272,256]{1,0:T(8,128)(2,1)S(1)} %shard_map.72), channel_id=1, source_target_pairs={{0,16},{8,120},{16,32},{24,8},{32,48},{40,24},{48,64},{56,40},{64,... | collective-permute-start | bytes 417800 | tf_op jit(solution)/shard_map/ppermute | solution.py:382
  27.8 2.2 %collective-permute-start.8 = (s16[272,256]{1,0:T(8,128)(2,1)S(1)}, s16[272,256]{1,0:T(8,128)(2,1)S(1)}, u32[]{:S(2)}, u32[]{:S(2)}) collective-permute-start(s16[272,256]{1,0:T(8,128)(2,1)S(1)} %shard_map.60), channel_id=1, source_target_pairs={{0,16},{8,120},{16,32},{24,8},{32,48},{40,24},{48,64},{56,40},{64,... | collective-permute-start | bytes 417800 | tf_op jit(solution)/shard_map/ppermute | solution.py:382
  30.0 0.7 %shard_map.61.r_1_ = f32[512,512]{1,0:T(8,128)S(1)} custom-call(bf16[2,256,1024]{2,1,0:T(8,128)(2,1)S(1)} %get-tuple-element.24.refs_0_, bf16[1024,512]{1,0:T(8,128)(2,1)S(1)} %bitcast.9), custom_call_target="tpu_custom_call" | custom-call | flops 536870912 | bytes 2097152 | tf_op jit(solution)/shard_map/pallas_call | solution.py:212
  30.7 4.0 %collective-permute-done.18.r_0_ = s16[272,256]{1,0:T(8,128)(2,1)S(1)} collective-permute-done((s16[272,256]{1,0:T(8,128)(2,1)S(1)}, s16[272,256]{1,0:T(8,128)(2,1)S(1)}, u32[]{:S(2)}, u32[]{:S(2)}) %collective-permute-start.18) | collective-permute-done | bytes 139296 | tf_op jit(solution)/shard_map/ppermute | solution.py:382
  34.7 0.2 shard_map.73
  34.9 1.2 %collective-permute-done.8.r_0_ = s16[272,256]{1,0:T(8,128)(2,1)S(1)} collective-permute-done((s16[272,256]{1,0:T(8,128)(2,1)S(1)}, s16[272,256]{1,0:T(8,128)(2,1)S(1)}, u32[]{:S(2)}, u32[]{:S(2)}) %collective-permute-start.8) | collective-permute-done | bytes 139296 | tf_op jit(solution)/shard_map/ppermute | solution.py:382
  36.2 0.2 shard_map.63
  36.4 0.7 %shard_map.64.r_1_ = f32[512,512]{1,0:T(8,128)S(1)} custom-call(bf16[2,256,1024]{2,1,0:T(8,128)(2,1)S(1)} %get-tuple-element.26.refs_0_, bf16[1024,512]{1,0:T(8,128)(2,1)S(1)} %bitcast.10), custom_call_target="tpu_custom_call" | custom-call | flops 536870912 | bytes 2097152 | tf_op jit(solution)/shard_map/pallas_call | solution.py:212
  37.2 5.5 %collective-permute-done.19.r_0_ = s16[528,256]{1,0:T(8,128)(2,1)S(1)} collective-permute-done((s16[528,256]{1,0:T(8,128)(2,1)S(1)}, s16[528,256]{1,0:T(8,128)(2,1)S(1)}, u32[]{:S(2)}, u32[]{:S(2)}) %collective-permute-start.19) | collective-permute-done | bytes 270368 | tf_op jit(solution)/shard_map/ppermute | solution.py:382
  42.6 0.2 shard_map.74
  42.9 2.6 %collective-permute-done.10.r_0_ = s16[528,256]{1,0:T(8,128)(2,1)S(1)} collective-permute-done((s16[528,256]{1,0:T(8,128)(2,1)S(1)}, s16[528,256]{1,0:T(8,128)(2,1)S(1)}, u32[]{:S(2)}, u32[]{:S(2)}) %collective-permute-start.10) | collective-permute-done | bytes 270368 | tf_op jit(solution)/shard_map/ppermute | solution.py:382
  45.5 0.2 shard_map.66
  45.8 0.8 %shard_map.70 = (f32[256,512]{1,0:T(8,128)S(1)}, s16[272,512]{1,0:T(8,128)(2,1)S(1)}) custom-call(bf16[2,256,1024]{2,1,0:T(8,128)(2,1)S(1)} %get-tuple-element.32.a_ref, bf16[1024,512]{1,0:T(8,128)(2,1)S(1)} %bitcast.11), custom_call_target="tpu_custom_call" | custom-call | flops 536870912 | bytes 2097152 | tf_op jit(solution)/shard_map/pallas_call | solution.py:298
  46.6 0.8 %collective-permute-start.16 = (s16[272,512]{1,0:T(8,128)(2,1)S(1)}, s16[272,512]{1,0:T(8,128)(2,1)S(1)}, u32[]{:S(2)}, u32[]{:S(2)}) collective-permute-start(s16[272,512]{1,0:T(8,128)(2,1)S(1)} %get-tuple-element.34), channel_id=1, source_target_pairs={{0,128},{8,136},{16,144},{24,152},{32,160},{40,168},{48,176},{56,1... | collective-permute-start | bytes 835592 | tf_op jit(solution)/shard_map/ppermute | solution.py:368
  47.3 0.7 %shard_map.67.r_1_ = f32[512,512]{1,0:T(8,128)S(1)} custom-call(bf16[2,256,1024]{2,1,0:T(8,128)(2,1)S(1)} %get-tuple-element.28.refs_0_, bf16[1024,512]{1,0:T(8,128)(2,1)S(1)} %bitcast.12), custom_call_target="tpu_custom_call" | custom-call | flops 536870912 | bytes 2097152 | tf_op jit(solution)/shard_map/pallas_call | solution.py:212
  48.0 2.5 %collective-permute-done.20.r_0_ = s16[528,256]{1,0:T(8,128)(2,1)S(1)} collective-permute-done((s16[528,256]{1,0:T(8,128)(2,1)S(1)}, s16[528,256]{1,0:T(8,128)(2,1)S(1)}, u32[]{:S(2)}, u32[]{:S(2)}) %collective-permute-start.20) | collective-permute-done | bytes 270368 | tf_op jit(solution)/shard_map/ppermute | solution.py:382
  50.5 0.2 shard_map.75
  50.8 1.9 %collective-permute-start.22 = (s16[272,256]{1,0:T(8,128)(2,1)S(1)}, s16[272,256]{1,0:T(8,128)(2,1)S(1)}, u32[]{:S(2)}, u32[]{:S(2)}) collective-permute-start(s16[272,256]{1,0:T(8,128)(2,1)S(1)} %get-tuple-element.38), channel_id=1, source_target_pairs={{0,144},{8,248},{16,160},{24,136},{32,176},{40,152},{48,192},{56,1... | collective-permute-start | bytes 417800 | tf_op jit(solution)/shard_map/ppermute | solution.py:384
  52.7 0.7 %collective-permute-done.12.r_0_ = s16[528,256]{1,0:T(8,128)(2,1)S(1)} collective-permute-done((s16[528,256]{1,0:T(8,128)(2,1)S(1)}, s16[528,256]{1,0:T(8,128)(2,1)S(1)}, u32[]{:S(2)}, u32[]{:S(2)}) %collective-permute-start.12) | collective-permute-done | bytes 270368 | tf_op jit(solution)/shard_map/ppermute | solution.py:382
  53.4 0.2 shard_map.69
  53.6 2.0 %collective-permute-start.14 = (s16[272,256]{1,0:T(8,128)(2,1)S(1)}, s16[272,256]{1,0:T(8,128)(2,1)S(1)}, u32[]{:S(2)}, u32[]{:S(2)}) collective-permute-start(s16[272,256]{1,0:T(8,128)(2,1)S(1)} %get-tuple-element.30), channel_id=1, source_target_pairs={{0,16},{8,120},{16,32},{24,8},{32,48},{40,24},{48,64},{56,40},{64,... | collective-permute-start | bytes 417800 | tf_op jit(solution)/shard_map/ppermute | solution.py:385
  55.6 2.6 %collective-permute-start.15 = (s16[272,256]{1,0:T(8,128)(2,1)S(1)}, s16[272,256]{1,0:T(8,128)(2,1)S(1)}, u32[]{:S(2)}, u32[]{:S(2)}) collective-permute-start(s16[272,256]{1,0:T(8,128)(2,1)S(1)} %get-tuple-element.31), channel_id=1, source_target_pairs={{0,144},{8,248},{16,160},{24,136},{32,176},{40,152},{48,192},{56,1... | collective-permute-start | bytes 417800 | tf_op jit(solution)/shard_map/ppermute | solution.py:384
  58.2 2.2 %collective-permute-done.16.r_3_ = s16[272,512]{1,0:T(8,128)(2,1)S(1)} collective-permute-done((s16[272,512]{1,0:T(8,128)(2,1)S(1)}, s16[272,512]{1,0:T(8,128)(2,1)S(1)}, u32[]{:S(2)}, u32[]{:S(2)}) %collective-permute-start.16) | collective-permute-done | bytes 278560 | tf_op jit(solution)/shard_map/ppermute | solution.py:368
  60.5 0.1 shard_map.76
  60.7 2.1 %collective-permute-done.15.r_1_ = s16[272,256]{1,0:T(8,128)(2,1)S(1)} collective-permute-done((s16[272,256]{1,0:T(8,128)(2,1)S(1)}, s16[272,256]{1,0:T(8,128)(2,1)S(1)}, u32[]{:S(2)}, u32[]{:S(2)}) %collective-permute-start.15) | collective-permute-done | bytes 139296 | tf_op jit(solution)/shard_map/ppermute | solution.py:384
  62.8 0.1 shard_map.71
  63.0 1.3 %collective-permute-done.17.r_2_ = f32[128,256]{1,0:T(8,128)S(1)} collective-permute-done((f32[128,256]{1,0:T(8,128)S(1)}, f32[128,256]{1,0:T(8,128)S(1)}, u32[]{:S(2)}, u32[]{:S(2)}) %collective-permute-start.17) | collective-permute-done | bytes 131104 | tf_op jit(solution)/shard_map/ppermute | solution.py:388
  64.3 0.8 %shard_map.77 = f32[128,2,256]{2,1,0:T(2,128)} custom-call(f32[2,128,256]{2,1,0:T(8,128)S(1)} %shard_map.55.keep_ref.r_0_, f32[128,256]{1,0:T(8,128)S(1)} %get-tuple-element.35.r_1_, f32[128,256]{1,0:T(8,128)S(1)} %collective-permute-done.17.r_2_, f32[128,256]{1,0:T(8,128)S(1)} %get-tuple-element.39.r_3_, f32[128,256]{1,0:T(8,128)S(1)} %collective-permute-done.23.r_4_), custom_call_target="tpu_custom_call" | custom-call | flops 524288 | bytes 917504 | tf_op jit(solution)/shard_map/pallas_call | solution.py:344
  (31 shorter events, 1.0 us)
Async XLA Ops:
  0.0 19.7 %copy-start = (bf16[2,4,32,256]{3,2,1,0:T(8,128)(2,1)S(1)}, bf16[2,4,32,256]{3,2,1,0:T(8,128)(2,1)}, u32[]{:S(2)}) copy-start(bf16[2,4,32,256]{3,2,1,0:T(8,128)(2,1)} %refs_0_.1) | copy-start | bytes 393220
  0.0 16.1 %copy-start.3 = (s32[128]{0:T(128)S(1)}, s32[128]{0:T(128)}, u32[]{:S(2)}) copy-start(s32[128]{0:T(128)} %param.9) | copy-start | bytes 1540
  0.0 16.1 %copy-start.2 = (s32[2,96]{1,0:T(2,128)S(1)}, s32[2,96]{1,0:T(2,128)}, u32[]{:S(2)}) copy-start(s32[2,96]{1,0:T(2,128)} %flags_ref.1) | copy-start | bytes 2308
  0.0 16.1 %copy-start.1 = (s32[2,96]{1,0:T(2,128)S(1)}, s32[2,96]{1,0:T(2,128)}, u32[]{:S(2)}) copy-start(s32[2,96]{1,0:T(2,128)} %ancestors_ref.1) | copy-start | bytes 2308
  0.0 8.0 %collective-permute-start = (bf16[2,4,32,256]{3,2,1,0:T(8,128)(2,1)}, bf16[2,4,32,256]{3,2,1,0:T(8,128)(2,1)S(1)}, u32[]{:S(2)}, u32[]{:S(2)}) collective-permute-start(bf16[2,4,32,256]{3,2,1,0:T(8,128)(2,1)} %refs_0_.1), channel_id=1, source_target_pairs={{0,1},{1,0},{2,3},{3,2},{4,5},{5,4},{6,7},{7,6},{8,9},{9,8},{10,11... | collective-permute-start | bytes 393224 | tf_op jit(solution)/shard_map/ppermute | solution.py:351
  3.3 6.8 %collective-permute-start.2 = (bf16[2,4,32,256]{3,2,1,0:T(8,128)(2,1)}, bf16[2,4,32,256]{3,2,1,0:T(8,128)(2,1)S(1)}, u32[]{:S(2)}, u32[]{:S(2)}) collective-permute-start(bf16[2,4,32,256]{3,2,1,0:T(8,128)(2,1)} %refs_0_.1), channel_id=1, source_target_pairs={{0,2},{1,3},{2,4},{3,5},{4,6},{5,7},{6,0},{7,1},{8,10},{9,11},{10,... | collective-permute-start | bytes 393224 | tf_op jit(solution)/shard_map/ppermute | solution.py:353
  4.8 11.6 %collective-permute-start.1 = (bf16[2,4,32,256]{3,2,1,0:T(8,128)(2,1)}, bf16[2,4,32,256]{3,2,1,0:T(8,128)(2,1)S(1)}, u32[]{:S(2)}, u32[]{:S(2)}) collective-permute-start(bf16[2,4,32,256]{3,2,1,0:T(8,128)(2,1)} %refs_0_.1), channel_id=1, source_target_pairs={{0,4},{1,5},{2,6},{3,7},{4,0},{5,1},{6,2},{7,3},{8,12},{9,13},{10,... | collective-permute-start | bytes 393224 | tf_op jit(solution)/shard_map/ppermute | solution.py:353
  5.9 10.5 %collective-permute-start.3 = (bf16[2,4,32,256]{3,2,1,0:T(8,128)(2,1)}, bf16[2,4,32,256]{3,2,1,0:T(8,128)(2,1)S(1)}, u32[]{:S(2)}, u32[]{:S(2)}) collective-permute-start(bf16[2,4,32,256]{3,2,1,0:T(8,128)(2,1)} %refs_0_.1), channel_id=1, source_target_pairs={{0,6},{1,7},{2,0},{3,1},{4,2},{5,3},{6,4},{7,5},{8,14},{9,15},{10,... | collective-permute-start | bytes 393224 | tf_op jit(solution)/shard_map/ppermute | solution.py:353
  8.1 9.0 %collective-permute-start.6 = (bf16[2,4,32,256]{3,2,1,0:T(8,128)(2,1)S(1)}, bf16[2,4,32,256]{3,2,1,0:T(8,128)(2,1)S(1)}, u32[]{:S(2)}, u32[]{:S(2)}) collective-permute-start(bf16[2,4,32,256]{3,2,1,0:T(8,128)(2,1)S(1)} %collective-permute-done.refs_1_), channel_id=1, source_target_pairs={{0,6},{1,7},{2,0},{3,1},{4,2},{5,3},{6,4},{7,5},{8,14},{9,15},{10,... | collective-permute-start | bytes 393224 | tf_op jit(solution)/shard_map/ppermute | solution.py:354
  9.5 7.6 %collective-permute-start.5 = (bf16[2,4,32,256]{3,2,1,0:T(8,128)(2,1)S(1)}, bf16[2,4,32,256]{3,2,1,0:T(8,128)(2,1)S(1)}, u32[]{:S(2)}, u32[]{:S(2)}) collective-permute-start(bf16[2,4,32,256]{3,2,1,0:T(8,128)(2,1)S(1)} %collective-permute-done.refs_1_), channel_id=1, source_target_pairs={{0,2},{1,3},{2,4},{3,5},{4,6},{5,7},{6,0},{7,1},{8,10},{9,11},{10,... | collective-permute-start | bytes 393224 | tf_op jit(solution)/shard_map/ppermute | solution.py:354
  10.1 9.6 %collective-permute-start.4 = (bf16[2,4,32,256]{3,2,1,0:T(8,128)(2,1)S(1)}, bf16[2,4,32,256]{3,2,1,0:T(8,128)(2,1)S(1)}, u32[]{:S(2)}, u32[]{:S(2)}) collective-permute-start(bf16[2,4,32,256]{3,2,1,0:T(8,128)(2,1)S(1)} %collective-permute-done.refs_1_), channel_id=1, source_target_pairs={{0,4},{1,5},{2,6},{3,7},{4,0},{5,1},{6,2},{7,3},{8,12},{9,13},{10,... | collective-permute-start | bytes 393224 | tf_op jit(solution)/shard_map/ppermute | solution.py:354
  20.6 14.1 %collective-permute-start.9 = (f32[512,512]{1,0:T(8,128)S(1)}, f32[512,512]{1,0:T(8,128)S(1)}, u32[]{:S(2)}, u32[]{:S(2)}) collective-permute-start(f32[512,512]{1,0:T(8,128)S(1)} %shard_map.62), channel_id=1, source_target_pairs={{0,8},{8,0},{16,24},{24,16},{32,40},{40,32},{48,56},{56,48},{64,72... | collective-permute-start | bytes 3145736 | tf_op jit(solution)/shard_map/ppermute | solution.py:362
  21.4 15.7 %collective-permute-start.11 = (f32[512,512]{1,0:T(8,128)S(1)}, f32[512,512]{1,0:T(8,128)S(1)}, u32[]{:S(2)}, u32[]{:S(2)}) collective-permute-start(f32[512,512]{1,0:T(8,128)S(1)} %shard_map.65), channel_id=1, source_target_pairs={{0,8},{8,0},{16,24},{24,16},{32,40},{40,32},{48,56},{56,48},{64,72... | collective-permute-start | bytes 3145736 | tf_op jit(solution)/shard_map/ppermute | solution.py:362
  22.4 3.2 %collective-permute-start.7 = (f32[256,512]{1,0:T(8,128)S(1)}, f32[256,512]{1,0:T(8,128)S(1)}, u32[]{:S(2)}, u32[]{:S(2)}) collective-permute-start(f32[256,512]{1,0:T(8,128)S(1)} %shard_map.59), channel_id=1, source_target_pairs={{0,8},{8,0},{16,24},{24,16},{32,40},{40,32},{48,56},{56,48},{64,72... | collective-permute-start | bytes 1572872 | tf_op jit(solution)/shard_map/ppermute | solution.py:362
  23.3 24.8 %collective-permute-start.13 = (f32[512,512]{1,0:T(8,128)S(1)}, f32[512,512]{1,0:T(8,128)S(1)}, u32[]{:S(2)}, u32[]{:S(2)}) collective-permute-start(f32[512,512]{1,0:T(8,128)S(1)} %shard_map.68), channel_id=1, source_target_pairs={{0,8},{8,0},{16,24},{24,16},{32,40},{40,32},{48,56},{56,48},{64,72... | collective-permute-start | bytes 3145736 | tf_op jit(solution)/shard_map/ppermute | solution.py:362
  25.7 9.0 %collective-permute-start.18 = (s16[272,256]{1,0:T(8,128)(2,1)S(1)}, s16[272,256]{1,0:T(8,128)(2,1)S(1)}, u32[]{:S(2)}, u32[]{:S(2)}) collective-permute-start(s16[272,256]{1,0:T(8,128)(2,1)S(1)} %shard_map.72), channel_id=1, source_target_pairs={{0,16},{8,120},{16,32},{24,8},{32,48},{40,24},{48,64},{56,40},{64,... | collective-permute-start | bytes 417800 | tf_op jit(solution)/shard_map/ppermute | solution.py:382
  27.8 8.4 %collective-permute-start.8 = (s16[272,256]{1,0:T(8,128)(2,1)S(1)}, s16[272,256]{1,0:T(8,128)(2,1)S(1)}, u32[]{:S(2)}, u32[]{:S(2)}) collective-permute-start(s16[272,256]{1,0:T(8,128)(2,1)S(1)} %shard_map.60), channel_id=1, source_target_pairs={{0,16},{8,120},{16,32},{24,8},{32,48},{40,24},{48,64},{56,40},{64,... | collective-permute-start | bytes 417800 | tf_op jit(solution)/shard_map/ppermute | solution.py:382
  34.9 7.7 %collective-permute-start.19 = (s16[528,256]{1,0:T(8,128)(2,1)S(1)}, s16[528,256]{1,0:T(8,128)(2,1)S(1)}, u32[]{:S(2)}, u32[]{:S(2)}) collective-permute-start(s16[528,256]{1,0:T(8,128)(2,1)S(1)} %shard_map.73), channel_id=1, source_target_pairs={{0,16},{8,120},{16,32},{24,8},{32,48},{40,24},{48,64},{56,40},{64,... | collective-permute-start | bytes 811016 | tf_op jit(solution)/shard_map/ppermute | solution.py:382
  36.3 9.2 %collective-permute-start.10 = (s16[528,256]{1,0:T(8,128)(2,1)S(1)}, s16[528,256]{1,0:T(8,128)(2,1)S(1)}, u32[]{:S(2)}, u32[]{:S(2)}) collective-permute-start(s16[528,256]{1,0:T(8,128)(2,1)S(1)} %shard_map.63), channel_id=1, source_target_pairs={{0,16},{8,120},{16,32},{24,8},{32,48},{40,24},{48,64},{56,40},{64,... | collective-permute-start | bytes 811016 | tf_op jit(solution)/shard_map/ppermute | solution.py:382
  42.8 7.7 %collective-permute-start.20 = (s16[528,256]{1,0:T(8,128)(2,1)S(1)}, s16[528,256]{1,0:T(8,128)(2,1)S(1)}, u32[]{:S(2)}, u32[]{:S(2)}) collective-permute-start(s16[528,256]{1,0:T(8,128)(2,1)S(1)} %shard_map.74), channel_id=1, source_target_pairs={{0,16},{8,120},{16,32},{24,8},{32,48},{40,24},{48,64},{56,40},{64,... | collective-permute-start | bytes 811016 | tf_op jit(solution)/shard_map/ppermute | solution.py:382
  45.7 7.7 %collective-permute-start.12 = (s16[528,256]{1,0:T(8,128)(2,1)S(1)}, s16[528,256]{1,0:T(8,128)(2,1)S(1)}, u32[]{:S(2)}, u32[]{:S(2)}) collective-permute-start(s16[528,256]{1,0:T(8,128)(2,1)S(1)} %shard_map.66), channel_id=1, source_target_pairs={{0,16},{8,120},{16,32},{24,8},{32,48},{40,24},{48,64},{56,40},{64,... | collective-permute-start | bytes 811016 | tf_op jit(solution)/shard_map/ppermute | solution.py:382
  46.6 13.9 %collective-permute-start.16 = (s16[272,512]{1,0:T(8,128)(2,1)S(1)}, s16[272,512]{1,0:T(8,128)(2,1)S(1)}, u32[]{:S(2)}, u32[]{:S(2)}) collective-permute-start(s16[272,512]{1,0:T(8,128)(2,1)S(1)} %get-tuple-element.34), channel_id=1, source_target_pairs={{0,128},{8,136},{16,144},{24,152},{32,160},{40,168},{48,176},{56,1... | collective-permute-start | bytes 835592 | tf_op jit(solution)/shard_map/ppermute | solution.py:368
  50.7 9.7 %collective-permute-start.21 = (s16[272,256]{1,0:T(8,128)(2,1)S(1)}, s16[272,256]{1,0:T(8,128)(2,1)S(1)}, u32[]{:S(2)}, u32[]{:S(2)}) collective-permute-start(s16[272,256]{1,0:T(8,128)(2,1)S(1)} %get-tuple-element.37), channel_id=1, source_target_pairs={{0,16},{8,120},{16,32},{24,8},{32,48},{40,24},{48,64},{56,40},{64,... | collective-permute-start | bytes 417800 | tf_op jit(solution)/shard_map/ppermute | solution.py:385
  50.8 9.7 %collective-permute-start.22 = (s16[272,256]{1,0:T(8,128)(2,1)S(1)}, s16[272,256]{1,0:T(8,128)(2,1)S(1)}, u32[]{:S(2)}, u32[]{:S(2)}) collective-permute-start(s16[272,256]{1,0:T(8,128)(2,1)S(1)} %get-tuple-element.38), channel_id=1, source_target_pairs={{0,144},{8,248},{16,160},{24,136},{32,176},{40,152},{48,192},{56,1... | collective-permute-start | bytes 417800 | tf_op jit(solution)/shard_map/ppermute | solution.py:384
  53.6 7.1 %collective-permute-start.14 = (s16[272,256]{1,0:T(8,128)(2,1)S(1)}, s16[272,256]{1,0:T(8,128)(2,1)S(1)}, u32[]{:S(2)}, u32[]{:S(2)}) collective-permute-start(s16[272,256]{1,0:T(8,128)(2,1)S(1)} %get-tuple-element.30), channel_id=1, source_target_pairs={{0,16},{8,120},{16,32},{24,8},{32,48},{40,24},{48,64},{56,40},{64,... | collective-permute-start | bytes 417800 | tf_op jit(solution)/shard_map/ppermute | solution.py:385
  55.6 7.2 %collective-permute-start.15 = (s16[272,256]{1,0:T(8,128)(2,1)S(1)}, s16[272,256]{1,0:T(8,128)(2,1)S(1)}, u32[]{:S(2)}, u32[]{:S(2)}) collective-permute-start(s16[272,256]{1,0:T(8,128)(2,1)S(1)} %get-tuple-element.31), channel_id=1, source_target_pairs={{0,144},{8,248},{16,160},{24,136},{32,176},{40,152},{48,192},{56,1... | collective-permute-start | bytes 417800 | tf_op jit(solution)/shard_map/ppermute | solution.py:384
  60.6 2.4 %collective-permute-start.23 = (f32[128,256]{1,0:T(8,128)S(1)}, f32[128,256]{1,0:T(8,128)S(1)}, u32[]{:S(2)}, u32[]{:S(2)}) collective-permute-start(f32[128,256]{1,0:T(8,128)S(1)} %get-tuple-element.40), channel_id=1, source_target_pairs={{0,8},{8,0},{16,24},{24,16},{32,40},{40,32},{48,56},{56,48},{64,72... | collective-permute-start | bytes 393224 | tf_op jit(solution)/shard_map/ppermute | solution.py:388
  62.9 1.4 %collective-permute-start.17 = (f32[128,256]{1,0:T(8,128)S(1)}, f32[128,256]{1,0:T(8,128)S(1)}, u32[]{:S(2)}, u32[]{:S(2)}) collective-permute-start(f32[128,256]{1,0:T(8,128)S(1)} %get-tuple-element.36), channel_id=1, source_target_pairs={{0,8},{8,0},{16,24},{24,16},{32,40},{40,32},{48,56},{56,48},{64,72... | collective-permute-start | bytes 393224 | tf_op jit(solution)/shard_map/ppermute | solution.py:388

commit v5 on v4

--- a/solution.py
+++ b/solution.py
@@ -349,9 +349,12 @@
     count = factor_panels.shape[0]
 
     across = lax.ppermute(factor_panels, "col", col_perm(0, 1))
-    pieces = [factor_panels, across]
-    pieces += [lax.ppermute(factor_panels, "col", col_perm(*move)) for move in MOVES[2:5]]
-    pieces += [lax.ppermute(across, "col", col_perm(dx, 0)) for dx, _ in MOVES[5:8]]
+    one, three = [lax.ppermute(factor_panels, "col", col_perm(dx, 0)) for dx in (1, 3)]
+    onward = []
+    for dx, _ in MOVES[5:8]:
+        onward.append(lax.ppermute(across, "col", col_perm(dx, 0)))
+    two = lax.ppermute(three, "col", col_perm(3, 0))
+    pieces = [factor_panels, across, two, one, three] + onward
     keep = members(ancestors, valid_flags, block_slot, width)
     panels = assemble(keep, pieces)
 

time: 65.9 us -> 65.6 us (level)
  the two profiles are of different devices: /device:TPU:2 before, /device:TPU:1 now
where the time goes in v5:
time: 65.6 us; the launch traced here: 65.5 us
  starting transfers between devices  40.9 us (62%)
  Pallas kernels  12.2 us (19%)
  waiting for transfers between devices  12.1 us (18%)
    ppermute x6, starting transfers between devices, per_device(): moving[s] = lax.ppermute(coded, 'row', ARM)  17.1 us
    ppermute x1, waiting for transfers between devices, per_device(): shared = lax.ppermute(rest, 'row', YLO)  5.99 us
    pallas_call x8, Pallas kernels, multiply(): return f(a, b)  5.04 us
    ppermute x4, starting transfers between devices, terms(): other = lax.ppermute(theirs, 'row', CORE)  3.77 us
    pallas_call x1, Pallas kernels, prepare(): return f(a)  3.65 us
    ppermute x2, starting transfers between devices, per_device(): lax.ppermute(factor_panels, 'col', col_perm(dx, 0))  3.38 us
    ppermute x1, starting transfers between devices, per_device(): across = lax.ppermute(factor_panels, 'col', col_perm(0, 1))  2.91 us
    ppermute x1, starting transfers between devices, per_device(): two = lax.ppermute(three, 'col', col_perm(3, 0))  2.88 us
  transfers between devices with their start and end apart: 24, of which 7 were waited for; matrix products, arithmetic and copies ran while one was open for 0% of the time, Pallas kernels for 16%

profile of v5, /device:TPU:1, one launch (start us, length us, event | category | flops | bytes accessed | tf_op | source)
XLA Modules:
  0.0 65.5 jit_solution(6966172869923453529)
XLA Ops:
  0.0 3.4 %collective-permute-start.1 = (bf16[2,4,32,256]{3,2,1,0:T(8,128)(2,1)}, bf16[2,4,32,256]{3,2,1,0:T(8,128)(2,1)S(1)}, u32[]{:S(2)}, u32[]{:S(2)}) collective-permute-start(bf16[2,4,32,256]{3,2,1,0:T(8,128)(2,1)} %refs_0_.1), channel_id=1, source_target_pairs={{0,6},{1,7},{2,0},{3,1},{4,2},{5,3},{6,4},{7,5},{8,14},{9,15},{10,... | collective-permute-start | bytes 393224 | tf_op jit(solution)/shard_map/ppermute | solution.py:352
  3.4 2.9 %collective-permute-start = (bf16[2,4,32,256]{3,2,1,0:T(8,128)(2,1)}, bf16[2,4,32,256]{3,2,1,0:T(8,128)(2,1)S(1)}, u32[]{:S(2)}, u32[]{:S(2)}) collective-permute-start(bf16[2,4,32,256]{3,2,1,0:T(8,128)(2,1)} %refs_0_.1), channel_id=1, source_target_pairs={{0,1},{1,0},{2,3},{3,2},{4,5},{5,4},{6,7},{7,6},{8,9},{9,8},{10,11... | collective-permute-start | bytes 393224 | tf_op jit(solution)/shard_map/ppermute | solution.py:351
  6.3 2.9 %collective-permute-start.2 = (bf16[2,4,32,256]{3,2,1,0:T(8,128)(2,1)S(1)}, bf16[2,4,32,256]{3,2,1,0:T(8,128)(2,1)S(1)}, u32[]{:S(2)}, u32[]{:S(2)}) collective-permute-start(bf16[2,4,32,256]{3,2,1,0:T(8,128)(2,1)S(1)} %collective-permute-done.1.refs_4_), channel_id=1, source_target_pairs={{0,6},{1,7},{2,0},{3,1},{4,2},{5,3},{6,4},{7,5},{8,14},{9,15},{10,... | collective-permute-start | bytes 393224 | tf_op jit(solution)/shard_map/ppermute | solution.py:356
  9.2 0.5 collective-permute-start.6
  9.8 0.9 %collective-permute-start.5 = (bf16[2,4,32,256]{3,2,1,0:T(8,128)(2,1)S(1)}, bf16[2,4,32,256]{3,2,1,0:T(8,128)(2,1)S(1)}, u32[]{:S(2)}, u32[]{:S(2)}) collective-permute-start(bf16[2,4,32,256]{3,2,1,0:T(8,128)(2,1)S(1)} %collective-permute-done.refs_1_), channel_id=1, source_target_pairs={{0,2},{1,3},{2,4},{3,5},{4,6},{5,7},{6,0},{7,1},{8,10},{9,11},{10,... | collective-permute-start | bytes 393224 | tf_op jit(solution)/shard_map/ppermute | solution.py:355
  10.7 0.5 collective-permute-start.4
  11.2 3.6 %shard_map.56 = (bf16[2,256,1024]{2,1,0:T(8,128)(2,1)S(1)}, bf16[2,256,1024]{2,1,0:T(8,128)(2,1)S(1)}, bf16[2,256,1024]{2,1,0:T(8,128)(2,1)S(1)}, bf16[2,256,102...) custom-call(bf16[16,2,8,16,4,256]{5,4,3,2,1,0:T(4,128)(2,1)} %bitcast.14), custom_call_target="tpu_custom_call" | custom-call | bytes 16777216 | tf_op jit(solution)/shard_map/pallas_call | solution.py:195
  14.9 0.2 shard_map.55.keep_ref.r_0_
  15.3 1.9 %collective-permute-done.4.refs_5_ = bf16[2,4,32,256]{3,2,1,0:T(8,128)(2,1)S(1)} collective-permute-done((bf16[2,4,32,256]{3,2,1,0:T(8,128)(2,1)S(1)}, bf16[2,4,32,256]{3,2,1,0:T(8,128)(2,1)S(1)}, u32[]{:S(2)}, u32[]{:S(2)}) %collective-permute-start.4) | collective-permute-done | bytes 131104 | tf_op jit(solution)/shard_map/ppermute | solution.py:355
  17.2 0.3 shard_map.57
  17.4 0.7 %shard_map.62 = f32[512,512]{1,0:T(8,128)S(1)} custom-call(bf16[2,256,1024]{2,1,0:T(8,128)(2,1)S(1)} %get-tuple-element.25.refs_0_, bf16[1024,512]{1,0:T(8,128)(2,1)S(1)} %bitcast.4), custom_call_target="tpu_custom_call" | custom-call | flops 536870912 | bytes 2097152 | tf_op jit(solution)/shard_map/pallas_call | solution.py:212
  18.1 3.0 %collective-permute-start.9 = (f32[512,512]{1,0:T(8,128)S(1)}, f32[512,512]{1,0:T(8,128)S(1)}, u32[]{:S(2)}, u32[]{:S(2)}) collective-permute-start(f32[512,512]{1,0:T(8,128)S(1)} %shard_map.62), channel_id=1, source_target_pairs={{0,8},{8,0},{16,24},{24,16},{32,40},{40,32},{48,56},{56,48},{64,72... | collective-permute-start | bytes 3145736 | tf_op jit(solution)/shard_map/ppermute | solution.py:365
  21.1 0.7 %shard_map.65 = f32[512,512]{1,0:T(8,128)S(1)} custom-call(bf16[2,256,1024]{2,1,0:T(8,128)(2,1)S(1)} %get-tuple-element.27.refs_0_, bf16[1024,512]{1,0:T(8,128)(2,1)S(1)} %bitcast.5), custom_call_target="tpu_custom_call" | custom-call | flops 536870912 | bytes 2097152 | tf_op jit(solution)/shard_map/pallas_call | solution.py:212
  21.9 0.4 shard_map.59
  22.4 0.6 collective-permute-start.7
  22.9 0.7 %shard_map.68 = f32[512,512]{1,0:T(8,128)S(1)} custom-call(bf16[2,256,1024]{2,1,0:T(8,128)(2,1)S(1)} %get-tuple-element.29.refs_0_, bf16[1024,512]{1,0:T(8,128)(2,1)S(1)} %bitcast.7), custom_call_target="tpu_custom_call" | custom-call | flops 536870912 | bytes 2097152 | tf_op jit(solution)/shard_map/pallas_call | solution.py:212
  23.7 0.4 shard_map.58.r_0_
  24.2 1.5 %collective-permute-done.7.r_1_ = f32[256,512]{1,0:T(8,128)S(1)} collective-permute-done((f32[256,512]{1,0:T(8,128)S(1)}, f32[256,512]{1,0:T(8,128)S(1)}, u32[]{:S(2)}, u32[]{:S(2)}) %collective-permute-start.7) | collective-permute-done | bytes 524320 | tf_op jit(solution)/shard_map/ppermute | solution.py:365
  25.7 5.9 %collective-permute-start.18 = (s16[272,256]{1,0:T(8,128)(2,1)S(1)}, s16[272,256]{1,0:T(8,128)(2,1)S(1)}, u32[]{:S(2)}, u32[]{:S(2)}) collective-permute-start(s16[272,256]{1,0:T(8,128)(2,1)S(1)} %shard_map.72), channel_id=1, source_target_pairs={{0,16},{8,120},{16,32},{24,8},{32,48},{40,24},{48,64},{56,40},{64,... | collective-permute-start | bytes 417800 | tf_op jit(solution)/shard_map/ppermute | solution.py:385
  31.8 0.8 %collective-permute-start.8 = (s16[272,256]{1,0:T(8,128)(2,1)S(1)}, s16[272,256]{1,0:T(8,128)(2,1)S(1)}, u32[]{:S(2)}, u32[]{:S(2)}) collective-permute-start(s16[272,256]{1,0:T(8,128)(2,1)S(1)} %shard_map.60), channel_id=1, source_target_pairs={{0,16},{8,120},{16,32},{24,8},{32,48},{40,24},{48,64},{56,40},{64,... | collective-permute-start | bytes 417800 | tf_op jit(solution)/shard_map/ppermute | solution.py:385
  32.6 0.7 %shard_map.61.r_1_ = f32[512,512]{1,0:T(8,128)S(1)} custom-call(bf16[2,256,1024]{2,1,0:T(8,128)(2,1)S(1)} %get-tuple-element.24.refs_0_, bf16[1024,512]{1,0:T(8,128)(2,1)S(1)} %bitcast.9), custom_call_target="tpu_custom_call" | custom-call | flops 536870912 | bytes 2097152 | tf_op jit(solution)/shard_map/pallas_call | solution.py:212
  33.3 0.4 collective-permute-done.18.r_0_
  33.7 0.2 shard_map.73
  33.9 3.2 %collective-permute-start.19 = (s16[528,256]{1,0:T(8,128)(2,1)S(1)}, s16[528,256]{1,0:T(8,128)(2,1)S(1)}, u32[]{:S(2)}, u32[]{:S(2)}) collective-permute-start(s16[528,256]{1,0:T(8,128)(2,1)S(1)} %shard_map.73), channel_id=1, source_target_pairs={{0,16},{8,120},{16,32},{24,8},{32,48},{40,24},{48,64},{56,40},{64,... | collective-permute-start | bytes 811016 | tf_op jit(solution)/shard_map/ppermute | solution.py:385
  37.0 0.2 shard_map.63
  37.2 1.3 %collective-permute-start.10 = (s16[528,256]{1,0:T(8,128)(2,1)S(1)}, s16[528,256]{1,0:T(8,128)(2,1)S(1)}, u32[]{:S(2)}, u32[]{:S(2)}) collective-permute-start(s16[528,256]{1,0:T(8,128)(2,1)S(1)} %shard_map.63), channel_id=1, source_target_pairs={{0,16},{8,120},{16,32},{24,8},{32,48},{40,24},{48,64},{56,40},{64,... | collective-permute-start | bytes 811016 | tf_op jit(solution)/shard_map/ppermute | solution.py:385
  38.5 0.7 %shard_map.64.r_1_ = f32[512,512]{1,0:T(8,128)S(1)} custom-call(bf16[2,256,1024]{2,1,0:T(8,128)(2,1)S(1)} %get-tuple-element.26.refs_0_, bf16[1024,512]{1,0:T(8,128)(2,1)S(1)} %bitcast.10), custom_call_target="tpu_custom_call" | custom-call | flops 536870912 | bytes 2097152 | tf_op jit(solution)/shard_map/pallas_call | solution.py:212
  39.2 1.2 %collective-permute-done.19.r_0_ = s16[528,256]{1,0:T(8,128)(2,1)S(1)} collective-permute-done((s16[528,256]{1,0:T(8,128)(2,1)S(1)}, s16[528,256]{1,0:T(8,128)(2,1)S(1)}, u32[]{:S(2)}, u32[]{:S(2)}) %collective-permute-start.19) | collective-permute-done | bytes 270368 | tf_op jit(solution)/shard_map/ppermute | solution.py:385
  40.4 0.2 shard_map.74
  40.6 3.2 %collective-permute-start.20 = (s16[528,256]{1,0:T(8,128)(2,1)S(1)}, s16[528,256]{1,0:T(8,128)(2,1)S(1)}, u32[]{:S(2)}, u32[]{:S(2)}) collective-permute-start(s16[528,256]{1,0:T(8,128)(2,1)S(1)} %shard_map.74), channel_id=1, source_target_pairs={{0,16},{8,120},{16,32},{24,8},{32,48},{40,24},{48,64},{56,40},{64,... | collective-permute-start | bytes 811016 | tf_op jit(solution)/shard_map/ppermute | solution.py:385
  43.8 0.2 shard_map.66
  44.0 2.7 %collective-permute-start.12 = (s16[528,256]{1,0:T(8,128)(2,1)S(1)}, s16[528,256]{1,0:T(8,128)(2,1)S(1)}, u32[]{:S(2)}, u32[]{:S(2)}) collective-permute-start(s16[528,256]{1,0:T(8,128)(2,1)S(1)} %shard_map.66), channel_id=1, source_target_pairs={{0,16},{8,120},{16,32},{24,8},{32,48},{40,24},{48,64},{56,40},{64,... | collective-permute-start | bytes 811016 | tf_op jit(solution)/shard_map/ppermute | solution.py:385
  46.7 0.8 %shard_map.70 = (f32[256,512]{1,0:T(8,128)S(1)}, s16[272,512]{1,0:T(8,128)(2,1)S(1)}) custom-call(bf16[2,256,1024]{2,1,0:T(8,128)(2,1)S(1)} %get-tuple-element.32.a_ref, bf16[1024,512]{1,0:T(8,128)(2,1)S(1)} %bitcast.11), custom_call_target="tpu_custom_call" | custom-call | flops 536870912 | bytes 2097152 | tf_op jit(solution)/shard_map/pallas_call | solution.py:298
  47.5 1.3 %collective-permute-start.16 = (s16[272,512]{1,0:T(8,128)(2,1)S(1)}, s16[272,512]{1,0:T(8,128)(2,1)S(1)}, u32[]{:S(2)}, u32[]{:S(2)}) collective-permute-start(s16[272,512]{1,0:T(8,128)(2,1)S(1)} %get-tuple-element.34), channel_id=1, source_target_pairs={{0,128},{8,136},{16,144},{24,152},{32,160},{40,168},{48,176},{56,1... | collective-permute-start | bytes 835592 | tf_op jit(solution)/shard_map/ppermute | solution.py:371
  48.8 0.7 %shard_map.67.r_1_ = f32[512,512]{1,0:T(8,128)S(1)} custom-call(bf16[2,256,1024]{2,1,0:T(8,128)(2,1)S(1)} %get-tuple-element.28.refs_0_, bf16[1024,512]{1,0:T(8,128)(2,1)S(1)} %bitcast.12), custom_call_target="tpu_custom_call" | custom-call | flops 536870912 | bytes 2097152 | tf_op jit(solution)/shard_map/pallas_call | solution.py:212
  49.6 0.2 shard_map.75
  49.8 0.8 %collective-permute-start.21 = (s16[272,256]{1,0:T(8,128)(2,1)S(1)}, s16[272,256]{1,0:T(8,128)(2,1)S(1)}, u32[]{:S(2)}, u32[]{:S(2)}) collective-permute-start(s16[272,256]{1,0:T(8,128)(2,1)S(1)} %get-tuple-element.37), channel_id=1, source_target_pairs={{0,16},{8,120},{16,32},{24,8},{32,48},{40,24},{48,64},{56,40},{64,... | collective-permute-start | bytes 417800 | tf_op jit(solution)/shard_map/ppermute | solution.py:388
  50.6 1.1 %collective-permute-start.22 = (s16[272,256]{1,0:T(8,128)(2,1)S(1)}, s16[272,256]{1,0:T(8,128)(2,1)S(1)}, u32[]{:S(2)}, u32[]{:S(2)}) collective-permute-start(s16[272,256]{1,0:T(8,128)(2,1)S(1)} %get-tuple-element.38), channel_id=1, source_target_pairs={{0,144},{8,248},{16,160},{24,136},{32,176},{40,152},{48,192},{56,1... | collective-permute-start | bytes 417800 | tf_op jit(solution)/shard_map/ppermute | solution.py:387
  51.7 0.2 shard_map.69
  51.8 1.7 %collective-permute-start.14 = (s16[272,256]{1,0:T(8,128)(2,1)S(1)}, s16[272,256]{1,0:T(8,128)(2,1)S(1)}, u32[]{:S(2)}, u32[]{:S(2)}) collective-permute-start(s16[272,256]{1,0:T(8,128)(2,1)S(1)} %get-tuple-element.30), channel_id=1, source_target_pairs={{0,16},{8,120},{16,32},{24,8},{32,48},{40,24},{48,64},{56,40},{64,... | collective-permute-start | bytes 417800 | tf_op jit(solution)/shard_map/ppermute | solution.py:388
  53.5 1.1 %collective-permute-start.15 = (s16[272,256]{1,0:T(8,128)(2,1)S(1)}, s16[272,256]{1,0:T(8,128)(2,1)S(1)}, u32[]{:S(2)}, u32[]{:S(2)}) collective-permute-start(s16[272,256]{1,0:T(8,128)(2,1)S(1)} %get-tuple-element.31), channel_id=1, source_target_pairs={{0,144},{8,248},{16,160},{24,136},{32,176},{40,152},{48,192},{56,1... | collective-permute-start | bytes 417800 | tf_op jit(solution)/shard_map/ppermute | solution.py:387
  54.6 6.0 %collective-permute-done.16.r_3_ = s16[272,512]{1,0:T(8,128)(2,1)S(1)} collective-permute-done((s16[272,512]{1,0:T(8,128)(2,1)S(1)}, s16[272,512]{1,0:T(8,128)(2,1)S(1)}, u32[]{:S(2)}, u32[]{:S(2)}) %collective-permute-start.16) | collective-permute-done | bytes 278560 | tf_op jit(solution)/shard_map/ppermute | solution.py:371
  60.6 0.1 shard_map.76
  60.7 0.7 %collective-permute-start.23 = (f32[128,256]{1,0:T(8,128)S(1)}, f32[128,256]{1,0:T(8,128)S(1)}, u32[]{:S(2)}, u32[]{:S(2)}) collective-permute-start(f32[128,256]{1,0:T(8,128)S(1)} %get-tuple-element.40), channel_id=1, source_target_pairs={{0,8},{8,0},{16,24},{24,16},{32,40},{40,32},{48,56},{56,48},{64,72... | collective-permute-start | bytes 393224 | tf_op jit(solution)/shard_map/ppermute | solution.py:391
  61.4 0.1 shard_map.71
  61.5 2.2 %collective-permute-start.17 = (f32[128,256]{1,0:T(8,128)S(1)}, f32[128,256]{1,0:T(8,128)S(1)}, u32[]{:S(2)}, u32[]{:S(2)}) collective-permute-start(f32[128,256]{1,0:T(8,128)S(1)} %get-tuple-element.36), channel_id=1, source_target_pairs={{0,8},{8,0},{16,24},{24,16},{32,40},{40,32},{48,56},{56,48},{64,72... | collective-permute-start | bytes 393224 | tf_op jit(solution)/shard_map/ppermute | solution.py:391
  63.7 1.0 %collective-permute-done.17.r_2_ = f32[128,256]{1,0:T(8,128)S(1)} collective-permute-done((f32[128,256]{1,0:T(8,128)S(1)}, f32[128,256]{1,0:T(8,128)S(1)}, u32[]{:S(2)}, u32[]{:S(2)}) %collective-permute-start.17) | collective-permute-done | bytes 131104 | tf_op jit(solution)/shard_map/ppermute | solution.py:391
  64.7 0.8 %shard_map.77 = f32[128,2,256]{2,1,0:T(2,128)} custom-call(f32[2,128,256]{2,1,0:T(8,128)S(1)} %shard_map.55.keep_ref.r_0_, f32[128,256]{1,0:T(8,128)S(1)} %get-tuple-element.35.r_1_, f32[128,256]{1,0:T(8,128)S(1)} %collective-permute-done.17.r_2_, f32[128,256]{1,0:T(8,128)S(1)} %get-tuple-element.39.r_3_, f32[128,256]{1,0:T(8,128)S(1)} %collective-permute-done.23.r_4_), custom_call_target="tpu_custom_call" | custom-call | flops 524288 | bytes 917504 | tf_op jit(solution)/shard_map/pallas_call | solution.py:344
  (31 shorter events, 0.6 us)
Async XLA Ops:
  0.0 17.2 %copy-start = (bf16[2,4,32,256]{3,2,1,0:T(8,128)(2,1)S(1)}, bf16[2,4,32,256]{3,2,1,0:T(8,128)(2,1)}, u32[]{:S(2)}) copy-start(bf16[2,4,32,256]{3,2,1,0:T(8,128)(2,1)} %refs_0_.1) | copy-start | bytes 393220
  0.0 14.9 %copy-start.3 = (s32[128]{0:T(128)S(1)}, s32[128]{0:T(128)}, u32[]{:S(2)}) copy-start(s32[128]{0:T(128)} %param.9) | copy-start | bytes 1540
  0.0 14.9 %copy-start.2 = (s32[2,96]{1,0:T(2,128)S(1)}, s32[2,96]{1,0:T(2,128)}, u32[]{:S(2)}) copy-start(s32[2,96]{1,0:T(2,128)} %flags_ref.1) | copy-start | bytes 2308
  0.0 14.9 %copy-start.1 = (s32[2,96]{1,0:T(2,128)S(1)}, s32[2,96]{1,0:T(2,128)}, u32[]{:S(2)}) copy-start(s32[2,96]{1,0:T(2,128)} %ancestors_ref.1) | copy-start | bytes 2308
  0.0 6.3 %collective-permute-start.1 = (bf16[2,4,32,256]{3,2,1,0:T(8,128)(2,1)}, bf16[2,4,32,256]{3,2,1,0:T(8,128)(2,1)S(1)}, u32[]{:S(2)}, u32[]{:S(2)}) collective-permute-start(bf16[2,4,32,256]{3,2,1,0:T(8,128)(2,1)} %refs_0_.1), channel_id=1, source_target_pairs={{0,6},{1,7},{2,0},{3,1},{4,2},{5,3},{6,4},{7,5},{8,14},{9,15},{10,... | collective-permute-start | bytes 393224 | tf_op jit(solution)/shard_map/ppermute | solution.py:352
  3.4 5.9 %collective-permute-start = (bf16[2,4,32,256]{3,2,1,0:T(8,128)(2,1)}, bf16[2,4,32,256]{3,2,1,0:T(8,128)(2,1)S(1)}, u32[]{:S(2)}, u32[]{:S(2)}) collective-permute-start(bf16[2,4,32,256]{3,2,1,0:T(8,128)(2,1)} %refs_0_.1), channel_id=1, source_target_pairs={{0,1},{1,0},{2,3},{3,2},{4,5},{5,4},{6,7},{7,6},{8,9},{9,8},{10,11... | collective-permute-start | bytes 393224 | tf_op jit(solution)/shard_map/ppermute | solution.py:351
  6.3 8.9 %collective-permute-start.3 = (bf16[2,4,32,256]{3,2,1,0:T(8,128)(2,1)}, bf16[2,4,32,256]{3,2,1,0:T(8,128)(2,1)S(1)}, u32[]{:S(2)}, u32[]{:S(2)}) collective-permute-start(bf16[2,4,32,256]{3,2,1,0:T(8,128)(2,1)} %refs_0_.1), channel_id=1, source_target_pairs={{0,2},{1,3},{2,4},{3,5},{4,6},{5,7},{6,0},{7,1},{8,10},{9,11},{10,... | collective-permute-start | bytes 393224 | tf_op jit(solution)/shard_map/ppermute | solution.py:352
  6.3 8.9 %collective-permute-start.2 = (bf16[2,4,32,256]{3,2,1,0:T(8,128)(2,1)S(1)}, bf16[2,4,32,256]{3,2,1,0:T(8,128)(2,1)S(1)}, u32[]{:S(2)}, u32[]{:S(2)}) collective-permute-start(bf16[2,4,32,256]{3,2,1,0:T(8,128)(2,1)S(1)} %collective-permute-done.1.refs_4_), channel_id=1, source_target_pairs={{0,6},{1,7},{2,0},{3,1},{4,2},{5,3},{6,4},{7,5},{8,14},{9,15},{10,... | collective-permute-start | bytes 393224 | tf_op jit(solution)/shard_map/ppermute | solution.py:356
  9.2 6.0 %collective-permute-start.6 = (bf16[2,4,32,256]{3,2,1,0:T(8,128)(2,1)S(1)}, bf16[2,4,32,256]{3,2,1,0:T(8,128)(2,1)S(1)}, u32[]{:S(2)}, u32[]{:S(2)}) collective-permute-start(bf16[2,4,32,256]{3,2,1,0:T(8,128)(2,1)S(1)} %collective-permute-done.refs_1_), channel_id=1, source_target_pairs={{0,6},{1,7},{2,0},{3,1},{4,2},{5,3},{6,4},{7,5},{8,14},{9,15},{10,... | collective-permute-start | bytes 393224 | tf_op jit(solution)/shard_map/ppermute | solution.py:355
  9.8 5.5 %collective-permute-start.5 = (bf16[2,4,32,256]{3,2,1,0:T(8,128)(2,1)S(1)}, bf16[2,4,32,256]{3,2,1,0:T(8,128)(2,1)S(1)}, u32[]{:S(2)}, u32[]{:S(2)}) collective-permute-start(bf16[2,4,32,256]{3,2,1,0:T(8,128)(2,1)S(1)} %collective-permute-done.refs_1_), channel_id=1, source_target_pairs={{0,2},{1,3},{2,4},{3,5},{4,6},{5,7},{6,0},{7,1},{8,10},{9,11},{10,... | collective-permute-start | bytes 393224 | tf_op jit(solution)/shard_map/ppermute | solution.py:355
  10.7 6.4 %collective-permute-start.4 = (bf16[2,4,32,256]{3,2,1,0:T(8,128)(2,1)S(1)}, bf16[2,4,32,256]{3,2,1,0:T(8,128)(2,1)S(1)}, u32[]{:S(2)}, u32[]{:S(2)}) collective-permute-start(bf16[2,4,32,256]{3,2,1,0:T(8,128)(2,1)S(1)} %collective-permute-done.refs_1_), channel_id=1, source_target_pairs={{0,4},{1,5},{2,6},{3,7},{4,0},{5,1},{6,2},{7,3},{8,12},{9,13},{10,... | collective-permute-start | bytes 393224 | tf_op jit(solution)/shard_map/ppermute | solution.py:355
  18.1 15.6 %collective-permute-start.9 = (f32[512,512]{1,0:T(8,128)S(1)}, f32[512,512]{1,0:T(8,128)S(1)}, u32[]{:S(2)}, u32[]{:S(2)}) collective-permute-start(f32[512,512]{1,0:T(8,128)S(1)} %shard_map.62), channel_id=1, source_target_pairs={{0,8},{8,0},{16,24},{24,16},{32,40},{40,32},{48,56},{56,48},{64,72... | collective-permute-start | bytes 3145736 | tf_op jit(solution)/shard_map/ppermute | solution.py:365
  21.8 17.4 %collective-permute-start.11 = (f32[512,512]{1,0:T(8,128)S(1)}, f32[512,512]{1,0:T(8,128)S(1)}, u32[]{:S(2)}, u32[]{:S(2)}) collective-permute-start(f32[512,512]{1,0:T(8,128)S(1)} %shard_map.65), channel_id=1, source_target_pairs={{0,8},{8,0},{16,24},{24,16},{32,40},{40,32},{48,56},{56,48},{64,72... | collective-permute-start | bytes 3145736 | tf_op jit(solution)/shard_map/ppermute | solution.py:365
  22.4 3.3 %collective-permute-start.7 = (f32[256,512]{1,0:T(8,128)S(1)}, f32[256,512]{1,0:T(8,128)S(1)}, u32[]{:S(2)}, u32[]{:S(2)}) collective-permute-start(f32[256,512]{1,0:T(8,128)S(1)} %shard_map.59), channel_id=1, source_target_pairs={{0,8},{8,0},{16,24},{24,16},{32,40},{40,32},{48,56},{56,48},{64,72... | collective-permute-start | bytes 1572872 | tf_op jit(solution)/shard_map/ppermute | solution.py:365
  23.6 25.9 %collective-permute-start.13 = (f32[512,512]{1,0:T(8,128)S(1)}, f32[512,512]{1,0:T(8,128)S(1)}, u32[]{:S(2)}, u32[]{:S(2)}) collective-permute-start(f32[512,512]{1,0:T(8,128)S(1)} %shard_map.68), channel_id=1, source_target_pairs={{0,8},{8,0},{16,24},{24,16},{32,40},{40,32},{48,56},{56,48},{64,72... | collective-permute-start | bytes 3145736 | tf_op jit(solution)/shard_map/ppermute | solution.py:365
  25.7 8.0 %collective-permute-start.18 = (s16[272,256]{1,0:T(8,128)(2,1)S(1)}, s16[272,256]{1,0:T(8,128)(2,1)S(1)}, u32[]{:S(2)}, u32[]{:S(2)}) collective-permute-start(s16[272,256]{1,0:T(8,128)(2,1)S(1)} %shard_map.72), channel_id=1, source_target_pairs={{0,16},{8,120},{16,32},{24,8},{32,48},{40,24},{48,64},{56,40},{64,... | collective-permute-start | bytes 417800 | tf_op jit(solution)/shard_map/ppermute | solution.py:385
  31.8 5.3 %collective-permute-start.8 = (s16[272,256]{1,0:T(8,128)(2,1)S(1)}, s16[272,256]{1,0:T(8,128)(2,1)S(1)}, u32[]{:S(2)}, u32[]{:S(2)}) collective-permute-start(s16[272,256]{1,0:T(8,128)(2,1)S(1)} %shard_map.60), channel_id=1, source_target_pairs={{0,16},{8,120},{16,32},{24,8},{32,48},{40,24},{48,64},{56,40},{64,... | collective-permute-start | bytes 417800 | tf_op jit(solution)/shard_map/ppermute | solution.py:385
  33.9 6.6 %collective-permute-start.19 = (s16[528,256]{1,0:T(8,128)(2,1)S(1)}, s16[528,256]{1,0:T(8,128)(2,1)S(1)}, u32[]{:S(2)}, u32[]{:S(2)}) collective-permute-start(s16[528,256]{1,0:T(8,128)(2,1)S(1)} %shard_map.73), channel_id=1, source_target_pairs={{0,16},{8,120},{16,32},{24,8},{32,48},{40,24},{48,64},{56,40},{64,... | collective-permute-start | bytes 811016 | tf_op jit(solution)/shard_map/ppermute | solution.py:385
  37.2 6.6 %collective-permute-start.10 = (s16[528,256]{1,0:T(8,128)(2,1)S(1)}, s16[528,256]{1,0:T(8,128)(2,1)S(1)}, u32[]{:S(2)}, u32[]{:S(2)}) collective-permute-start(s16[528,256]{1,0:T(8,128)(2,1)S(1)} %shard_map.63), channel_id=1, source_target_pairs={{0,16},{8,120},{16,32},{24,8},{32,48},{40,24},{48,64},{56,40},{64,... | collective-permute-start | bytes 811016 | tf_op jit(solution)/shard_map/ppermute | solution.py:385
  40.6 8.9 %collective-permute-start.20 = (s16[528,256]{1,0:T(8,128)(2,1)S(1)}, s16[528,256]{1,0:T(8,128)(2,1)S(1)}, u32[]{:S(2)}, u32[]{:S(2)}) collective-permute-start(s16[528,256]{1,0:T(8,128)(2,1)S(1)} %shard_map.74), channel_id=1, source_target_pairs={{0,16},{8,120},{16,32},{24,8},{32,48},{40,24},{48,64},{56,40},{64,... | collective-permute-start | bytes 811016 | tf_op jit(solution)/shard_map/ppermute | solution.py:385
  44.0 7.7 %collective-permute-start.12 = (s16[528,256]{1,0:T(8,128)(2,1)S(1)}, s16[528,256]{1,0:T(8,128)(2,1)S(1)}, u32[]{:S(2)}, u32[]{:S(2)}) collective-permute-start(s16[528,256]{1,0:T(8,128)(2,1)S(1)} %shard_map.66), channel_id=1, source_target_pairs={{0,16},{8,120},{16,32},{24,8},{32,48},{40,24},{48,64},{56,40},{64,... | collective-permute-start | bytes 811016 | tf_op jit(solution)/shard_map/ppermute | solution.py:385
  47.5 13.0 %collective-permute-start.16 = (s16[272,512]{1,0:T(8,128)(2,1)S(1)}, s16[272,512]{1,0:T(8,128)(2,1)S(1)}, u32[]{:S(2)}, u32[]{:S(2)}) collective-permute-start(s16[272,512]{1,0:T(8,128)(2,1)S(1)} %get-tuple-element.34), channel_id=1, source_target_pairs={{0,128},{8,136},{16,144},{24,152},{32,160},{40,168},{48,176},{56,1... | collective-permute-start | bytes 835592 | tf_op jit(solution)/shard_map/ppermute | solution.py:371
  49.8 10.8 %collective-permute-start.21 = (s16[272,256]{1,0:T(8,128)(2,1)S(1)}, s16[272,256]{1,0:T(8,128)(2,1)S(1)}, u32[]{:S(2)}, u32[]{:S(2)}) collective-permute-start(s16[272,256]{1,0:T(8,128)(2,1)S(1)} %get-tuple-element.37), channel_id=1, source_target_pairs={{0,16},{8,120},{16,32},{24,8},{32,48},{40,24},{48,64},{56,40},{64,... | collective-permute-start | bytes 417800 | tf_op jit(solution)/shard_map/ppermute | solution.py:388
  50.6 9.9 %collective-permute-start.22 = (s16[272,256]{1,0:T(8,128)(2,1)S(1)}, s16[272,256]{1,0:T(8,128)(2,1)S(1)}, u32[]{:S(2)}, u32[]{:S(2)}) collective-permute-start(s16[272,256]{1,0:T(8,128)(2,1)S(1)} %get-tuple-element.38), channel_id=1, source_target_pairs={{0,144},{8,248},{16,160},{24,136},{32,176},{40,152},{48,192},{56,1... | collective-permute-start | bytes 417800 | tf_op jit(solution)/shard_map/ppermute | solution.py:387
  51.8 9.5 %collective-permute-start.14 = (s16[272,256]{1,0:T(8,128)(2,1)S(1)}, s16[272,256]{1,0:T(8,128)(2,1)S(1)}, u32[]{:S(2)}, u32[]{:S(2)}) collective-permute-start(s16[272,256]{1,0:T(8,128)(2,1)S(1)} %get-tuple-element.30), channel_id=1, source_target_pairs={{0,16},{8,120},{16,32},{24,8},{32,48},{40,24},{48,64},{56,40},{64,... | collective-permute-start | bytes 417800 | tf_op jit(solution)/shard_map/ppermute | solution.py:388
  53.5 7.9 %collective-permute-start.15 = (s16[272,256]{1,0:T(8,128)(2,1)S(1)}, s16[272,256]{1,0:T(8,128)(2,1)S(1)}, u32[]{:S(2)}, u32[]{:S(2)}) collective-permute-start(s16[272,256]{1,0:T(8,128)(2,1)S(1)} %get-tuple-element.31), channel_id=1, source_target_pairs={{0,144},{8,248},{16,160},{24,136},{32,176},{40,152},{48,192},{56,1... | collective-permute-start | bytes 417800 | tf_op jit(solution)/shard_map/ppermute | solution.py:387
  60.7 3.0 %collective-permute-start.23 = (f32[128,256]{1,0:T(8,128)S(1)}, f32[128,256]{1,0:T(8,128)S(1)}, u32[]{:S(2)}, u32[]{:S(2)}) collective-permute-start(f32[128,256]{1,0:T(8,128)S(1)} %get-tuple-element.40), channel_id=1, source_target_pairs={{0,8},{8,0},{16,24},{24,16},{32,40},{40,32},{48,56},{56,48},{64,72... | collective-permute-start | bytes 393224 | tf_op jit(solution)/shard_map/ppermute | solution.py:391
  61.5 3.2 %collective-permute-start.17 = (f32[128,256]{1,0:T(8,128)S(1)}, f32[128,256]{1,0:T(8,128)S(1)}, u32[]{:S(2)}, u32[]{:S(2)}) collective-permute-start(f32[128,256]{1,0:T(8,128)S(1)} %get-tuple-element.36), channel_id=1, source_target_pairs={{0,8},{8,0},{16,24},{24,16},{32,40},{40,32},{48,56},{56,48},{64,72... | collective-permute-start | bytes 393224 | tf_op jit(solution)/shard_map/ppermute | solution.py:391
